TPU v7x, 32 devices: a whole 2x2x4 slice. The times are simulated.
32 devices in a mesh: dom: 8 (over z, y), mp: 4 (over x, core).
Axes of the slice: x: 2, y: 2, z: 4, core: 2. Of those that a mesh axis runs over, the one named last changes fastest.
Arguments:
- vertex_embedding: bfloat16 [4096, 512], P('dom'), may hold values from -6 to 6
- prenorm_mixer_scale: float32 [512], replicated, may hold values from 0.25 to 1.75
- prenorm_perceptron_scale: float32 [512], replicated, may hold values from 0.25 to 1.75
- triple_projector_stack: bfloat16 [3, 512, 512], P(None, None, 'mp'), may hold values from -0.25 to 0.25
- channel_logit_scaling: float32 [8], P('mp'), may hold values from 0.06 to 8
- mixer_final_projector: bfloat16 [512, 512], P('mp'), may hold values from -0.25 to 0.25
- neighbour_mixer_projector: bfloat16 [512, 512], P('mp'), may hold values from -0.25 to 0.25
- expand_projector: bfloat16 [512, 2048], P(None, 'mp'), may hold values from -0.25 to 0.25
- contract_projector: bfloat16 [2048, 512], P('mp'), may hold values from -0.125 to 0.125
- matched_companion: int32 [2, 8], replicated, may hold values from 0 to 7, as said below
- boundary_sender_vertex: int32 [8, 8, 128], P('dom'), may hold values from 0 to 511
- boundary_slot_tally: int32 [8, 8], P('dom'), may hold values from 0 to 128, as said below
- boundary_landing_vertex: int32 [8, 8, 128], P('dom'), may hold values from 0 to 511
- partition_edge_tail: int32 [8, 16384], P('dom'), may hold values from 0 to 511
- partition_edge_sink: int32 [8, 16384], P('dom'), may hold values from 0 to 511
Outputs:
- updated: bfloat16 [4096, 512], P(('dom', 'mp'))
Inputs may be any that keep to these rules, and one draw needn't show every extreme that they name: matched_companion[j, b] equals b XOR c_j for one number c_j of each matching; c_0 and c_1 are at least 1 and differ. Slots at and beyond boundary_slot_tally[s, d] of the 128 slots from s to d are unused; the diagonal is 0; the largest entry is 128.
All inputs are finite; a program needn't handle non-finite values.
Results may differ from a plain program's by a relative error of at most 0.012.
The roundings to bfloat16 on the way count: a program that leaves them out, or rounds other values in their place, can miss the bound.
Values may be sent and summed in bfloat16 or wider, within the bound.
No kernel may reach another device: no remote copies, remote signals or barrier semaphores. Data moves between devices by JAX's collectives and lax.ppermute only.
A program may use at most 64 MiB of HBM per device.

v0:
```python
import math

import jax
import jax.numpy as jnp
from jax import lax
from jax.sharding import PartitionSpec as P

HEAD_SIZE = 64
BLOCK_NODES = 512
CAP = 128


epsilon = 1e-05


def swapped_2(block, axis, bit):
    count = lax.axis_size(axis)
    route = []
    for low in range(count):
        high = low | 1 << bit
        if high != low and high < count:
            route += [(low, high), (high, low)]
    return lax.ppermute(block, axis, route)


def normalize(matrix, scale_gain):
    matrix = matrix.astype(jnp.float32)
    row_mean = jnp.mean(matrix, -1, keepdims=True)
    centred = matrix - row_mean
    variance = jnp.mean(centred * centred, -1, keepdims=True)
    return (centred * lax.rsqrt(variance + epsilon) * scale_gain).astype(jnp.bfloat16)


def tile_softmax_mixing(asking_vertices, lookup_tensor, content_tensor, channel_logit_scaling):
    affinity_table = jnp.einsum(
        "rhd,shd->hrs", asking_vertices, lookup_tensor, preferred_element_type=jnp.float32
    )
    affinity_table = affinity_table * channel_logit_scaling[:, None, None]
    weights = jax.nn.softmax(affinity_table, axis=-1).astype(jnp.bfloat16)
    attended = jnp.einsum(
        "hrs,shd->rhd", weights, content_tensor, preferred_element_type=jnp.float32
    )
    return attended.astype(jnp.bfloat16)


def land_rows(values, targets, flags, node_rows):
    total = targets.shape[0]
    feature_width = values.shape[1]
    step_rows = math.gcd(total, 2048)
    turns = total // step_rows
    columns = jnp.arange(node_rows, dtype=jnp.int32)

    def accumulate(carry, inputs):
        sums, counts = carry
        part_values, part_targets, part_flags = inputs
        selector = (part_targets[:, None] == columns[None, :]).astype(jnp.bfloat16)
        sums = sums + jnp.einsum(
            "mr,mw->rw", selector, part_values, preferred_element_type=jnp.float32
        )
        counts = counts + jnp.dot(part_flags, selector, preferred_element_type=jnp.float32)
        return ((sums, counts), None)

    initial = (
        jnp.zeros((node_rows, feature_width), jnp.float32),
        jnp.zeros((node_rows,), jnp.float32),
    )
    (sums, counts), unused = lax.scan(
        accumulate,
        initial,
        (
            values.reshape(turns, step_rows, feature_width),
            targets.reshape(turns, step_rows),
            flags.reshape(turns, step_rows),
        ),
    )
    return (sums, counts)


def body(
    vertex_embedding,
    prenorm_mixer_scale,
    prenorm_perceptron_scale,
    triple_projector_stack,
    channel_logit_scaling,
    mixer_final_projector,
    neighbour_mixer_projector,
    expand_projector,
    contract_projector,
    matched_companion,
    boundary_sender_vertex,
    boundary_slot_tally,
    boundary_landing_vertex,
    partition_edge_tail,
    partition_edge_sink,
):
    node_dev = vertex_embedding.shape[0]
    blocks = node_dev // BLOCK_NODES
    partition_channel_split = channel_logit_scaling.shape[0]
    width_here = partition_channel_split * HEAD_SIZE
    normed = normalize(vertex_embedding, prenorm_mixer_scale)
    projected = jnp.einsum(
        "nd,tdc->tnc", normed, triple_projector_stack, preferred_element_type=jnp.float32
    ).astype(jnp.bfloat16)
    asking_vertices = projected[0]
    key_value = jnp.concatenate([projected[1], projected[2]], axis=1)
    mask_pair = matched_companion[:, 0]
    device_mask = mask_pair // blocks
    local_mask = mask_pair % blocks
    routed_one = key_value
    routed_two = key_value
    for bit_number in range(lax.axis_size("dom").bit_length() - 1):
        swapped = swapped_2((routed_one, routed_two), "dom", bit_number)
        take_flags = jnp.bitwise_and(jnp.right_shift(device_mask, bit_number), 1) == 1
        routed_one = jnp.where(take_flags[0], swapped[0], routed_one)
        routed_two = jnp.where(take_flags[1], swapped[1], routed_two)
    block_order = jnp.arange(blocks, dtype=jnp.int32)
    fetched_one = routed_one.reshape(blocks, BLOCK_NODES, 2 * width_here)[
        jnp.bitwise_xor(block_order, local_mask[0])
    ]
    fetched_two = routed_two.reshape(blocks, BLOCK_NODES, 2 * width_here)[
        jnp.bitwise_xor(block_order, local_mask[1])
    ]
    own_pairs = key_value.reshape(blocks, BLOCK_NODES, 2 * width_here)
    all_pairs = jnp.concatenate([own_pairs, fetched_one, fetched_two], axis=1)

    def per_block(inputs):
        block_queries, pair_block = inputs
        block_keys = pair_block[:, :width_here].reshape(
            3 * BLOCK_NODES, partition_channel_split, HEAD_SIZE
        )
        block_values = pair_block[:, width_here:].reshape(
            3 * BLOCK_NODES, partition_channel_split, HEAD_SIZE
        )
        return tile_softmax_mixing(
            block_queries.reshape(BLOCK_NODES, partition_channel_split, HEAD_SIZE),
            block_keys,
            block_values,
            channel_logit_scaling,
        )

    attended = lax.map(
        per_block, (asking_vertices.reshape(blocks, BLOCK_NODES, width_here), all_pairs)
    ).reshape(node_dev, width_here)
    attn_term = jnp.dot(attended, mixer_final_projector, preferred_element_type=jnp.float32)
    mp_index = lax.axis_index("mp")
    width_q = neighbour_mixer_projector.shape[0]
    quarter = lax.dynamic_slice_in_dim(vertex_embedding, mp_index * width_q, width_q, 1)
    slot_index = jnp.arange(CAP, dtype=jnp.int32)
    live_slots = slot_index[None, :] < boundary_slot_tally[0][:, None]
    outgoing = jnp.where(
        live_slots[..., None], quarter[boundary_sender_vertex[0]], jnp.zeros((), jnp.bfloat16)
    )
    incoming, arrived = (
        lax.all_to_all(outgoing, "dom", split_axis=0, concat_axis=0, tiled=True),
        lax.all_to_all(
            live_slots.astype(jnp.bfloat16), "dom", split_axis=0, concat_axis=0, tiled=True
        ),
    )
    targets = boundary_landing_vertex[0].reshape(-1)
    boundary, degree = land_rows(
        incoming.reshape(-1, width_q), targets, arrived.reshape(-1), node_dev
    )
    edge_count = partition_edge_sink.shape[1]
    local_sum, local_degree = land_rows(
        quarter[partition_edge_tail[0]],
        partition_edge_sink[0],
        jnp.ones((edge_count,), jnp.bfloat16),
        node_dev,
    )
    degree = degree + local_degree
    message = (
        (quarter.astype(jnp.float32) + local_sum + boundary) / (1.0 + degree)[:, None]
    ).astype(jnp.bfloat16)
    partial_terms = attn_term + jnp.dot(
        message, neighbour_mixer_projector, preferred_element_type=jnp.float32
    )
    share_rows = node_dev // lax.axis_size("mp")
    summed = lax.psum_scatter(
        partial_terms.astype(jnp.bfloat16), "mp", scatter_dimension=0, tiled=True
    ).astype(jnp.float32)
    own_rows = lax.dynamic_slice_in_dim(vertex_embedding, mp_index * share_rows, share_rows, 0)
    mixed_share = own_rows.astype(jnp.float32) + summed
    normed_share = normalize(mixed_share, prenorm_perceptron_scale)
    hidden = jax.nn.gelu(
        jnp.dot(
            lax.all_gather(normed_share, "mp", axis=0, tiled=True),
            expand_projector,
            preferred_element_type=jnp.float32,
        ),
        approximate=False,
    ).astype(jnp.bfloat16)
    down_share = lax.psum_scatter(
        jnp.dot(hidden, contract_projector, preferred_element_type=jnp.float32).astype(
            jnp.bfloat16
        ),
        "mp",
        scatter_dimension=0,
        tiled=True,
    ).astype(jnp.float32)
    return (mixed_share + down_share).astype(jnp.bfloat16)


def solution(mesh):
    return jax.shard_map(
        body,
        mesh=mesh,
        in_specs=(
            P("dom", None),
            P(),
            P(),
            P(None, None, "mp"),
            P("mp"),
            P("mp", None),
            P("mp", None),
            P(None, "mp"),
            P("mp", None),
            P(),
            P("dom", None, None),
            P("dom", None),
            P("dom", None, None),
            P("dom", None),
            P("dom", None),
        ),
        out_specs=P(("dom", "mp"), None),
        check_vma=False,
    )
```

profile of v0, /device:TPU:0, one launch (start us, length us, event | category | flops | bytes accessed | tf_op | source)
XLA Modules:
  0.0 230.9 jit_solution(13320501125665430070)
XLA Ops:
  6.6 1.3 copy.18
  7.8 1.2 convert_reduce_fusion
  9.0 1.3 fusion.27
  10.4 1.6 fusion.46
  12.1 3.1 %collective-permute-start = (bf16[512,256]{0,1:T(8,128)(2,1)S(1)}, bf16[512,256]{0,1:T(8,128)(2,1)S(1)}, u32[]{:S(2)}, u32[]{:S(2)}) collective-permute-start(bf16[512,256]{0,1:T(8,128)(2,1)S(1)} %pad_maximum_fusion), channel_id=1, source_target_pairs={{0,4},{4,0},{8,12},{12,8},{16,20},{20,16},{24,28},{28,24},{1,5},{5... | collective-permute-start | bytes 786440 | tf_op jit(solution)/shard_map/ppermute | solution.py:23
  15.8 4.9 %all-to-all-start.1 = ((bf16[8,1,128]{2,1,0:T(2,128)(2,1)}), bf16[8,1,128]{2,1,0:T(2,128)(2,1)S(1)}, u32[]{:S(2)}, u32[]{:S(2)}) async-start(bf16[8,1,128]{2,1,0:T(2,128)(2,1)} %compare_convert_fusion), calls=%async_computation.1 | async-start | bytes 8192 | tf_op jit(solution)/shard_map/all_to_all | solution.py:155
  22.3 57.8 %gather_fusion = bf16[16384,128]{1,0:T(8,128)(2,1)} fusion(bf16[512,128]{1,0:T(8,128)(2,1)S(1)} %constant_dynamic-slice_fusion.1, s32[16384]{0:T(1024)S(1)} %broadcast_clamp_fusion), kind=kCustom, calls=%fused_computation | custom fusion | bytes 8454144 | tf_op jit(solution)/shard_map/gather | solution.py:165
  80.1 27.8 %while.3 = (s32[]{:T(128)}, f32[512,128]{1,0:T(8,128)S(1)}, f32[512]{0:T(512)S(1)}, s32[8,2048]{1,0:T(8,128)S(1)}, bf16[8,2048,128]{2,1,0:T(8,128)(2,1)}, /*index=5*/s32[]{:T(128)}, s32[]{:T(128)}) while((s32[]{:T(128)}, f32[512,128]{1,0:T(8,128)S(1)}, f32[512]{0:T(512)S(1)}, s32[8,2048]{1,0:T(8,128)S(1)}, ...), condition=%wide.region_5.6_spmd.clone, body=%wide.region_4.5_spmd.clone.sunk | while | flops 272761856 | bytes 1089640 | solution.py:67
  80.1 2.6 %fusion.147 = f32[512,128]{1,0:T(8,128)S(1)} fusion(s32[2048]{0:T(1024)S(1)} %bitcast.80, bf16[8,2048,128]{2,1,0:T(8,128)(2,1)} %get-tuple-element.176, s32[]{:T(128)S(6)} %copy.22, f32[512,128]{1,0:T(8,128)S(1)} %get-tuple-element.166, pred[]{:T(512)S(6)} %compare.5), kind=kOutput, calls=%fused_computation.8.clone.1 | convolution fusion | flops 269615104 | bytes 1056773 | tf_op jit(solution)/shard_map/while/body/eval_jaxpr/mr,mw->rw/dot_general | solution.py:57
  83.6 2.6 %fusion.147 = f32[512,128]{1,0:T(8,128)S(1)} fusion(s32[2048]{0:T(1024)S(1)} %bitcast.80, bf16[8,2048,128]{2,1,0:T(8,128)(2,1)} %get-tuple-element.176, s32[]{:T(128)S(6)} %copy.22, f32[512,128]{1,0:T(8,128)S(1)} %get-tuple-element.166, pred[]{:T(512)S(6)} %compare.5), kind=kOutput, calls=%fused_computation.8.clone.1 | convolution fusion | flops 269615104 | bytes 1056773 | tf_op jit(solution)/shard_map/while/body/eval_jaxpr/mr,mw->rw/dot_general | solution.py:57
  87.1 2.6 %fusion.147 = f32[512,128]{1,0:T(8,128)S(1)} fusion(s32[2048]{0:T(1024)S(1)} %bitcast.80, bf16[8,2048,128]{2,1,0:T(8,128)(2,1)} %get-tuple-element.176, s32[]{:T(128)S(6)} %copy.22, f32[512,128]{1,0:T(8,128)S(1)} %get-tuple-element.166, pred[]{:T(512)S(6)} %compare.5), kind=kOutput, calls=%fused_computation.8.clone.1 | convolution fusion | flops 269615104 | bytes 1056773 | tf_op jit(solution)/shard_map/while/body/eval_jaxpr/mr,mw->rw/dot_general | solution.py:57
  90.6 2.6 %fusion.147 = f32[512,128]{1,0:T(8,128)S(1)} fusion(s32[2048]{0:T(1024)S(1)} %bitcast.80, bf16[8,2048,128]{2,1,0:T(8,128)(2,1)} %get-tuple-element.176, s32[]{:T(128)S(6)} %copy.22, f32[512,128]{1,0:T(8,128)S(1)} %get-tuple-element.166, pred[]{:T(512)S(6)} %compare.5), kind=kOutput, calls=%fused_computation.8.clone.1 | convolution fusion | flops 269615104 | bytes 1056773 | tf_op jit(solution)/shard_map/while/body/eval_jaxpr/mr,mw->rw/dot_general | solution.py:57
  94.0 2.6 %fusion.147 = f32[512,128]{1,0:T(8,128)S(1)} fusion(s32[2048]{0:T(1024)S(1)} %bitcast.80, bf16[8,2048,128]{2,1,0:T(8,128)(2,1)} %get-tuple-element.176, s32[]{:T(128)S(6)} %copy.22, f32[512,128]{1,0:T(8,128)S(1)} %get-tuple-element.166, pred[]{:T(512)S(6)} %compare.5), kind=kOutput, calls=%fused_computation.8.clone.1 | convolution fusion | flops 269615104 | bytes 1056773 | tf_op jit(solution)/shard_map/while/body/eval_jaxpr/mr,mw->rw/dot_general | solution.py:57
  97.5 2.6 %fusion.147 = f32[512,128]{1,0:T(8,128)S(1)} fusion(s32[2048]{0:T(1024)S(1)} %bitcast.80, bf16[8,2048,128]{2,1,0:T(8,128)(2,1)} %get-tuple-element.176, s32[]{:T(128)S(6)} %copy.22, f32[512,128]{1,0:T(8,128)S(1)} %get-tuple-element.166, pred[]{:T(512)S(6)} %compare.5), kind=kOutput, calls=%fused_computation.8.clone.1 | convolution fusion | flops 269615104 | bytes 1056773 | tf_op jit(solution)/shard_map/while/body/eval_jaxpr/mr,mw->rw/dot_general | solution.py:57
  101.0 2.6 %fusion.147 = f32[512,128]{1,0:T(8,128)S(1)} fusion(s32[2048]{0:T(1024)S(1)} %bitcast.80, bf16[8,2048,128]{2,1,0:T(8,128)(2,1)} %get-tuple-element.176, s32[]{:T(128)S(6)} %copy.22, f32[512,128]{1,0:T(8,128)S(1)} %get-tuple-element.166, pred[]{:T(512)S(6)} %compare.5), kind=kOutput, calls=%fused_computation.8.clone.1 | convolution fusion | flops 269615104 | bytes 1056773 | tf_op jit(solution)/shard_map/while/body/eval_jaxpr/mr,mw->rw/dot_general | solution.py:57
  104.5 2.6 %fusion.147 = f32[512,128]{1,0:T(8,128)S(1)} fusion(s32[2048]{0:T(1024)S(1)} %bitcast.80, bf16[8,2048,128]{2,1,0:T(8,128)(2,1)} %get-tuple-element.176, s32[]{:T(128)S(6)} %copy.22, f32[512,128]{1,0:T(8,128)S(1)} %get-tuple-element.166, pred[]{:T(512)S(6)} %compare.5), kind=kOutput, calls=%fused_computation.8.clone.1 | convolution fusion | flops 269615104 | bytes 1056773 | tf_op jit(solution)/shard_map/while/body/eval_jaxpr/mr,mw->rw/dot_general | solution.py:57
  108.5 3.2 %gather_fusion.1 = bf16[1024,128]{1,0:T(8,128)(2,1)S(1)} fusion(bf16[512,128]{1,0:T(8,128)(2,1)S(1)} %constant_dynamic-slice_fusion.1, s32[1024]{0:T(1024)S(1)} %fusion.86), kind=kCustom, calls=%fused_computation.1 | custom fusion | bytes 528384 | tf_op jit(solution)/shard_map/gather | solution.py:151
  112.6 1.4 broadcast_select_fusion.3
  114.0 2.1 collective-permute-start.3
  116.7 6.0 %all-to-all-start = ((bf16[8,128,128]{2,1,0:T(8,128)(2,1)}), bf16[8,128,128]{2,1,0:T(8,128)(2,1)S(1)}, u32[]{:S(2)}, u32[]{:S(2)}) async-start(bf16[8,128,128]{2,1,0:T(8,128)(2,1)} %broadcast_select_fusion), calls=%async_computation | async-start | bytes 524288 | tf_op jit(solution)/shard_map/all_to_all | solution.py:154
  123.9 3.0 %collective-permute-start.4 = (bf16[512,256]{0,1:T(8,128)(2,1)S(1)}, bf16[512,256]{0,1:T(8,128)(2,1)S(1)}, u32[]{:S(2)}, u32[]{:S(2)}) collective-permute-start(bf16[512,256]{0,1:T(8,128)(2,1)S(1)} %broadcast_select_fusion.2), channel_id=1, source_target_pairs={{0,16},{16,0},{4,20},{20,4},{8,24},{24,8},{12,28},{28,12},{1,17},{... | collective-permute-start | bytes 786440 | tf_op jit(solution)/shard_map/ppermute | solution.py:23
  126.9 6.9 %collective-permute-done.1 = bf16[512,256]{0,1:T(8,128)(2,1)S(1)} collective-permute-done((bf16[512,256]{0,1:T(8,128)(2,1)S(1)}, bf16[512,256]{0,1:T(8,128)(2,1)S(1)}, u32[]{:S(2)}, u32[]{:S(2)}) %collective-permute-start.1) | collective-permute-done | bytes 262176 | tf_op jit(solution)/shard_map/ppermute | solution.py:23
  134.9 14.8 %collective-permute-done.4 = bf16[512,256]{0,1:T(8,128)(2,1)S(1)} collective-permute-done((bf16[512,256]{0,1:T(8,128)(2,1)S(1)}, bf16[512,256]{0,1:T(8,128)(2,1)S(1)}, u32[]{:S(2)}, u32[]{:S(2)}) %collective-permute-start.4) | collective-permute-done | bytes 262176 | tf_op jit(solution)/shard_map/ppermute | solution.py:23
  150.4 2.3 %collective-permute-done.2 = bf16[512,256]{0,1:T(8,128)(2,1)S(1)} collective-permute-done((bf16[512,256]{0,1:T(8,128)(2,1)S(1)}, bf16[512,256]{0,1:T(8,128)(2,1)S(1)}, u32[]{:S(2)}, u32[]{:S(2)}) %collective-permute-start.2) | collective-permute-done | bytes 262176 | tf_op jit(solution)/shard_map/ppermute | solution.py:23
  153.5 4.5 %fusion.124 = (f32[2,512]{1,0:T(2,128)S(1)}, f32[2,512,1536]{2,1,0:T(8,128)}) fusion(f32[2]{0:T(128)S(1)} %copy-done.13, bf16[512,2,64]{0,2,1:T(8,128)(2,1)S(1)} %bitcast.83, bf16[1536,2,64]{0,2,1:T(8,128)(2,1)S(1)} %bitcast.77), kind=kOutput, calls=%fused_computation.169 | convolution fusion | flops 206046720 | bytes 6819848 | tf_op jit(solution)/shard_map/while/body/eval_jaxpr/sub | solution.py:39
  158.0 4.0 %fusion.26 = bf16[2,64,512]{2,1,0:T(8,128)(2,1)S(1)} fusion(bf16[1536,2,64]{0,2,1:T(8,128)(2,1)S(1)} %bitcast.76, f32[2,512,1536]{2,1,0:T(8,128)} %get-tuple-element.124, f32[2,512]{1,0:T(2,128)S(1)} %get-tuple-element.123), kind=kOutput, calls=%fused_computation.37 | convolution fusion | flops 204537856 | bytes 6819840 | tf_op jit(solution)/shard_map/while/body/eval_jaxpr/hrs,shd->rhd/dot_general | solution.py:40
  162.3 1.9 fusion.20
  164.3 22.1 %reduce-scatter.3.cloned.1.call-done = bf16[128,512]{1,0:T(8,128)(2,1)} async-done(((bf16[512,512]{1,0:T(8,128)(2,1)}), bf16[128,512]{1,0:T(8,128)(2,1)}) %reduce-scatter.3.cloned.1.call-update) | async-done | bytes 131088 | tf_op jit(solution)/shard_map/reduce_scatter | solution.py:178
  189.6 6.8 %all_gather.3 = bf16[512,512]{1,0:T(8,128)(2,1)S(1)} all-gather(bf16[128,512]{1,0:T(8,128)(2,1)S(1)} %multiply_convert_fusion), channel_id=1, replica_groups=mesh['dom'=8,'mp'=4] {'mp'}, dimensions={0}, use_global_device_ids=true | all-gather | bytes 655360 | tf_op jit(solution)/shard_map/all_gather | solution.py:186
  196.4 3.7 %convolution_convert_fusion = bf16[512,512]{1,0:T(8,128)(2,1)} fusion(bf16[512,512]{1,0:T(8,128)(2,1)S(1)} %copy-done, bf16[512,512]{1,0:T(8,128)(2,1)S(1)} %all_gather.3, bf16[512,512]{1,0:T(8,128)(2,1)S(1)} %copy-done.10), kind=kOutput, calls=%fused_computation.31 | convolution fusion | flops 554172416 | bytes 2097152 | tf_op jit(solution)/shard_map/dot_general | solution.py:193
  200.1 22.3 %reduce-scatter.5.cloned.1.call-done = bf16[128,512]{1,0:T(8,128)(2,1)} async-done(((bf16[512,512]{1,0:T(8,128)(2,1)}), bf16[128,512]{1,0:T(8,128)(2,1)}) %reduce-scatter.5.cloned.1.call-update) | async-done | bytes 131088 | tf_op jit(solution)/shard_map/reduce_scatter | solution.py:192
  222.5 1.6 add_convert_fusion
  (96 shorter events, 18.2 us)
Async XLA Ops:
  6.5 189.9 %copy-start = (bf16[512,512]{1,0:T(8,128)(2,1)S(1)}, bf16[512,512]{1,0:T(8,128)(2,1)}, u32[]{:S(2)}) copy-start(bf16[512,512]{1,0:T(8,128)(2,1)} %param.25) | copy-start | bytes 1572868
  6.5 14.3 %copy-start.1 = (bf16[512,512]{1,0:T(8,128)(2,1)S(1)}, bf16[512,512]{1,0:T(8,128)(2,1)}, u32[]{:S(2)}) copy-start(bf16[512,512]{1,0:T(8,128)(2,1)} %param.17) | copy-start | bytes 1572868
  6.5 8.6 %copy-start.9 = (s32[1,8]{1,0:T(1,128)S(1)}, s32[1,8]{1,0:T(1,128)}, u32[]{:S(2)}) copy-start(s32[1,8]{1,0:T(1,128)} %param.28) | copy-start | bytes 100
  6.5 14.2 %copy-start.8 = (s32[2,8]{1,0:T(2,128)S(1)}, s32[2,8]{1,0:T(2,128)}, u32[]{:S(2)}) copy-start(s32[2,8]{1,0:T(2,128)} %param.26) | copy-start | bytes 196
  6.5 14.3 %copy-start.6 = (s32[1,8,128]{2,1,0:T(8,128)S(1)}, s32[1,8,128]{2,1,0:T(8,128)}, u32[]{:S(2)}) copy-start(s32[1,8,128]{2,1,0:T(8,128)} %param.27) | copy-start | bytes 12292
  6.5 14.9 %copy-start.4 = (s32[1,16384]{1,0:T(1,128)S(1)}, s32[1,16384]{1,0:T(1,128)}, u32[]{:S(2)}) copy-start(s32[1,16384]{1,0:T(1,128)} %param.31) | copy-start | bytes 196612
  6.6 15.7 %copy-start.5 = (s32[1,16384]{1,0:T(1,128)S(1)}, s32[1,16384]{1,0:T(1,128)}, u32[]{:S(2)}) copy-start(s32[1,16384]{1,0:T(1,128)} %param.30) | copy-start | bytes 196612
  12.1 100.5 %collective-permute-start = (bf16[512,256]{0,1:T(8,128)(2,1)S(1)}, bf16[512,256]{0,1:T(8,128)(2,1)S(1)}, u32[]{:S(2)}, u32[]{:S(2)}) collective-permute-start(bf16[512,256]{0,1:T(8,128)(2,1)S(1)} %pad_maximum_fusion), channel_id=1, source_target_pairs={{0,4},{4,0},{8,12},{12,8},{16,20},{20,16},{24,28},{28,24},{1,5},{5... | collective-permute-start | bytes 786440 | tf_op jit(solution)/shard_map/ppermute | solution.py:23
  15.8 100.9 %all-to-all-start.1 = ((bf16[8,1,128]{2,1,0:T(2,128)(2,1)}), bf16[8,1,128]{2,1,0:T(2,128)(2,1)S(1)}, u32[]{:S(2)}, u32[]{:S(2)}) async-start(bf16[8,1,128]{2,1,0:T(2,128)(2,1)} %compare_convert_fusion), calls=%async_computation.1 | async-start | bytes 8192 | tf_op jit(solution)/shard_map/all_to_all | solution.py:155
  107.9 14.8 %copy-start.12 = (s32[1,8,128]{2,1,0:T(8,128)S(1)}, s32[1,8,128]{2,1,0:T(8,128)}, u32[]{:S(2)}) copy-start(s32[1,8,128]{2,1,0:T(8,128)} %param.29) | copy-start | bytes 12292
  112.6 40.8 %copy-start.13 = (f32[2]{0:T(128)S(1)}, f32[2]{0:T(128)}, u32[]{:S(2)}) copy-start(f32[2]{0:T(128)} %param.21) | copy-start | bytes 28
  114.0 9.2 %collective-permute-start.3 = (bf16[512,256]{0,1:T(8,128)(2,1)S(1)}, bf16[512,256]{0,1:T(8,128)(2,1)S(1)}, u32[]{:S(2)}, u32[]{:S(2)}) collective-permute-start(bf16[512,256]{0,1:T(8,128)(2,1)S(1)} %get-tuple-element.109), channel_id=1, source_target_pairs={{0,8},{8,0},{4,12},{12,4},{16,24},{24,16},{20,28},{28,20},{1,9},{9... | collective-permute-start | bytes 786440 | tf_op jit(solution)/shard_map/ppermute | solution.py:23
  116.7 17.2 %collective-permute-start.1 = (bf16[512,256]{0,1:T(8,128)(2,1)S(1)}, bf16[512,256]{0,1:T(8,128)(2,1)S(1)}, u32[]{:S(2)}, u32[]{:S(2)}) collective-permute-start(bf16[512,256]{0,1:T(8,128)(2,1)S(1)} %get-tuple-element.108), channel_id=1, source_target_pairs={{0,8},{8,0},{4,12},{12,4},{16,24},{24,16},{20,28},{28,20},{1,9},{9... | collective-permute-start | bytes 786440 | tf_op jit(solution)/shard_map/ppermute | solution.py:23
  116.7 45.6 %all-to-all-start = ((bf16[8,128,128]{2,1,0:T(8,128)(2,1)}), bf16[8,128,128]{2,1,0:T(8,128)(2,1)S(1)}, u32[]{:S(2)}, u32[]{:S(2)}) async-start(bf16[8,128,128]{2,1,0:T(8,128)(2,1)} %broadcast_select_fusion), calls=%async_computation | async-start | bytes 524288 | tf_op jit(solution)/shard_map/all_to_all | solution.py:154
  122.7 63.7 %reduce-scatter.3.cloned.1.call-start = ((), (), s32[]{:S(2)}) async-start(), calls=%async_computation.4 | async-start | bytes 655360 | tf_op jit(solution)/shard_map/reduce_scatter | solution.py:178
  123.9 25.8 %collective-permute-start.4 = (bf16[512,256]{0,1:T(8,128)(2,1)S(1)}, bf16[512,256]{0,1:T(8,128)(2,1)S(1)}, u32[]{:S(2)}, u32[]{:S(2)}) collective-permute-start(bf16[512,256]{0,1:T(8,128)(2,1)S(1)} %broadcast_select_fusion.2), channel_id=1, source_target_pairs={{0,16},{16,0},{4,20},{20,4},{8,24},{24,8},{12,28},{28,12},{1,17},{... | collective-permute-start | bytes 786440 | tf_op jit(solution)/shard_map/ppermute | solution.py:23
  134.5 18.2 %collective-permute-start.2 = (bf16[512,256]{0,1:T(8,128)(2,1)S(1)}, bf16[512,256]{0,1:T(8,128)(2,1)S(1)}, u32[]{:S(2)}, u32[]{:S(2)}) collective-permute-start(bf16[512,256]{0,1:T(8,128)(2,1)S(1)} %broadcast_select_fusion.4), channel_id=1, source_target_pairs={{0,16},{16,0},{4,20},{20,4},{8,24},{24,8},{12,28},{28,12},{1,17},{... | collective-permute-start | bytes 786440 | tf_op jit(solution)/shard_map/ppermute | solution.py:23
  158.0 4.0 %copy-start.3 = (bf16[128,512]{1,0:T(8,128)(2,1)S(1)}, bf16[128,512]{1,0:T(8,128)(2,1)}, u32[]{:S(2)}) copy-start(bf16[128,512]{1,0:T(8,128)(2,1)} %param.22) | copy-start | bytes 393220
  158.0 4.3 %copy-start.11 = (bf16[128,512]{1,0:T(8,128)(2,1)S(1)}, bf16[128,512]{1,0:T(8,128)(2,1)}, u32[]{:S(2)}) copy-start(bf16[128,512]{1,0:T(8,128)(2,1)} %param.23) | copy-start | bytes 393220
  162.0 26.6 %copy-start.7 = (f32[512]{0:T(512)S(1)}, f32[512]{0:T(512)}, u32[]{:S(2)}) copy-start(f32[512]{0:T(512)} %param.19) | copy-start | bytes 6148
  162.0 34.4 %copy-start.10 = (bf16[512,512]{1,0:T(8,128)(2,1)S(1)}, bf16[512,512]{1,0:T(8,128)(2,1)}, u32[]{:S(2)}) copy-start(bf16[512,512]{1,0:T(8,128)(2,1)} %param.24) | copy-start | bytes 1572868
  164.3 58.2 %reduce-scatter.5.cloned.1.call-start = ((), (), s32[]{:S(2)}) async-start(), calls=%async_computation.5 | async-start | bytes 655360 | tf_op jit(solution)/shard_map/reduce_scatter | solution.py:192
  196.4 26.1 %copy-start.2 = (bf16[128,512]{1,0:T(8,128)(2,1)S(1)}, bf16[128,512]{1,0:T(8,128)(2,1)}, u32[]{:S(2)}) copy-start(bf16[128,512]{1,0:T(8,128)(2,1)} %reduce-scatter.3.cloned.1.call-done) | copy-start | bytes 393220
Sparse Core Ops, SparseCore 0:
  164.4 22.0 reduce-scatter.2
  200.3 22.1 reduce-scatter.4
where the time goes:
time: 232 us; the launch traced here: 231 us
  waiting for transfers between devices  68.6 us (30%)
  local copies, waits for them, and re-layouts  64.2 us (28%)
  matrix products  43.9 us (19%)
  starting transfers between devices  19.6 us (8%)
  other arithmetic  14 us (6%)
  between operations  13.7 us (6%)
  blocking collectives  6.79 us (3%)
    gather x1, local copies, waits for them, and re-layouts, body(): quarter[partition_edge_tail[0]]  57.8 us
    ppermute x5, waiting for transfers between devices, swapped_2(): return lax.ppermute(block, axis, route)  24.1 us
    reduce_scatter x1, waiting for transfers between devices, body(): lax.psum_scatter(jnp.dot(hidden, contract_projector, preferred_element_ty...  22.3 us
    reduce_scatter x1, waiting for transfers between devices, body(): lax.psum_scatter(partial_terms.astype(jnp.bfloat16), 'mp', scatter_dimens...  22.1 us
    dot_general x8, matrix products, accumulate(): jnp.einsum('mr,mw->rw', selector, part_values, preferred_element_type=jnp...  21.1 us
    ppermute x5, starting transfers between devices, swapped_2(): return lax.ppermute(block, axis, route)  8.6 us
    dot_general x9, matrix products, accumulate(): jnp.dot(part_flags, selector, preferred_element_type=jnp.float32)  6.8 us
    all_gather x1, blocking collectives, body(): lax.all_gather(normed_share, 'mp', axis=0, tiled=True)  6.79 us
  transfers between devices with their start and end apart: 9, of which 5 were waited for; matrix products, arithmetic and copies ran while one was open for 46% of the time, Pallas kernels for 0%

commit v1 on v0

v1 whole, which is shorter than its diff:
```python
import functools
import math

import jax
import jax.numpy as jnp
from jax import lax
from jax.experimental import pallas as pl
from jax.experimental.pallas import tpu as pltpu
from jax.sharding import PartitionSpec as P


HEAD_SIZE = 64
EPSILON = 1e-05
FLAG_ROWS = 8
EDGE_STEP = 1024

f32 = jnp.float32
bf16 = jnp.bfloat16
f8 = jnp.float8_e4m3fn

VMEM = pl.BlockSpec(memory_space=pltpu.VMEM)
SMEM = pl.BlockSpec(memory_space=pltpu.SMEM)

NT = (((1,), (1,)), ((), ()))
NN = (((1,), (0,)), ((), ()))

PARAMS = pltpu.CompilerParams(vmem_limit_bytes=24 << 20)


def dot(a, b, dims=NN):
    return lax.dot_general(a, b, dims, preferred_element_type=f32)


def norm_rows(rows, gain):
    mean = jnp.mean(rows, -1, keepdims=True)
    centred = rows - mean
    variance = jnp.mean(centred * centred, -1, keepdims=True)
    return (centred * lax.rsqrt(variance + EPSILON) * gain).astype(bf16)


def one_hot_columns(index_row, count, live=None):
    hit = lax.broadcasted_iota(jnp.int32, (count, index_row.shape[1]), 0) == index_row
    if live is not None:
        hit = jnp.logical_and(hit, live)
    return jnp.where(hit, 1.0, 0.0).astype(bf16)


def narrow_one_hot(index_row, count):
    numbers = lax.broadcasted_iota(jnp.int16, (count, index_row.shape[1]), 0)
    hit = numbers == index_row.astype(jnp.int16)
    return jnp.where(hit, jnp.ones((), bf16), jnp.zeros((), bf16)).astype(f8)


def xor_route(count, mask):
    return [(i, i ^ mask) for i in range(count)]


def prologue_kernel(
    place_ref, tally_ref, companion_ref, x_ref, gain_ref, w_ref, sender_ref,
    choice_ref, q_ref, kv_ref, k_ref, v_ref, *out_refs,
):
    one, two = companion_ref[0, 0], companion_ref[1, 0]
    low, high = jnp.minimum(one, two), jnp.maximum(one, two)
    choice_ref[0] = low
    choice_ref[1] = high
    choice_ref[2] = lax.shift_right_logical((high - 1) * (high - 2), 1) + low - 1
    nodes, _ = x_ref.shape
    cols = q_ref.shape[1]
    normed = norm_rows(x_ref[...].astype(f32), gain_ref[...])
    weights = jnp.concatenate([w_ref[0], w_ref[1], w_ref[2]], axis=1)
    projected = dot(normed, weights).astype(bf16)
    q_ref[...] = projected[:, :cols]
    kv_ref[...] = projected[:, cols:]
    k_ref[...] = projected[:, cols : 2 * cols]
    v_ref[...] = projected[:, 2 * cols :]
    me, part = place_ref[0], place_ref[1]
    quarter = x_ref[:, pl.ds(pl.multiple_of(part * cols, 128), cols)]
    quarter_t = quarter.astype(f32).T.astype(bf16)
    cap = sender_ref.shape[1]
    slot = lax.broadcasted_iota(jnp.int32, (1, cap), 1)
    near = len(out_refs)
    for a, out_ref in enumerate(out_refs):
        for h in range(out_ref.shape[0]):
            dest = jnp.bitwise_xor(me, h * near + a)
            live = slot < tally_ref[0, dest]
            pick = one_hot_columns(sender_ref[pl.ds(dest, 1), :], nodes, live)
            out_ref[h, :cols, :] = dot(quarter_t, pick).astype(bf16)
            out_ref[h, cols:, :] = jnp.broadcast_to(
                jnp.where(live, 1.0, 0.0), (FLAG_ROWS, cap)
            ).astype(bf16)


def prologue(place, tally, companion, x, gain, w, sender, near):
    nodes, width = x.shape
    cols = w.shape[2]
    peers, cap = sender.shape
    far = peers // near
    return pl.pallas_call(
        prologue_kernel,
        out_shape=[
            jax.ShapeDtypeStruct((3,), jnp.int32),
            jax.ShapeDtypeStruct((nodes, cols), bf16),
            jax.ShapeDtypeStruct((nodes, 2 * cols), bf16),
            jax.ShapeDtypeStruct((nodes, cols), bf16),
            jax.ShapeDtypeStruct((nodes, cols), bf16),
        ]
        + [jax.ShapeDtypeStruct((far, cols + FLAG_ROWS, cap), bf16)] * near,
        in_specs=[SMEM] * 3 + [VMEM] * 4,
        out_specs=[SMEM] + [VMEM] * (near + 4),
        name="prologue",
        compiler_params=PARAMS,
        cost_estimate=pl.CostEstimate(
            flops=2 * nodes * width * 3 * cols, bytes_accessed=4 << 20, transcendentals=0
        ),
    )(place, tally, companion, x, gain, w, sender)


def edge_kernel(tail_ref, sink_ref, counts_ref):
    nodes = counts_ref.shape[0]
    edges = tail_ref.shape[1]
    step = math.gcd(edges, EDGE_STEP)
    counts_ref[...] = jnp.zeros_like(counts_ref)

    def add(turn, unused):
        at = pl.ds(pl.multiple_of(turn * step, step), step)
        sink = narrow_one_hot(sink_ref[:, at], nodes)
        tail = narrow_one_hot(tail_ref[:, at], nodes)
        counts_ref[...] += dot(sink, tail, NT)
        return unused

    lax.fori_loop(0, edges // step, add, 0)


def edge_counts(tail, sink, nodes):
    edges = tail.shape[1]
    return pl.pallas_call(
        edge_kernel,
        out_shape=jax.ShapeDtypeStruct((nodes, nodes), f32),
        in_specs=[VMEM, VMEM],
        out_specs=VMEM,
        name="edge_counts",
        compiler_params=PARAMS,
        cost_estimate=pl.CostEstimate(
            flops=2 * nodes * nodes * edges, bytes_accessed=2 << 20, transcendentals=0
        ),
    )(tail, sink)


def message_kernel(origins, place_ref, counts_ref, x_ref, landing_ref, *refs):
    count = len(set(i for i, _, _ in origins))
    ins, outs = refs[:count], refs[count:]
    me, part = place_ref[0], place_ref[1]
    nodes = x_ref.shape[0]
    rows, cols = outs[0].shape
    land = jnp.concatenate(
        [
            one_hot_columns(landing_ref[pl.ds(jnp.bitwise_xor(me, k), 1), :], nodes)
            for _, _, k in origins
        ],
        axis=1,
    )
    arrived = jnp.concatenate([ins[i][j] for i, j, _ in origins], axis=1)
    boundary = dot(land, arrived, NT)
    quarter = x_ref[:, pl.ds(pl.multiple_of(part * cols, 128), cols)]
    filled = jnp.concatenate([quarter, jnp.ones((nodes, 128), bf16)], axis=1)
    counts = counts_ref[...]
    high = jnp.floor(counts * (1.0 / 256.0))
    low = counts - 256.0 * high
    total = 256.0 * dot(high.astype(bf16), filled) + dot(low.astype(bf16), filled)
    quarter = quarter.astype(f32)
    degree = total[:, cols : cols + 1] + boundary[:, cols : cols + 1]
    message = (quarter + total[:, :cols] + boundary[:, :cols]) / (1.0 + degree)
    whole_ref = outs[-1]
    whole_ref[...] = message.astype(bf16)
    for k, out_ref in enumerate(outs[:-1]):
        at = jnp.bitwise_xor(part, k) * rows
        out_ref[...] = whole_ref[pl.ds(pl.multiple_of(at, rows), rows), :]


def messages(place, counts, x, landing, arrived, origins, cols, shares):
    nodes = x.shape[0]
    rows = nodes // shares
    return pl.pallas_call(
        functools.partial(message_kernel, origins),
        out_shape=[jax.ShapeDtypeStruct((rows, cols), bf16)] * shares,
        in_specs=[SMEM] + [VMEM] * (3 + len(arrived)),
        out_specs=[VMEM] * shares,
        scratch_shapes=[pltpu.VMEM((nodes, cols), bf16)],
        name="messages",
        compiler_params=PARAMS,
        cost_estimate=pl.CostEstimate(
            flops=2 * nodes * 1024 * 256, bytes_accessed=2 << 20, transcendentals=0
        ),
    )(place, counts, x, landing, *arrived)


def attention_kernel(place_ref, scale_ref, q_ref, own_ref, one_ref, two_ref, *outs):
    part = place_ref[1]
    rows, cols = outs[0].shape
    heads = cols // HEAD_SIZE
    for k, out_ref in enumerate(outs):
        at = pl.multiple_of(jnp.bitwise_xor(part, k) * rows, rows)
        for h in range(heads):
            band = slice(h * HEAD_SIZE, (h + 1) * HEAD_SIZE)
            value_band = slice(cols + h * HEAD_SIZE, cols + (h + 1) * HEAD_SIZE)
            q = q_ref[pl.ds(at, rows), band]
            scores = [
                dot(q, r[:, band], NT) * scale_ref[h] for r in (own_ref, one_ref, two_ref)
            ]
            top = functools.reduce(
                jnp.maximum, [jnp.max(s, -1, keepdims=True) for s in scores]
            )
            powers = [jnp.exp(s - top) for s in scores]
            total = sum(jnp.sum(p, -1, keepdims=True) for p in powers)
            inverse = 1.0 / total
            attended = sum(
                dot((p * inverse).astype(bf16), r[:, value_band])
                for p, r in zip(powers, (own_ref, one_ref, two_ref))
            )
            out_ref[:, band] = attended.astype(bf16)


def attention(place, scale, q, own, one, two, shares):
    nodes, cols = q.shape
    rows = nodes // shares
    return pl.pallas_call(
        attention_kernel,
        out_shape=[jax.ShapeDtypeStruct((rows, cols), bf16)] * shares,
        in_specs=[SMEM, SMEM] + [VMEM] * 4,
        out_specs=[VMEM] * shares,
        name="attention",
        compiler_params=PARAMS,
        cost_estimate=pl.CostEstimate(
            flops=4 * nodes * 3 * nodes * 256, bytes_accessed=2 << 20, transcendentals=2 << 20
        ),
    )(place, scale, q, own, one, two)


def final_kernel(shares, place_ref, x_ref, gain_ref, *refs):
    att, msg, wo, wn, up, down = (refs[i * shares : (i + 1) * shares] for i in range(6))
    out_ref = refs[6 * shares]
    rows = out_ref.shape[0]
    part = place_ref[1]
    mixed = x_ref[pl.ds(pl.multiple_of(part * rows, rows), rows), :].astype(f32)
    terms = jnp.concatenate([r[...] for r in (*att, *msg)], axis=1)
    mixed = mixed + dot(terms, jnp.concatenate([r[...] for r in (*wo, *wn)], axis=0))
    normed = norm_rows(mixed, gain_ref[...])
    total = mixed
    for k in range(shares):
        wide = dot(normed, up[k][...])
        hidden = (0.5 * wide * (1.0 + lax.erf(wide * (0.5**0.5)))).astype(bf16)
        total = total + dot(hidden, down[k][...])
    out_ref[...] = total.astype(bf16)


def final(place, x, gain, att, msg, wo, wn, up, down):
    shares = len(att)
    rows = x.shape[0] // shares
    width = x.shape[1]
    return pl.pallas_call(
        functools.partial(final_kernel, shares),
        out_shape=jax.ShapeDtypeStruct((rows, width), bf16),
        in_specs=[SMEM] + [VMEM] * (2 + 6 * shares),
        out_specs=VMEM,
        name="final",
        compiler_params=PARAMS,
        cost_estimate=pl.CostEstimate(
            flops=2 * rows * width * 4096, bytes_accessed=6 << 20, transcendentals=1 << 18
        ),
    )(place, x, gain, *att, *msg, *wo, *wn, *up, *down)


def gather_pieces(piece, axis):
    count = lax.axis_size(axis)
    pieces = {0: piece}
    bit = count // 2
    while bit:
        for k in list(pieces):
            pieces[k | bit] = lax.ppermute(pieces[k], axis, xor_route(count, bit))
        bit //= 2
    return [pieces[k] for k in range(count)]


def swap_chunks(chunks, axis):
    count = lax.axis_size(axis)
    return [chunks[0]] + [
        lax.ppermute(chunks[k], axis, xor_route(count, k)) for k in range(1, count)
    ]


def layer(
    x,
    mixer_gain,
    perceptron_gain,
    projectors,
    scale,
    out_projector,
    neighbour_projector,
    expand,
    contract,
    companion,
    sender,
    tally,
    landing,
    tail,
    sink,
):
    peers = lax.axis_size("dom")
    shares = lax.axis_size("mp")
    cols = projectors.shape[2]
    place = jnp.stack([lax.axis_index("dom"), lax.axis_index("mp")]).astype(jnp.int32)

    up = gather_pieces(expand, "mp")
    down = gather_pieces(contract, "mp")
    wo = gather_pieces(out_projector, "mp")
    wn = gather_pieces(neighbour_projector, "mp")

    near = 1 << ((peers.bit_length() - 1) // 2)
    far = peers // near
    choice, q, kv, k, v, *outgoing = prologue(
        place, tally, companion, x, mixer_gain[None, :], projectors, sender[0], near
    )

    def shared(outgoing, tail, sink):
        counts = edge_counts(tail, sink, x.shape[0])
        held = [outgoing[0]] + [
            lax.ppermute(outgoing[a], "dom", xor_route(peers, a)) for a in range(1, near)
        ]
        arrived = [
            lax.ppermute(
                jnp.stack([block[h] for block in held]), "dom", xor_route(peers, h * near)
            )
            for h in range(1, far)
        ]
        return counts, held[1:] + arrived

    origins = tuple((a - 1, 0, a) for a in range(1, near)) + tuple(
        (near - 2 + h, a, h * near + a) for h in range(1, far) for a in range(near)
    )

    def send(block, mask):
        return lax.ppermute(block, "dom", xor_route(peers, mask))

    operands = (kv, k, v, outgoing, tail, sink)
    if peers * (peers - 1) // 2 <= 32:
        branches = []
        for high in range(1, peers):
            for low in range(1, high):

                def branch(kv, k, v, *rest, low=low, high=high):
                    if low & high & (peers // 2):
                        one_k, one_v = send(k, low), send(v, low)
                        two_k, two_v = send(one_k, low ^ high), send(one_v, low ^ high)
                        one = jnp.concatenate([one_k, one_v], axis=1)
                        two = jnp.concatenate([two_k, two_v], axis=1)
                    else:
                        one, two = send(kv, low), send(kv, high)
                    return (one, two) + shared(*rest)

                branches.append(branch)
        one, two, counts, arrived = lax.switch(choice[2], branches, *operands)
    else:
        hops = [lambda kv, mask=mask: send(kv, mask) for mask in range(1, peers)]
        one = lax.switch(choice[0] - 1, hops, kv)
        two = lax.switch(choice[1] - 1, hops, kv)
        counts, arrived = shared(outgoing, tail, sink)

    msg = messages(place, counts, x, landing[0], arrived, origins, cols, shares)
    msg = swap_chunks(msg, "mp")
    att = attention(place, scale, q, kv, one, two, shares)
    att = swap_chunks(att, "mp")
    return final(place, x, perceptron_gain[None, :], att, msg, wo, wn, up, down)


def solution(mesh):
    return jax.shard_map(
        layer,
        mesh=mesh,
        in_specs=(
            P("dom", None),
            P(),
            P(),
            P(None, None, "mp"),
            P("mp"),
            P("mp", None),
            P("mp", None),
            P(None, "mp"),
            P("mp", None),
            P(),
            P("dom", None, None),
            P("dom", None),
            P("dom", None, None),
            P("dom", None),
            P("dom", None),
        ),
        out_specs=P(("dom", "mp"), None),
        check_vma=False,
    )
```

time: 232 us -> 81.9 us (0.35)
  local copies, waits for them, and re-layouts: 64.2 us -> 6.04 us
  matrix products: 43.9 us -> 0 us
  waiting for transfers between devices: 68.6 us -> 36.1 us
  Pallas kernels: 0 us -> 19.3 us
  other arithmetic: 14 us -> 0.1 us
  between operations: 13.7 us -> 0.79 us
  blocking collectives: 6.79 us -> 0 us
    gather x2 -> x0, local copies, waits for them, and re-layouts: 61 us -> none  [the longest x1 57.8 us: body(): quarter[partition_edge_tail[0]]]
    reduce_scatter x2 -> x0, waiting for transfers between devices: 44.5 us -> none  [the longest x1 22.3 us: body(): lax.psum_scatter(jnp.dot(hidden, contract_projector, preferred_element_ty...]
    dot_general x21 -> x0, matrix products: 37.8 us -> none  [the longest x8 21.1 us: accumulate(): jnp.einsum('mr,mw->rw', selector, part_values, preferred_element_type=jnp...]
    pallas_call x0 -> x5, Pallas kernels: none -> 19.3 us  [the longest x1 6.81 us: edge_counts(): pl.pallas_call(edge_kernel, out_shape=jax.ShapeDtypeStruct((nodes, nodes)...]
    ppermute x5 -> x24, waiting for transfers between devices: 24.1 us -> 36.1 us  [the longest x6 22 us: swap_chunks(): lax.ppermute(chunks[k], axis, xor_route(count, k))]
    all_to_all x2 -> x0, starting transfers between devices: 10.9 us -> none  [the longest x1 5.99 us: body(): lax.all_to_all(outgoing, 'dom', split_axis=0, concat_axis=0, tiled=True)]
    ppermute x5 -> x24, starting transfers between devices: 8.6 us -> 18.8 us  [the longest x12 5.83 us: gather_pieces(): pieces[k | bit] = lax.ppermute(pieces[k], axis, xor_route(count, bit))]
    all_gather x1 -> x0, blocking collectives: 6.79 us -> none  [body(): lax.all_gather(normed_share, 'mp', axis=0, tiled=True)]
  transfers between devices with their start and end apart: 9 -> 24, of which waited for: 5 -> 9; matrix products, arithmetic and copies ran while one was open for 46% -> 0% of each run, Pallas kernels for 0% -> 18%
where the time goes in v1:
time: 81.9 us; the launch traced here: 81.6 us
  waiting for transfers between devices  36.1 us (44%)
  Pallas kernels  19.3 us (24%)
  starting transfers between devices  18.8 us (23%)
  local copies, waits for them, and re-layouts  6.04 us (7%)
    ppermute x6, waiting for transfers between devices, swap_chunks(): lax.ppermute(chunks[k], axis, xor_route(count, k))  22 us
    ppermute x12, waiting for transfers between devices, gather_pieces(): pieces[k | bit] = lax.ppermute(pieces[k], axis, xor_route(count, bit))  7.97 us
    pallas_call x1, Pallas kernels, edge_counts(): pl.pallas_call(edge_kernel, out_shape=jax.ShapeDtypeStruct((nodes, nodes)...  6.81 us
    ppermute x1, waiting for transfers between devices, shared(): lax.ppermute(outgoing[a], 'dom', xor_route(peers, a))  6.18 us
    pallas_call x1, Pallas kernels, attention(): pl.pallas_call(attention_kernel, out_shape=[jax.ShapeDtypeStruct((rows, c...  5.87 us
    ppermute x12, starting transfers between devices, gather_pieces(): pieces[k | bit] = lax.ppermute(pieces[k], axis, xor_route(count, bit))  5.83 us
    ppermute x2, starting transfers between devices, send(): return lax.ppermute(block, 'dom', xor_route(peers, mask))  5.65 us
    unnamed x38, local copies, waits for them, and re-layouts  4.8 us
  transfers between devices with their start and end apart: 24, of which 9 were waited for; matrix products, arithmetic and copies ran while one was open for 0% of the time, Pallas kernels for 18%

profile of v1, /device:TPU:0, one launch (start us, length us, event | category | flops | bytes accessed | tf_op | source)
XLA Modules:
  0.0 81.6 jit_solution(13120925491330302767)
XLA Ops:
  0.1 0.5 copy-done.7
  0.8 1.0 %copy-done = bf16[512,512]{1,0:T(8,128)(2,1)S(1)} copy-done((bf16[512,512]{1,0:T(8,128)(2,1)S(1)}, bf16[512,512]{1,0:T(8,128)(2,1)}, u32[]{:S(2)}) %copy-start) | copy-done | bytes 524312
  1.8 1.0 %copy-done.4 = bf16[3,512,128]{2,1,0:T(8,128)(2,1)S(1)} copy-done((bf16[3,512,128]{2,1,0:T(8,128)(2,1)S(1)}, bf16[3,512,128]{2,1,0:T(8,128)(2,1)}, u32[]{:S(2)}) %copy-start.4) | copy-done | bytes 393240
  2.8 1.9 %prologue.1 = (s32[3]{0:T(128)S(1)}, bf16[512,128]{1,0:T(8,128)(2,1)S(1)}, bf16[512,256]{1,0:T(8,128)(2,1)S(1)}, bf16[512,128]{1,0:T(8,128)(2,1)S(1)}, bf16[512,...) custom-call(s32[2]{0:T(128)S(1)} %pad_add_fusion.place_ref, ...), custom_call_target="tpu_custom_call" | custom-call | flops 201326592 | bytes 4194304 | tf_op jit(solution)/shard_map/prologue/pallas_call | solution.py:98
  4.8 0.6 slice.381
  6.0 24.8 %conditional.1 = (bf16[512,256]{1,0:T(8,128)(2,1)}, bf16[512,256]{1,0:T(8,128)(2,1)}, f32[512,512]{1,0:T(8,128)S(1)}, bf16[4,136,128]{2,1,0:T(8,128)(2,1)}, bf16...) conditional(s32[]{:T(128)} %bitcast.5, ...), branch_computations={%region_0.0_spmd, %region_1.0_spmd, %region_2.0_spmd, %region_3.0_... | conditional | flops 8591087616 | bytes 8028564 | solution.py:361
  6.1 3.1 %collective-permute-start.18 = (bf16[512,256]{1,0:T(8,128)(2,1)S(1)}, bf16[512,256]{1,0:T(8,128)(2,1)}, u32[]{:S(2)}, u32[]{:S(2)}) collective-permute-start(bf16[512,256]{1,0:T(8,128)(2,1)S(1)} %get-tuple-element.242), channel_id=1, source_target_pairs={{0,4},{4,0},{8,12},{12,8},{16,20},{20,16},{24,28},{28,24},{1,5},{5... | collective-permute-start | bytes 786440 | tf_op jit(solution)/shard_map/cond/branch_3_fun/ppermute | solution.py:342
  9.2 2.6 %collective-permute-start.19 = (bf16[512,256]{1,0:T(8,128)(2,1)S(1)}, bf16[512,256]{1,0:T(8,128)(2,1)}, u32[]{:S(2)}, u32[]{:S(2)}) collective-permute-start(bf16[512,256]{1,0:T(8,128)(2,1)S(1)} %get-tuple-element.242), channel_id=1, source_target_pairs={{0,16},{4,20},{8,24},{12,28},{16,0},{20,4},{24,8},{28,12},{1,17},{... | collective-permute-start | bytes 786440 | tf_op jit(solution)/shard_map/cond/branch_3_fun/ppermute | solution.py:342
  11.7 0.5 collective-permute-start.20
  12.3 6.2 %collective-permute-done.20 = bf16[4,136,128]{2,1,0:T(8,128)(2,1)S(1)} collective-permute-done((bf16[4,136,128]{2,1,0:T(8,128)(2,1)S(1)}, bf16[4,136,128]{2,1,0:T(8,128)(2,1)S(1)}, u32[]{:S(2)}, u32[]{:S(2)}) %collective-permute-start.20) | collective-permute-done | bytes 139296 | tf_op jit(solution)/shard_map/cond/branch_3_fun/ppermute | solution.py:327
  18.5 0.6 copy-done.19
  19.1 1.8 %collective-permute-start.21 = (bf16[2,136,128]{2,1,0:T(8,128)(2,1)S(1)}, bf16[2,136,128]{2,1,0:T(8,128)(2,1)}, u32[]{:S(2)}, u32[]{:S(2)}) collective-permute-start(bf16[2,136,128]{2,1,0:T(8,128)(2,1)S(1)} %pad_maximum_fusion.9), channel_id=1, source_target_pairs={{0,8},{4,12},{8,0},{12,4},{16,24},{20,28},{24,16},{28,20},{1,9},{5... | collective-permute-start | bytes 208904 | tf_op jit(solution)/shard_map/cond/branch_3_fun/ppermute | solution.py:330
  20.9 2.7 %collective-permute-start.22 = (bf16[2,136,128]{2,1,0:T(8,128)(2,1)S(1)}, bf16[2,136,128]{2,1,0:T(8,128)(2,1)}, u32[]{:S(2)}, u32[]{:S(2)}) collective-permute-start(bf16[2,136,128]{2,1,0:T(8,128)(2,1)S(1)} %pad_maximum_fusion.10), channel_id=1, source_target_pairs={{0,16},{4,20},{8,24},{12,28},{16,0},{20,4},{24,8},{28,12},{1,17},{... | collective-permute-start | bytes 208904 | tf_op jit(solution)/shard_map/cond/branch_3_fun/ppermute | solution.py:330
  23.7 6.8 %edge_counts.24 = f32[512,512]{1,0:T(8,128)S(1)} custom-call(s32[1,16384]{1,0:T(1,128)S(1)} %get-tuple-element.243.tail_ref, s32[1,16384]{1,0:T(1,128)S(1)} %get-tuple-element.244.sink_ref), custom_call_target="tpu_custom_call" | custom-call | flops 8589934592 | bytes 2097152 | tf_op jit(solution)/shard_map/cond/branch_3_fun/edge_counts/pallas_call | solution.py:136
  30.8 1.8 %collective-permute-start.151 = (bf16[512,512]{1,0:T(8,128)(2,1)S(1)}, bf16[512,512]{1,0:T(8,128)(2,1)S(1)}, u32[]{:S(2)}, u32[]{:S(2)}) collective-permute-start(bf16[512,512]{1,0:T(8,128)(2,1)S(1)} %copy-done.2), channel_id=1, source_target_pairs={{0,2},{1,3},{2,0},{3,1},{4,6},{5,7},{6,4},{7,5},{8,10},{9,11},{10,... | collective-permute-start | bytes 1572872 | tf_op jit(solution)/shard_map/ppermute | solution.py:279
  32.9 0.7 copy-done.8
  33.6 5.9 %attention.1 = (bf16[128,128]{1,0:T(8,128)(2,1)S(1)}, bf16[128,128]{1,0:T(8,128)(2,1)S(1)}, bf16[128,128]{1,0:T(8,128)(2,1)S(1)}, bf16[128,128]{1,0:T(8,128)(2,1)S(1)}) custom-call(s32[2]{0:T(128)S(1)} %copy-done.8, f32[2]{0:T(128)S(1)} %copy-done.15, bf16[512,128]{1,0:T(8,128)(2,1)S(1)} %get-tuple-element.360.q_ref, ...), custom_call_target="tpu_custom_call" | custom-call | flops 805306368 | bytes 2097152 | tf_op jit(solution)/shard_map/attention/pallas_call | solution.py:226
  39.5 1.8 %collective-permute-start.139 = (bf16[128,128]{1,0:T(8,128)(2,1)S(1)}, bf16[128,128]{1,0:T(8,128)(2,1)S(1)}, u32[]{:S(2)}, u32[]{:S(2)}) collective-permute-start(bf16[128,128]{1,0:T(8,128)(2,1)S(1)} %get-tuple-element.371), channel_id=1, source_target_pairs={{0,2},{1,3},{2,0},{3,1},{4,6},{5,7},{6,4},{7,5},{8,10},{9,11},{10,... | collective-permute-start | bytes 98312 | tf_op jit(solution)/shard_map/ppermute | solution.py:287
  41.8 13.9 %collective-permute-done.139.refs_2_ = bf16[128,128]{1,0:T(8,128)(2,1)S(1)} collective-permute-done((bf16[128,128]{1,0:T(8,128)(2,1)S(1)}, bf16[128,128]{1,0:T(8,128)(2,1)S(1)}, u32[]{:S(2)}, u32[]{:S(2)}) %collective-permute-start.139) | collective-permute-done | bytes 32800 | tf_op jit(solution)/shard_map/ppermute | solution.py:287
  55.6 1.7 %collective-permute-start.145 = (bf16[128,512]{1,0:T(8,128)(2,1)S(1)}, bf16[128,512]{1,0:T(8,128)(2,1)S(1)}, u32[]{:S(2)}, u32[]{:S(2)}) collective-permute-start(bf16[128,512]{1,0:T(8,128)(2,1)S(1)} %copy-done.5), channel_id=1, source_target_pairs={{0,2},{1,3},{2,0},{3,1},{4,6},{5,7},{6,4},{7,5},{8,10},{9,11},{10,... | collective-permute-start | bytes 393224 | tf_op jit(solution)/shard_map/ppermute | solution.py:279
  57.3 0.7 copy-done.10
  58.0 1.8 %messages.1 = (bf16[128,128]{1,0:T(8,128)(2,1)S(1)}, bf16[128,128]{1,0:T(8,128)(2,1)S(1)}, bf16[128,128]{1,0:T(8,128)(2,1)S(1)}, bf16[128,128]{1,0:T(8,128)(2,1)S(1)}) custom-call(s32[2]{0:T(128)S(1)} %copy-done.8, f32[512,512]{1,0:T(8,128)S(1)} %get-tuple-element.373.counts_ref, bf16[512,512]{1,0:T(8,128)(2,1)S(1)} %copy-done.1, s32[8,128]{1,0:T(8,128)S(1)} %bitcast.8, ...), custom_call_target="tpu_custom_call" | custom-call | flops 268435456 | bytes 2097152 | tf_op jit(solution)/shard_map/messages/pallas_call | solution.py:183
  59.9 1.2 %collective-permute-done.141.refs_5_ = bf16[128,128]{1,0:T(8,128)(2,1)S(1)} collective-permute-done((bf16[128,128]{1,0:T(8,128)(2,1)S(1)}, bf16[128,128]{1,0:T(8,128)(2,1)S(1)}, u32[]{:S(2)}, u32[]{:S(2)}) %collective-permute-start.141) | collective-permute-done | bytes 32800 | tf_op jit(solution)/shard_map/ppermute | solution.py:287
  61.4 3.6 %collective-permute-done.142.refs_6_ = bf16[128,128]{1,0:T(8,128)(2,1)S(1)} collective-permute-done((bf16[128,128]{1,0:T(8,128)(2,1)S(1)}, bf16[128,128]{1,0:T(8,128)(2,1)S(1)}, u32[]{:S(2)}, u32[]{:S(2)}) %collective-permute-start.142) | collective-permute-done | bytes 32800 | tf_op jit(solution)/shard_map/ppermute | solution.py:287
  65.0 3.3 %collective-permute-done.143.refs_7_ = bf16[128,128]{1,0:T(8,128)(2,1)S(1)} collective-permute-done((bf16[128,128]{1,0:T(8,128)(2,1)S(1)}, bf16[128,128]{1,0:T(8,128)(2,1)S(1)}, u32[]{:S(2)}, u32[]{:S(2)}) %collective-permute-start.143) | collective-permute-done | bytes 32800 | tf_op jit(solution)/shard_map/ppermute | solution.py:287
  68.4 0.5 collective-permute-start.150
  69.0 0.4 collective-permute-start.152
  70.1 5.2 %collective-permute-done.148.refs_14_ = bf16[128,512]{1,0:T(8,128)(2,1)S(1)} collective-permute-done((bf16[128,512]{1,0:T(8,128)(2,1)S(1)}, bf16[128,512]{1,0:T(8,128)(2,1)S(1)}, u32[]{:S(2)}, u32[]{:S(2)}) %collective-permute-start.148) | collective-permute-done | bytes 131104 | tf_op jit(solution)/shard_map/ppermute | solution.py:279
  75.3 1.3 %collective-permute-done.146.refs_11_ = bf16[128,512]{1,0:T(8,128)(2,1)S(1)} collective-permute-done((bf16[128,512]{1,0:T(8,128)(2,1)S(1)}, bf16[128,512]{1,0:T(8,128)(2,1)S(1)}, u32[]{:S(2)}, u32[]{:S(2)}) %collective-permute-start.146) | collective-permute-done | bytes 131104 | tf_op jit(solution)/shard_map/ppermute | solution.py:279
  76.8 1.2 %collective-permute-done.149.refs_15_ = bf16[128,512]{1,0:T(8,128)(2,1)S(1)} collective-permute-done((bf16[128,512]{1,0:T(8,128)(2,1)S(1)}, bf16[128,512]{1,0:T(8,128)(2,1)S(1)}, u32[]{:S(2)}, u32[]{:S(2)}) %collective-permute-start.149) | collective-permute-done | bytes 131104 | tf_op jit(solution)/shard_map/ppermute | solution.py:279
  78.0 0.7 copy-done.12
  78.7 2.9 %final.1 = bf16[128,512]{1,0:T(8,128)(2,1)} custom-call(s32[2]{0:T(128)S(1)} %copy-done.8, bf16[512,512]{1,0:T(8,128)(2,1)S(1)} %copy-done.1, f32[1,512]{1,0:T(1,128)S(1)} %bitcast.10, bf16[128,128]{1,0:T(8,128)(2,1)S(1)} %get-tuple-element.369.refs_0_, bf16[128,128]{1,0:T(8,128)(2,1)S(1)} %collective-permute-done.138.refs_1_, ...), custom_call_target="tpu_custom_call" | custom-call | flops 536870912 | bytes 6291456 | tf_op jit(solution)/shard_map/final/pallas_call | solution.py:260
  (69 shorter events, 2.7 us)
Async XLA Ops:
  2.8 3.2 %copy-start.38 = (s32[1,16384]{1,0:T(1,128)S(1)}, s32[1,16384]{1,0:T(1,128)}, u32[]{:S(2)}) copy-start(s32[1,16384]{1,0:T(1,128)} %param.49) | copy-start | bytes 196612
  2.8 3.2 %copy-start.39 = (s32[1,16384]{1,0:T(1,128)S(1)}, s32[1,16384]{1,0:T(1,128)}, u32[]{:S(2)}) copy-start(s32[1,16384]{1,0:T(1,128)} %param.50) | copy-start | bytes 196612
  6.0 24.8 %copy-start.2 = (bf16[512,512]{1,0:T(8,128)(2,1)S(1)}, bf16[512,512]{1,0:T(8,128)(2,1)}, u32[]{:S(2)}) copy-start(bf16[512,512]{1,0:T(8,128)(2,1)} %refs_16_.1) | copy-start | bytes 1572868
  6.0 26.6 %copy-start.3 = (bf16[512,512]{1,0:T(8,128)(2,1)S(1)}, bf16[512,512]{1,0:T(8,128)(2,1)}, u32[]{:S(2)}) copy-start(bf16[512,512]{1,0:T(8,128)(2,1)} %refs_20_.1) | copy-start | bytes 1572868
  6.1 24.4 %collective-permute-start.18 = (bf16[512,256]{1,0:T(8,128)(2,1)S(1)}, bf16[512,256]{1,0:T(8,128)(2,1)}, u32[]{:S(2)}, u32[]{:S(2)}) collective-permute-start(bf16[512,256]{1,0:T(8,128)(2,1)S(1)} %get-tuple-element.242), channel_id=1, source_target_pairs={{0,4},{4,0},{8,12},{12,8},{16,20},{20,16},{24,28},{28,24},{1,5},{5... | collective-permute-start | bytes 786440 | tf_op jit(solution)/shard_map/cond/branch_3_fun/ppermute | solution.py:342
  9.2 21.4 %collective-permute-start.19 = (bf16[512,256]{1,0:T(8,128)(2,1)S(1)}, bf16[512,256]{1,0:T(8,128)(2,1)}, u32[]{:S(2)}, u32[]{:S(2)}) collective-permute-start(bf16[512,256]{1,0:T(8,128)(2,1)S(1)} %get-tuple-element.242), channel_id=1, source_target_pairs={{0,16},{4,20},{8,24},{12,28},{16,0},{20,4},{24,8},{28,12},{1,17},{... | collective-permute-start | bytes 786440 | tf_op jit(solution)/shard_map/cond/branch_3_fun/ppermute | solution.py:342
  11.7 6.7 %collective-permute-start.20 = (bf16[4,136,128]{2,1,0:T(8,128)(2,1)S(1)}, bf16[4,136,128]{2,1,0:T(8,128)(2,1)S(1)}, u32[]{:S(2)}, u32[]{:S(2)}) collective-permute-start(bf16[4,136,128]{2,1,0:T(8,128)(2,1)S(1)} %get-tuple-element.245), channel_id=1, source_target_pairs={{0,4},{4,0},{8,12},{12,8},{16,20},{20,16},{24,28},{28,24},{1,5},{5... | collective-permute-start | bytes 417800 | tf_op jit(solution)/shard_map/cond/branch_3_fun/ppermute | solution.py:327
  19.1 11.4 %collective-permute-start.21 = (bf16[2,136,128]{2,1,0:T(8,128)(2,1)S(1)}, bf16[2,136,128]{2,1,0:T(8,128)(2,1)}, u32[]{:S(2)}, u32[]{:S(2)}) collective-permute-start(bf16[2,136,128]{2,1,0:T(8,128)(2,1)S(1)} %pad_maximum_fusion.9), channel_id=1, source_target_pairs={{0,8},{4,12},{8,0},{12,4},{16,24},{20,28},{24,16},{28,20},{1,9},{5... | collective-permute-start | bytes 208904 | tf_op jit(solution)/shard_map/cond/branch_3_fun/ppermute | solution.py:330
  20.9 9.6 %collective-permute-start.22 = (bf16[2,136,128]{2,1,0:T(8,128)(2,1)S(1)}, bf16[2,136,128]{2,1,0:T(8,128)(2,1)}, u32[]{:S(2)}, u32[]{:S(2)}) collective-permute-start(bf16[2,136,128]{2,1,0:T(8,128)(2,1)S(1)} %pad_maximum_fusion.10), channel_id=1, source_target_pairs={{0,16},{4,20},{8,24},{12,28},{16,0},{20,4},{24,8},{28,12},{1,17},{... | collective-permute-start | bytes 208904 | tf_op jit(solution)/shard_map/cond/branch_3_fun/ppermute | solution.py:330
  23.6 6.9 %collective-permute-start.23 = (bf16[2,136,128]{2,1,0:T(8,128)(2,1)S(1)}, bf16[2,136,128]{2,1,0:T(8,128)(2,1)}, u32[]{:S(2)}, u32[]{:S(2)}) collective-permute-start(bf16[2,136,128]{2,1,0:T(8,128)(2,1)S(1)} %pad_maximum_fusion.11), channel_id=1, source_target_pairs={{0,24},{4,28},{8,16},{12,20},{16,8},{20,12},{24,0},{28,4},{1,25},{... | collective-permute-start | bytes 208904 | tf_op jit(solution)/shard_map/cond/branch_3_fun/ppermute | solution.py:330
  30.8 38.1 %collective-permute-start.151 = (bf16[512,512]{1,0:T(8,128)(2,1)S(1)}, bf16[512,512]{1,0:T(8,128)(2,1)S(1)}, u32[]{:S(2)}, u32[]{:S(2)}) collective-permute-start(bf16[512,512]{1,0:T(8,128)(2,1)S(1)} %copy-done.2), channel_id=1, source_target_pairs={{0,2},{1,3},{2,0},{3,1},{4,6},{5,7},{6,4},{7,5},{8,10},{9,11},{10,... | collective-permute-start | bytes 1572872 | tf_op jit(solution)/shard_map/ppermute | solution.py:279
  32.6 36.8 %collective-permute-start.154 = (bf16[512,512]{1,0:T(8,128)(2,1)S(1)}, bf16[512,512]{1,0:T(8,128)(2,1)S(1)}, u32[]{:S(2)}, u32[]{:S(2)}) collective-permute-start(bf16[512,512]{1,0:T(8,128)(2,1)S(1)} %copy-done.3), channel_id=1, source_target_pairs={{0,2},{1,3},{2,0},{3,1},{4,6},{5,7},{6,4},{7,5},{8,10},{9,11},{10,... | collective-permute-start | bytes 1572872 | tf_op jit(solution)/shard_map/ppermute | solution.py:279
  33.6 7.8 %copy-start.5 = (bf16[128,512]{1,0:T(8,128)(2,1)S(1)}, bf16[128,512]{1,0:T(8,128)(2,1)}, u32[]{:S(2)}) copy-start(bf16[128,512]{1,0:T(8,128)(2,1)} %refs_8_.1) | copy-start | bytes 393220
  33.6 23.7 %copy-start.1 = (bf16[512,512]{1,0:T(8,128)(2,1)S(1)}, bf16[512,512]{1,0:T(8,128)(2,1)}, u32[]{:S(2)}) copy-start(bf16[512,512]{1,0:T(8,128)(2,1)} %x_ref.5) | copy-start | bytes 1572868
  33.6 23.7 %copy-start.37 = (bf16[4,136,128]{2,1,0:T(8,128)(2,1)S(1)}, bf16[4,136,128]{2,1,0:T(8,128)(2,1)}, u32[]{:S(2)}) copy-start(bf16[4,136,128]{2,1,0:T(8,128)(2,1)} %get-tuple-element.374.refs_0_) | copy-start | bytes 417796
  39.5 1.9 %collective-permute-start.138 = (bf16[128,128]{1,0:T(8,128)(2,1)S(1)}, bf16[128,128]{1,0:T(8,128)(2,1)S(1)}, u32[]{:S(2)}, u32[]{:S(2)}) collective-permute-start(bf16[128,128]{1,0:T(8,128)(2,1)S(1)} %get-tuple-element.370), channel_id=1, source_target_pairs={{0,1},{1,0},{2,3},{3,2},{4,5},{5,4},{6,7},{7,6},{8,9},{9,8},{10,11... | collective-permute-start | bytes 98312 | tf_op jit(solution)/shard_map/ppermute | solution.py:287
  39.5 16.1 %collective-permute-start.139 = (bf16[128,128]{1,0:T(8,128)(2,1)S(1)}, bf16[128,128]{1,0:T(8,128)(2,1)S(1)}, u32[]{:S(2)}, u32[]{:S(2)}) collective-permute-start(bf16[128,128]{1,0:T(8,128)(2,1)S(1)} %get-tuple-element.371), channel_id=1, source_target_pairs={{0,2},{1,3},{2,0},{3,1},{4,6},{5,7},{6,4},{7,5},{8,10},{9,11},{10,... | collective-permute-start | bytes 98312 | tf_op jit(solution)/shard_map/ppermute | solution.py:287
  41.3 18.5 %collective-permute-start.140 = (bf16[128,128]{1,0:T(8,128)(2,1)S(1)}, bf16[128,128]{1,0:T(8,128)(2,1)S(1)}, u32[]{:S(2)}, u32[]{:S(2)}) collective-permute-start(bf16[128,128]{1,0:T(8,128)(2,1)S(1)} %get-tuple-element.372), channel_id=1, source_target_pairs={{0,3},{1,2},{2,1},{3,0},{4,7},{5,6},{6,5},{7,4},{8,11},{9,10},{10,... | collective-permute-start | bytes 98312 | tf_op jit(solution)/shard_map/ppermute | solution.py:287
  41.4 27.0 %collective-permute-start.144 = (bf16[128,512]{1,0:T(8,128)(2,1)S(1)}, bf16[128,512]{1,0:T(8,128)(2,1)S(1)}, u32[]{:S(2)}, u32[]{:S(2)}) collective-permute-start(bf16[128,512]{1,0:T(8,128)(2,1)S(1)} %copy-done.5), channel_id=1, source_target_pairs={{0,1},{1,0},{2,3},{3,2},{4,5},{5,4},{6,7},{7,6},{8,9},{9,8},{10,11... | collective-permute-start | bytes 393224 | tf_op jit(solution)/shard_map/ppermute | solution.py:279
  55.6 13.3 %collective-permute-start.145 = (bf16[128,512]{1,0:T(8,128)(2,1)S(1)}, bf16[128,512]{1,0:T(8,128)(2,1)S(1)}, u32[]{:S(2)}, u32[]{:S(2)}) collective-permute-start(bf16[128,512]{1,0:T(8,128)(2,1)S(1)} %copy-done.5), channel_id=1, source_target_pairs={{0,2},{1,3},{2,0},{3,1},{4,6},{5,7},{6,4},{7,5},{8,10},{9,11},{10,... | collective-permute-start | bytes 393224 | tf_op jit(solution)/shard_map/ppermute | solution.py:279
  58.0 10.4 %copy-start.6 = (bf16[128,512]{1,0:T(8,128)(2,1)S(1)}, bf16[128,512]{1,0:T(8,128)(2,1)}, u32[]{:S(2)}) copy-start(bf16[128,512]{1,0:T(8,128)(2,1)} %refs_12_.1) | copy-start | bytes 393220
  59.8 1.3 %collective-permute-start.141 = (bf16[128,128]{1,0:T(8,128)(2,1)S(1)}, bf16[128,128]{1,0:T(8,128)(2,1)S(1)}, u32[]{:S(2)}, u32[]{:S(2)}) collective-permute-start(bf16[128,128]{1,0:T(8,128)(2,1)S(1)} %get-tuple-element.379), channel_id=1, source_target_pairs={{0,1},{1,0},{2,3},{3,2},{4,5},{5,4},{6,7},{7,6},{8,9},{9,8},{10,11... | collective-permute-start | bytes 98312 | tf_op jit(solution)/shard_map/ppermute | solution.py:287
  61.1 3.9 %collective-permute-start.142 = (bf16[128,128]{1,0:T(8,128)(2,1)S(1)}, bf16[128,128]{1,0:T(8,128)(2,1)S(1)}, u32[]{:S(2)}, u32[]{:S(2)}) collective-permute-start(bf16[128,128]{1,0:T(8,128)(2,1)S(1)} %get-tuple-element.380), channel_id=1, source_target_pairs={{0,2},{1,3},{2,0},{3,1},{4,6},{5,7},{6,4},{7,5},{8,10},{9,11},{10,... | collective-permute-start | bytes 98312 | tf_op jit(solution)/shard_map/ppermute | solution.py:287
  65.0 3.3 %collective-permute-start.143 = (bf16[128,128]{1,0:T(8,128)(2,1)S(1)}, bf16[128,128]{1,0:T(8,128)(2,1)S(1)}, u32[]{:S(2)}, u32[]{:S(2)}) collective-permute-start(bf16[128,128]{1,0:T(8,128)(2,1)S(1)} %get-tuple-element.381), channel_id=1, source_target_pairs={{0,3},{1,2},{2,1},{3,0},{4,7},{5,6},{6,5},{7,4},{8,11},{9,10},{10,... | collective-permute-start | bytes 98312 | tf_op jit(solution)/shard_map/ppermute | solution.py:287
  68.4 1.3 %collective-permute-start.147 = (bf16[128,512]{1,0:T(8,128)(2,1)S(1)}, bf16[128,512]{1,0:T(8,128)(2,1)S(1)}, u32[]{:S(2)}, u32[]{:S(2)}) collective-permute-start(bf16[128,512]{1,0:T(8,128)(2,1)S(1)} %copy-done.6), channel_id=1, source_target_pairs={{0,1},{1,0},{2,3},{3,2},{4,5},{5,4},{6,7},{7,6},{8,9},{9,8},{10,11... | collective-permute-start | bytes 393224 | tf_op jit(solution)/shard_map/ppermute | solution.py:279
  68.4 9.6 %collective-permute-start.150 = (bf16[512,512]{1,0:T(8,128)(2,1)S(1)}, bf16[512,512]{1,0:T(8,128)(2,1)S(1)}, u32[]{:S(2)}, u32[]{:S(2)}) collective-permute-start(bf16[512,512]{1,0:T(8,128)(2,1)S(1)} %copy-done.2), channel_id=1, source_target_pairs={{0,1},{1,0},{2,3},{3,2},{4,5},{5,4},{6,7},{7,6},{8,9},{9,8},{10,11... | collective-permute-start | bytes 1572872 | tf_op jit(solution)/shard_map/ppermute | solution.py:279
  68.9 9.1 %collective-permute-start.153 = (bf16[512,512]{1,0:T(8,128)(2,1)S(1)}, bf16[512,512]{1,0:T(8,128)(2,1)S(1)}, u32[]{:S(2)}, u32[]{:S(2)}) collective-permute-start(bf16[512,512]{1,0:T(8,128)(2,1)S(1)} %copy-done.3), channel_id=1, source_target_pairs={{0,1},{1,0},{2,3},{3,2},{4,5},{5,4},{6,7},{7,6},{8,9},{9,8},{10,11... | collective-permute-start | bytes 1572872 | tf_op jit(solution)/shard_map/ppermute | solution.py:279
  69.0 9.1 %collective-permute-start.152 = (bf16[512,512]{1,0:T(8,128)(2,1)S(1)}, bf16[512,512]{1,0:T(8,128)(2,1)S(1)}, u32[]{:S(2)}, u32[]{:S(2)}) collective-permute-start(bf16[512,512]{1,0:T(8,128)(2,1)S(1)} %collective-permute-done.151.refs_18_), channel_id=1, source_target_pairs={{0,1},{1,0},{2,3},{3,2},{4,5},{5,4},{6,7},{7,6},{8,9},{9,8},{10,11... | collective-permute-start | bytes 1572872 | tf_op jit(solution)/shard_map/ppermute | solution.py:279
  69.4 8.6 %collective-permute-start.155 = (bf16[512,512]{1,0:T(8,128)(2,1)S(1)}, bf16[512,512]{1,0:T(8,128)(2,1)S(1)}, u32[]{:S(2)}, u32[]{:S(2)}) collective-permute-start(bf16[512,512]{1,0:T(8,128)(2,1)S(1)} %collective-permute-done.154.refs_22_), channel_id=1, source_target_pairs={{0,1},{1,0},{2,3},{3,2},{4,5},{5,4},{6,7},{7,6},{8,9},{9,8},{10,11... | collective-permute-start | bytes 1572872 | tf_op jit(solution)/shard_map/ppermute | solution.py:279
  69.7 5.6 %collective-permute-start.148 = (bf16[128,512]{1,0:T(8,128)(2,1)S(1)}, bf16[128,512]{1,0:T(8,128)(2,1)S(1)}, u32[]{:S(2)}, u32[]{:S(2)}) collective-permute-start(bf16[128,512]{1,0:T(8,128)(2,1)S(1)} %copy-done.6), channel_id=1, source_target_pairs={{0,2},{1,3},{2,0},{3,1},{4,6},{5,7},{6,4},{7,5},{8,10},{9,11},{10,... | collective-permute-start | bytes 393224 | tf_op jit(solution)/shard_map/ppermute | solution.py:279
  75.3 1.3 %collective-permute-start.146 = (bf16[128,512]{1,0:T(8,128)(2,1)S(1)}, bf16[128,512]{1,0:T(8,128)(2,1)S(1)}, u32[]{:S(2)}, u32[]{:S(2)}) collective-permute-start(bf16[128,512]{1,0:T(8,128)(2,1)S(1)} %collective-permute-done.145.refs_10_), channel_id=1, source_target_pairs={{0,1},{1,0},{2,3},{3,2},{4,5},{5,4},{6,7},{7,6},{8,9},{9,8},{10,11... | collective-permute-start | bytes 393224 | tf_op jit(solution)/shard_map/ppermute | solution.py:279
  76.7 1.3 %collective-permute-start.149 = (bf16[128,512]{1,0:T(8,128)(2,1)S(1)}, bf16[128,512]{1,0:T(8,128)(2,1)S(1)}, u32[]{:S(2)}, u32[]{:S(2)}) collective-permute-start(bf16[128,512]{1,0:T(8,128)(2,1)S(1)} %collective-permute-done.148.refs_14_), channel_id=1, source_target_pairs={{0,1},{1,0},{2,3},{3,2},{4,5},{5,4},{6,7},{7,6},{8,9},{9,8},{10,11... | collective-permute-start | bytes 393224 | tf_op jit(solution)/shard_map/ppermute | solution.py:279
  (12 other events, 8.7 us)

commit v2 on v1

v2 whole, which is shorter than its diff:
```python
import functools
import math

import jax
import jax.numpy as jnp
from jax import lax
from jax.experimental import pallas as pl
from jax.experimental.pallas import tpu as pltpu
from jax.sharding import PartitionSpec as P


HEAD_SIZE = 64
EPSILON = 1e-05
FLAG_ROWS = 8
EDGE_STEP = 1024

f32 = jnp.float32
bf16 = jnp.bfloat16
f8 = jnp.float8_e4m3fn

VMEM = pl.BlockSpec(memory_space=pltpu.VMEM)
SMEM = pl.BlockSpec(memory_space=pltpu.SMEM)
HBM = pl.BlockSpec(memory_space=pltpu.HBM)

NT = (((1,), (1,)), ((), ()))
NN = (((1,), (0,)), ((), ()))

PARAMS = pltpu.CompilerParams(vmem_limit_bytes=24 << 20)


def dot(a, b, dims=NN):
    return lax.dot_general(a, b, dims, preferred_element_type=f32)


def norm_rows(rows, gain):
    mean = jnp.mean(rows, -1, keepdims=True)
    centred = rows - mean
    variance = jnp.mean(centred * centred, -1, keepdims=True)
    return (centred * lax.rsqrt(variance + EPSILON) * gain).astype(bf16)


def one_hot_columns(index_row, count, live=None):
    hit = lax.broadcasted_iota(jnp.int32, (count, index_row.shape[1]), 0) == index_row
    if live is not None:
        hit = jnp.logical_and(hit, live)
    return jnp.where(hit, 1.0, 0.0).astype(bf16)


def narrow_one_hot(index_row, count):
    numbers = lax.broadcasted_iota(jnp.int16, (count, index_row.shape[1]), 0)
    hit = numbers == index_row.astype(jnp.int16)
    return jnp.where(hit, jnp.ones((), bf16), jnp.zeros((), bf16)).astype(f8)


def in_hbm(*arrays):
    return [pltpu.with_memory_space_constraint(array, pltpu.HBM) for array in arrays]


def xor_route(count, mask):
    return [(i, i ^ mask) for i in range(count)]


def prologue_kernel(
    x_hbm, gain_hbm, w_hbm, sender_hbm, wo_hbm, wn_hbm, late_gain_hbm, landing_hbm,
    tally_hbm, companion_hbm, scale_hbm,
    low_ref, high_ref, pair_ref, q_ref, kv_ref, k_ref, v_ref, mix_ref, scales_ref, quarter_ref,
    share_ref, late_gain_ref, landing_ref, *rest,
):
    out_refs = rest[:-8]
    x_ref, gain_ref, w_ref, sender_ref, tally_ref, companion_ref, scale_ref, sems = rest[-8:]
    nodes, _ = x_ref.shape
    cols = q_ref.shape[1]
    sources = (
        (x_hbm, x_ref),
        (gain_hbm, gain_ref),
        (w_hbm, w_ref),
        (sender_hbm, sender_ref),
        (wo_hbm, mix_ref.at[pl.ds(0, cols)]),
        (wn_hbm, mix_ref.at[pl.ds(cols, cols)]),
        (late_gain_hbm, late_gain_ref),
        (landing_hbm, landing_ref),
        (tally_hbm, tally_ref),
        (companion_hbm, companion_ref),
        (scale_hbm, scale_ref),
    )
    copies = [
        pltpu.make_async_copy(source, target, sems.at[i])
        for i, (source, target) in enumerate(sources)
    ]
    for copy in copies:
        copy.start()

    copies[0].wait()
    copies[1].wait()
    normed = norm_rows(x_ref[...].astype(f32), gain_ref[...])
    copies[2].wait()
    weights = jnp.concatenate([w_ref[0], w_ref[1], w_ref[2]], axis=1)
    projected = dot(normed, weights).astype(bf16)
    q_ref[...] = projected[:, :cols]
    kv_ref[...] = projected[:, cols:]
    k_ref[...] = projected[:, cols : 2 * cols]
    v_ref[...] = projected[:, 2 * cols :]

    for copy in copies[3:]:
        copy.wait()
    one, two = companion_ref[0, 0], companion_ref[1, 0]
    low, high = jnp.minimum(one, two), jnp.maximum(one, two)
    low_ref[0] = low - 1
    high_ref[0] = high - 1
    pair_ref[0] = lax.shift_right_logical((high - 1) * (high - 2), 1) + low - 1
    for h in range(scales_ref.shape[0]):
        scales_ref[h] = jnp.full(scales_ref.shape[1:], scale_ref[h], f32)

    me, part = lax.axis_index("dom"), lax.axis_index("mp")
    rows = share_ref.shape[0]
    share_ref[...] = x_ref[pl.ds(pl.multiple_of(part * rows, rows), rows), :]
    quarter = x_ref[:, pl.ds(pl.multiple_of(part * cols, 128), cols)]
    quarter_ref[...] = quarter
    quarter_t = quarter.astype(f32).T.astype(bf16)
    cap = sender_ref.shape[1]
    slot = lax.broadcasted_iota(jnp.int32, (1, cap), 1)
    near = len(out_refs)
    for a, out_ref in enumerate(out_refs):
        for h in range(out_ref.shape[0]):
            dest = jnp.bitwise_xor(me, h * near + a)
            live = slot < tally_ref[0, dest]
            pick = one_hot_columns(sender_ref[pl.ds(dest, 1), :], nodes, live)
            out_ref[h, :cols, :] = dot(quarter_t, pick).astype(bf16)
            out_ref[h, cols:, :] = jnp.broadcast_to(
                jnp.where(live, 1.0, 0.0), (FLAG_ROWS, cap)
            ).astype(bf16)


def prologue(
    tally, companion, scale, x, gain, w, sender, wo, wn, late_gain, landing, near, shares
):
    nodes, width = x.shape
    cols = w.shape[2]
    peers, cap = sender.shape
    return pl.pallas_call(
        prologue_kernel,
        out_shape=[jax.ShapeDtypeStruct((1,), jnp.int32)] * 3
        + [jax.ShapeDtypeStruct((nodes, n * cols), bf16) for n in (1, 2, 1, 1)]
        + [
            jax.ShapeDtypeStruct((2 * cols, width), bf16),
            jax.ShapeDtypeStruct((scale.shape[0], 8, 128), f32),
            jax.ShapeDtypeStruct((nodes, cols), bf16),
            jax.ShapeDtypeStruct((nodes // shares, width), bf16),
            jax.ShapeDtypeStruct(late_gain.shape, f32),
            jax.ShapeDtypeStruct(landing.shape, jnp.int32),
        ]
        + [jax.ShapeDtypeStruct((peers // near, cols + FLAG_ROWS, cap), bf16)] * near,
        in_specs=[HBM] * 11,
        out_specs=[SMEM] * 3 + [VMEM] * (10 + near),
        scratch_shapes=[
            pltpu.VMEM(x.shape, bf16),
            pltpu.VMEM(gain.shape, f32),
            pltpu.VMEM(w.shape, bf16),
            pltpu.VMEM(sender.shape, jnp.int32),
            pltpu.SMEM(tally.shape, jnp.int32),
            pltpu.SMEM(companion.shape, jnp.int32),
            pltpu.SMEM(scale.shape, f32),
            pltpu.SemaphoreType.DMA((11,)),
        ],
        name="prologue",
        compiler_params=PARAMS,
        cost_estimate=pl.CostEstimate(
            flops=2 * nodes * width * 3 * cols, bytes_accessed=4 << 20, transcendentals=0
        ),
    )(
        *in_hbm(
            x, gain, w, sender, wo, wn, late_gain, landing, tally, companion, scale
        )
    )


def pack_kernel(*refs):
    near = refs[-1].shape[0]
    for h, out_ref in enumerate(refs[near:], start=1):
        for a in range(near):
            out_ref[a] = refs[a][h]


def pack(held):
    far, *block = held[0].shape
    return pl.pallas_call(
        pack_kernel,
        out_shape=[jax.ShapeDtypeStruct((len(held), *block), bf16)] * (far - 1),
        in_specs=[VMEM] * len(held),
        out_specs=[VMEM] * (far - 1),
        name="pack",
        compiler_params=PARAMS,
        cost_estimate=pl.CostEstimate(flops=0, bytes_accessed=1 << 20, transcendentals=0),
    )(*held)


def edge_kernel(start, tail_hbm, sink_hbm, *refs):
    before, (counts_ref, tail_ref, sink_ref, sems) = refs[:-4], refs[-4:]
    edges = tail_ref.shape[1]
    copies = [
        pltpu.make_async_copy(tail_hbm.at[:, pl.ds(start, edges)], tail_ref, sems.at[0]),
        pltpu.make_async_copy(sink_hbm.at[:, pl.ds(start, edges)], sink_ref, sems.at[1]),
    ]
    for copy in copies:
        copy.start()
    nodes = counts_ref.shape[0]
    step = math.gcd(edges, EDGE_STEP)
    counts_ref[...] = before[0][...] if before else jnp.zeros_like(counts_ref)
    for copy in copies:
        copy.wait()

    def add(turn, unused):
        at = pl.ds(pl.multiple_of(turn * step, step), step)
        sink = narrow_one_hot(sink_ref[:, at], nodes)
        tail = narrow_one_hot(tail_ref[:, at], nodes)
        counts_ref[...] += dot(sink, tail, NT)
        return unused

    lax.fori_loop(0, edges // step, add, 0)


def edge_counts(tail, sink, nodes, start, stop, *before):
    edges = stop - start
    return pl.pallas_call(
        functools.partial(edge_kernel, start),
        out_shape=jax.ShapeDtypeStruct((nodes, nodes), f32),
        in_specs=[HBM, HBM] + [VMEM] * len(before),
        out_specs=VMEM,
        scratch_shapes=[
            pltpu.VMEM((1, edges), jnp.int32),
            pltpu.VMEM((1, edges), jnp.int32),
            pltpu.SemaphoreType.DMA((2,)),
        ],
        name="edge_counts",
        compiler_params=PARAMS,
        cost_estimate=pl.CostEstimate(
            flops=2 * nodes * nodes * edges, bytes_accessed=2 << 20, transcendentals=0
        ),
    )(*in_hbm(tail, sink), *before)


def message_kernel(origins, counts_ref, quarter_ref, landing_ref, *refs):
    count = len(set(i for i, _, _ in origins))
    ins, outs = refs[:count], refs[count:]
    me, part = lax.axis_index("dom"), lax.axis_index("mp")
    nodes = quarter_ref.shape[0]
    rows, cols = outs[0].shape
    land = jnp.concatenate(
        [
            one_hot_columns(landing_ref[pl.ds(jnp.bitwise_xor(me, k), 1), :], nodes)
            for _, _, k in origins
        ],
        axis=1,
    )
    arrived = jnp.concatenate([ins[i][j] for i, j, _ in origins], axis=1)
    boundary = dot(land, arrived, NT)
    quarter = quarter_ref[...]
    filled = jnp.concatenate([quarter, jnp.ones((nodes, 128), bf16)], axis=1)
    counts = counts_ref[...]
    high = jnp.floor(counts * (1.0 / 256.0))
    low = counts - 256.0 * high
    total = 256.0 * dot(high.astype(bf16), filled) + dot(low.astype(bf16), filled)
    quarter = quarter.astype(f32)
    degree = total[:, cols : cols + 1] + boundary[:, cols : cols + 1]
    message = (quarter + total[:, :cols] + boundary[:, :cols]) / (1.0 + degree)
    whole_ref = outs[-1]
    whole_ref[...] = message.astype(bf16)
    for k, out_ref in enumerate(outs[:-1]):
        at = jnp.bitwise_xor(part, k) * rows
        out_ref[...] = whole_ref[pl.ds(pl.multiple_of(at, rows), rows), :]


def messages(counts, quarter, landing, arrived, origins, shares):
    nodes, cols = quarter.shape
    rows = nodes // shares
    return pl.pallas_call(
        functools.partial(message_kernel, origins),
        out_shape=[jax.ShapeDtypeStruct((rows, cols), bf16)] * shares,
        in_specs=[VMEM] * (3 + len(arrived)),
        out_specs=[VMEM] * shares,
        scratch_shapes=[pltpu.VMEM((nodes, cols), bf16)],
        name="messages",
        compiler_params=PARAMS,
        cost_estimate=pl.CostEstimate(
            flops=2 * nodes * 1024 * 256, bytes_accessed=2 << 20, transcendentals=0
        ),
    )(counts, quarter, landing, *arrived)


def attention_kernel(
    offsets, scales_ref, q_ref, own_ref, one_any, two_any, *refs
):
    outs, (one_ref, two_ref, block_ref, sems) = refs[:-4], refs[-4:]
    copies = [
        pltpu.make_async_copy(one_any, one_ref, sems.at[0]),
        pltpu.make_async_copy(two_any, two_ref, sems.at[1]),
    ]
    for copy in copies:
        copy.start()
    part = lax.axis_index("mp")
    rows, cols = outs[0].shape
    heads = cols // HEAD_SIZE
    count = len(offsets)
    base = jnp.bitwise_xor(part, offsets[0]) // count * count
    at = pl.multiple_of(base * rows, count * rows)
    sources = (own_ref, one_ref, two_ref)
    for h in range(heads):
        band = slice(h * HEAD_SIZE, (h + 1) * HEAD_SIZE)
        q = q_ref[pl.ds(at, count * rows), band]
        factor = scales_ref[h, :1, :1] * math.log2(math.e)
        parts = []
        for i, r in enumerate(sources):
            if h == 0 and i > 0:
                copies[i - 1].wait()
            parts.append(dot(q, r[:, band], NT) * factor)
        top = functools.reduce(jnp.maximum, [jnp.max(s, -1, keepdims=True) for s in parts])
        powers = [jnp.exp2(s - top) for s in parts]
        inverse = 1.0 / sum(jnp.sum(p, -1, keepdims=True) for p in powers)
        value_band = slice(cols + h * HEAD_SIZE, cols + (h + 1) * HEAD_SIZE)
        attended = sum(
            dot((p * inverse).astype(bf16), r[:, value_band]) for p, r in zip(powers, sources)
        )
        block_ref[:, band] = attended.astype(bf16)
    for k, out_ref in zip(offsets, outs):
        place = (jnp.bitwise_xor(part, k) - base) * rows
        out_ref[...] = block_ref[pl.ds(pl.multiple_of(place, rows), rows), :]


def attention(scales, q, own, one, two, shares, offsets):
    nodes, cols = q.shape
    rows = nodes // shares
    any_space = pl.BlockSpec(memory_space=pl.ANY)
    return pl.pallas_call(
        functools.partial(attention_kernel, offsets),
        out_shape=[jax.ShapeDtypeStruct((rows, cols), bf16)] * len(offsets),
        in_specs=[VMEM] * 3 + [any_space] * 2,
        out_specs=[VMEM] * len(offsets),
        scratch_shapes=[
            pltpu.VMEM(one.shape, bf16),
            pltpu.VMEM(two.shape, bf16),
            pltpu.VMEM((len(offsets) * rows, cols), bf16),
            pltpu.SemaphoreType.DMA((2,)),
        ],
        name="attention",
        compiler_params=PARAMS,
        cost_estimate=pl.CostEstimate(
            flops=4 * rows * len(offsets) * 3 * nodes * 256,
            bytes_accessed=2 << 20,
            transcendentals=1 << 20,
        ),
    )(scales, q, own, one, two)


def final_kernel(shares, share_ref, gain_ref, *refs):
    att, msg, mixes, ups, downs = (refs[i * shares : (i + 1) * shares] for i in range(5))
    out_ref, mix_buf, up_buf, down_buf, sems = refs[5 * shares :]
    _, width = out_ref.shape
    copies = []
    for i, (sources, buf) in enumerate(((mixes, mix_buf), (ups, up_buf), (downs, down_buf))):
        copies.append(
            [
                pltpu.make_async_copy(source, buf.at[k], sems.at[i, k])
                for k, source in enumerate(sources)
            ]
        )
    for copy in copies[0]:
        copy.start()
    for k in range(shares):
        copies[1][k].start()
        copies[2][k].start()
    mixed = share_ref[...].astype(f32)
    terms = jnp.concatenate([r[...] for pair in zip(att, msg) for r in pair], axis=1)
    for copy in copies[0]:
        copy.wait()
    mixed = mixed + dot(terms, mix_buf[...].reshape(-1, width))
    normed = norm_rows(mixed, gain_ref[...])
    total = mixed
    for k in range(shares):
        copies[1][k].wait()
        wide = dot(normed, up_buf[k])
        hidden = (0.5 * wide * (1.0 + lax.erf(wide * (0.5**0.5)))).astype(bf16)
        copies[2][k].wait()
        total = total + dot(hidden, down_buf[k])
    out_ref[...] = total.astype(bf16)


def final(share, gain, att, msg, mixes, ups, downs):
    shares = len(att)
    rows, width = share.shape
    any_space = pl.BlockSpec(memory_space=pl.ANY)
    return pl.pallas_call(
        functools.partial(final_kernel, shares),
        out_shape=jax.ShapeDtypeStruct((rows, width), bf16),
        in_specs=[VMEM] * (2 + 2 * shares) + [any_space] * (3 * shares),
        out_specs=VMEM,
        scratch_shapes=[
            pltpu.VMEM((shares, *group[0].shape), bf16) for group in (mixes, ups, downs)
        ]
        + [pltpu.SemaphoreType.DMA((3, shares))],
        name="final",
        compiler_params=PARAMS,
        cost_estimate=pl.CostEstimate(
            flops=2 * rows * width * 4096, bytes_accessed=6 << 20, transcendentals=1 << 18
        ),
    )(share, gain, *att, *msg, *mixes, *ups, *downs)


def gather_pieces(piece, axis):
    count = lax.axis_size(axis)
    pieces = {0: piece}
    bit = count // 2
    while bit:
        for k in list(pieces):
            pieces[k | bit] = lax.ppermute(pieces[k], axis, xor_route(count, bit))
        bit //= 2
    return [pieces[k] for k in range(count)]


def layer(
    x,
    mixer_gain,
    perceptron_gain,
    projectors,
    scale,
    out_projector,
    neighbour_projector,
    expand,
    contract,
    companion,
    sender,
    tally,
    landing,
    tail,
    sink,
):
    peers = lax.axis_size("dom")
    shares = lax.axis_size("mp")

    def send(block, mask):
        return lax.ppermute(block, "dom", xor_route(peers, mask))

    near = 1 << ((peers.bit_length() - 1) // 2)
    far = peers // near
    (
        low_mask, high_mask, pair, q, kv, k, v, mix, scales, quarter, share, late_gain, landing,
        *outgoing,
    ) = prologue(
        tally, companion, scale, x, mixer_gain[None, :], projectors, sender[0],
        out_projector, neighbour_projector, perceptron_gain[None, :], landing[0], near, shares,
    )
    ups = gather_pieces(expand, "mp")
    downs = gather_pieces(contract, "mp")
    mixes = gather_pieces(mix, "mp")
    nodes, edges = x.shape[0], tail.shape[1]

    def shared(outgoing, tail, sink):
        held = [outgoing[0]] + [send(outgoing[a], a) for a in range(1, near)]
        arrived = [send(block, h * near) for h, block in enumerate(pack(held), start=1)]
        counts = edge_counts(tail, sink, nodes, 0, edges)
        return counts, held[1:] + arrived

    origins = tuple((a - 1, 0, a) for a in range(1, near)) + tuple(
        (near - 2 + h, a, h * near + a) for h in range(1, far) for a in range(near)
    )
    operands = (kv, k, v, outgoing, tail, sink)
    if peers * (peers - 1) // 2 <= 32:
        branches = []
        for high in range(1, peers):
            for low in range(1, high):

                def branch(kv, k, v, *rest, low=low, high=high):
                    landed = shared(*rest)
                    if low & high & (peers // 2):
                        one_k, one_v = send(k, low), send(v, low)
                        two_k, two_v = send(one_k, low ^ high), send(one_v, low ^ high)
                        one = jnp.concatenate([one_k, one_v], axis=1)
                        two = jnp.concatenate([two_k, two_v], axis=1)
                    else:
                        one, two = send(kv, low), send(kv, high)
                    return (one, two) + landed

                branches.append(branch)
        one, two, counts, arrived = lax.switch(pair[0], branches, *operands)
    else:
        hops = [lambda kv, mask=mask: send(kv, mask) for mask in range(1, peers)]
        one = lax.switch(low_mask[0], hops, kv)
        two = lax.switch(high_mask[0], hops, kv)
        counts, arrived = shared(outgoing, tail, sink)

    msg = messages(counts, quarter, landing, arrived, origins, shares)

    def swap(chunk, k):
        return lax.ppermute(chunk, "mp", xor_route(shares, k)) if k else chunk

    msg = [swap(chunk, k) for k, chunk in enumerate(msg)]
    groups = [tuple(range(shares // 2, shares)), tuple(range(shares // 2))]
    att = [None] * shares
    for group in groups:
        chunks = attention(scales, q, kv, one, two, shares, group)
        for k, chunk in zip(group, chunks):
            att[k] = swap(chunk, k)
    return final(share, late_gain, att, msg, mixes, ups, downs)


def solution(mesh):
    return jax.shard_map(
        layer,
        mesh=mesh,
        in_specs=(
            P("dom", None),
            P(),
            P(),
            P(None, None, "mp"),
            P("mp"),
            P("mp", None),
            P("mp", None),
            P(None, "mp"),
            P("mp", None),
            P(),
            P("dom", None, None),
            P("dom", None),
            P("dom", None, None),
            P("dom", None),
            P("dom", None),
        ),
        out_specs=P(("dom", "mp"), None),
        check_vma=False,
    )
```

time: 81.9 us -> 74.2 us (0.906)
  waiting for transfers between devices: 36.1 us -> 30.1 us
  local copies, waits for them, and re-layouts: 6.04 us -> 0.64 us
  Pallas kernels: 19.3 us -> 21.3 us
  starting transfers between devices: 18.8 us -> 19.9 us
    ppermute x10 -> x6, waiting for transfers between devices: 28.2 us -> 22.7 us  [swap(): return lax.ppermute(chunk, 'mp', xor_route(shares, k)) if k else chunk]
    ppermute x2 -> x6, starting transfers between devices: 5.65 us -> 10.8 us  [send(): return lax.ppermute(block, 'dom', xor_route(peers, mask))]
    unnamed x38 -> x4, local copies, waits for them, and re-layouts: 4.8 us -> 0.01 us
    ppermute x12 -> x9, waiting for transfers between devices: 7.97 us -> 3.68 us  [gather_pieces(): pieces[k | bit] = lax.ppermute(pieces[k], axis, xor_route(count, bit))]
    ppermute x2 -> x6, waiting for transfers between devices: 0.01 us -> 3.72 us  [send(): return lax.ppermute(block, 'dom', xor_route(peers, mask))]
    ppermute x10 -> x6, starting transfers between devices: 7.35 us -> 4.18 us  [swap(): return lax.ppermute(chunk, 'mp', xor_route(shares, k)) if k else chunk]
    pallas_call x3 -> x5, Pallas kernels: 14.6 us -> 16.2 us  [the longest x1 7.63 us: edge_counts(): pl.pallas_call(functools.partial(edge_kernel, start), out_shape=jax.Shape...]
    ppermute x12 -> x9, starting transfers between devices: 5.83 us -> 4.86 us  [gather_pieces(): pieces[k | bit] = lax.ppermute(pieces[k], axis, xor_route(count, bit))]
  transfers between devices with their start and end apart: 24 -> 21, of which waited for: 9 -> 6; matrix products, arithmetic and copies ran while one was open for 0% -> 0% of each run, Pallas kernels for 18% -> 21%
where the time goes in v2:
time: 74.2 us; the launch traced here: 73.3 us
  waiting for transfers between devices  30.1 us (41%)
  Pallas kernels  21.3 us (29%)
  starting transfers between devices  19.9 us (27%)
  between operations  0.96 us (1%)
    ppermute x6, waiting for transfers between devices, swap(): return lax.ppermute(chunk, 'mp', xor_route(shares, k)) if k else chunk  22.7 us
    ppermute x6, starting transfers between devices, send(): return lax.ppermute(block, 'dom', xor_route(peers, mask))  10.8 us
    pallas_call x1, Pallas kernels, edge_counts(): pl.pallas_call(functools.partial(edge_kernel, start), out_shape=jax.Shape...  7.63 us
    pallas_call x2, Pallas kernels, attention(): pl.pallas_call(functools.partial(attention_kernel, offsets), out_shape=[j...  5.88 us
    ppermute x9, starting transfers between devices, gather_pieces(): pieces[k | bit] = lax.ppermute(pieces[k], axis, xor_route(count, bit))  4.86 us
    ppermute x6, starting transfers between devices, swap(): return lax.ppermute(chunk, 'mp', xor_route(shares, k)) if k else chunk  4.18 us
    ppermute x6, waiting for transfers between devices, send(): return lax.ppermute(block, 'dom', xor_route(peers, mask))  3.72 us
    ppermute x9, waiting for transfers between devices, gather_pieces(): pieces[k | bit] = lax.ppermute(pieces[k], axis, xor_route(count, bit))  3.68 us
  transfers between devices with their start and end apart: 21, of which 6 were waited for; matrix products, arithmetic and copies ran while one was open for 0% of the time, Pallas kernels for 21%

profile of v2, /device:TPU:0, one launch (start us, length us, event | category | flops | bytes accessed | tf_op | source)
XLA Modules:
  0.0 73.3 jit_solution(5699839588574261948)
XLA Ops:
  0.0 2.7 %prologue.1 = (s32[1]{0:T(128)}, s32[1]{0:T(128)}, s32[1]{0:T(128)}, bf16[512,128]{1,0:T(8,128)(2,1)S(1)}, bf16[512,256]{1,0:T(8,128)(2,1)S(1)}, /*index=5*/bf16...) custom-call(bf16[512,512]{1,0:T(8,128)(2,1)} %x_hbm.1, ...), custom_call_target="tpu_custom_call" | custom-call | flops 201326592 | bytes 4194304 | tf_op jit(solution)/shard_map/prologue/pallas_call | solution.py:140
  3.4 23.2 %conditional.1 = (bf16[512,256]{1,0:T(8,128)(2,1)}, bf16[512,256]{1,0:T(8,128)(2,1)}, f32[512,512]{1,0:T(8,128)S(1)}, bf16[4,136,128]{2,1,0:T(8,128)(2,1)}, bf16...) conditional(s32[]{:T(128)} %bitcast.4, ...), branch_computations={%region_0.0_spmd, %region_1.0_spmd, %region_2.0_spmd, %region_3.0_... | conditional | flops 8590983168 | bytes 8241556 | solution.py:483
  3.4 3.1 %collective-permute-start.20 = (bf16[4,136,128]{2,1,0:T(8,128)(2,1)S(1)}, bf16[4,136,128]{2,1,0:T(8,128)(2,1)S(1)}, u32[]{:S(2)}, u32[]{:S(2)}) collective-permute-start(bf16[4,136,128]{2,1,0:T(8,128)(2,1)S(1)} %get-tuple-element.254), channel_id=1, source_target_pairs={{0,4},{4,0},{8,12},{12,8},{16,20},{20,16},{24,28},{28,24},{1,5},{5... | collective-permute-start | bytes 417800 | tf_op jit(solution)/shard_map/cond/branch_3_fun/ppermute | solution.py:440
  6.5 0.1 collective-permute-start.18
  6.6 3.0 %collective-permute-start.19 = (bf16[512,256]{1,0:T(8,128)(2,1)S(1)}, bf16[512,256]{1,0:T(8,128)(2,1)}, u32[]{:S(2)}, u32[]{:S(2)}) collective-permute-start(bf16[512,256]{1,0:T(8,128)(2,1)S(1)} %get-tuple-element.251), channel_id=1, source_target_pairs={{0,16},{4,20},{8,24},{12,28},{16,0},{20,4},{24,8},{28,12},{1,17},{... | collective-permute-start | bytes 786440 | tf_op jit(solution)/shard_map/cond/branch_3_fun/ppermute | solution.py:440
  9.6 1.4 %collective-permute-done.20.refs_1_ = bf16[4,136,128]{2,1,0:T(8,128)(2,1)S(1)} collective-permute-done((bf16[4,136,128]{2,1,0:T(8,128)(2,1)S(1)}, bf16[4,136,128]{2,1,0:T(8,128)(2,1)S(1)}, u32[]{:S(2)}, u32[]{:S(2)}) %collective-permute-start.20) | collective-permute-done | bytes 139296 | tf_op jit(solution)/shard_map/cond/branch_3_fun/ppermute | solution.py:440
  11.0 0.6 copy-done.5
  11.7 2.1 %collective-permute-start.21 = (bf16[2,136,128]{2,1,0:T(8,128)(2,1)S(1)}, bf16[2,136,128]{2,1,0:T(8,128)(2,1)}, u32[]{:S(2)}, u32[]{:S(2)}) collective-permute-start(bf16[2,136,128]{2,1,0:T(8,128)(2,1)S(1)} %get-tuple-element.256), channel_id=1, source_target_pairs={{0,8},{4,12},{8,0},{12,4},{16,24},{20,28},{24,16},{28,20},{1,9},{5... | collective-permute-start | bytes 208904 | tf_op jit(solution)/shard_map/cond/branch_3_fun/ppermute | solution.py:440
  13.7 2.6 %collective-permute-start.22 = (bf16[2,136,128]{2,1,0:T(8,128)(2,1)S(1)}, bf16[2,136,128]{2,1,0:T(8,128)(2,1)}, u32[]{:S(2)}, u32[]{:S(2)}) collective-permute-start(bf16[2,136,128]{2,1,0:T(8,128)(2,1)S(1)} %get-tuple-element.257), channel_id=1, source_target_pairs={{0,16},{4,20},{8,24},{12,28},{16,0},{20,4},{24,8},{28,12},{1,17},{... | collective-permute-start | bytes 208904 | tf_op jit(solution)/shard_map/cond/branch_3_fun/ppermute | solution.py:440
  16.3 7.6 %edge_counts.24 = f32[512,512]{1,0:T(8,128)S(1)} custom-call(s32[1,16384]{1,0:T(1,128)} %get-tuple-element.252.tail_hbm, s32[1,16384]{1,0:T(1,128)} %get-tuple-element.253.sink_hbm), custom_call_target="tpu_custom_call" | custom-call | flops 8589934592 | bytes 2097152 | tf_op jit(solution)/shard_map/cond/branch_3_fun/edge_counts/pallas_call | solution.py:224
  24.0 2.3 %collective-permute-done.22 = bf16[2,136,128]{2,1,0:T(8,128)(2,1)} collective-permute-done((bf16[2,136,128]{2,1,0:T(8,128)(2,1)S(1)}, bf16[2,136,128]{2,1,0:T(8,128)(2,1)}, u32[]{:S(2)}, u32[]{:S(2)}) %collective-permute-start.22) | collective-permute-done | bytes 69664 | tf_op jit(solution)/shard_map/cond/branch_3_fun/ppermute | solution.py:440
  26.6 1.6 %collective-permute-start.148 = (bf16[512,512]{1,0:T(8,128)(2,1)S(1)}, bf16[512,512]{1,0:T(8,128)(2,1)S(1)}, u32[]{:S(2)}, u32[]{:S(2)}) collective-permute-start(bf16[512,512]{1,0:T(8,128)(2,1)S(1)} %copy-done), channel_id=1, source_target_pairs={{0,2},{1,3},{2,0},{3,1},{4,6},{5,7},{6,4},{7,5},{8,10},{9,11},{10,... | collective-permute-start | bytes 1572872 | tf_op jit(solution)/shard_map/ppermute | solution.py:414
  28.2 0.5 collective-permute-start.151
  28.7 1.5 %collective-permute-start.145 = (bf16[256,512]{1,0:T(8,128)(2,1)S(1)}, bf16[256,512]{1,0:T(8,128)(2,1)S(1)}, u32[]{:S(2)}, u32[]{:S(2)}) collective-permute-start(bf16[256,512]{1,0:T(8,128)(2,1)S(1)} %get-tuple-element.456.refs_8_), channel_id=1, source_target_pairs={{0,2},{1,3},{2,0},{3,1},{4,6},{5,7},{6,4},{7,5},{8,10},{9,11},{10,... | collective-permute-start | bytes 786440 | tf_op jit(solution)/shard_map/ppermute | solution.py:414
  30.2 1.8 %messages.1 = (bf16[128,128]{1,0:T(8,128)(2,1)S(1)}, bf16[128,128]{1,0:T(8,128)(2,1)S(1)}, bf16[128,128]{1,0:T(8,128)(2,1)S(1)}, bf16[128,128]{1,0:T(8,128)(2,1)S(1)}) custom-call(f32[512,512]{1,0:T(8,128)S(1)} %get-tuple-element.445.counts_ref, bf16[512,128]{1,0:T(8,128)(2,1)S(1)} %get-tuple-element.446.quarter_ref, ...), custom_call_target="tpu_custom_call" | custom-call | flops 268435456 | bytes 2097152 | tf_op jit(solution)/shard_map/messages/pallas_call | solution.py:276
  32.0 0.1 collective-permute-start.141
  32.1 0.5 collective-permute-start.142
  32.7 2.9 %attention.3 = (bf16[128,128]{1,0:T(8,128)(2,1)S(1)}, bf16[128,128]{1,0:T(8,128)(2,1)S(1)}) custom-call(f32[2,8,128]{2,1,0:T(8,128)S(1)} %get-tuple-element.431.scales_ref, bf16[512,128]{1,0:T(8,128)(2,1)S(1)} %get-tuple-element.432.q_ref, bf16[512,256]{1,0:T(8,128)(2,1)S(1)} %get-tuple-element.433.own_ref, bf16[512,256]{1,0:T(8,128)(2,1)} %get-tuple-element.439.one_any, ...), custom_call_target="tpu_custom_call" | custom-call | flops 402653184 | bytes 2097152 | tf_op jit(solution)/shard_map/attention/pallas_call | solution.py:333
  35.6 1.4 %collective-permute-start.143 = (bf16[128,128]{1,0:T(8,128)(2,1)S(1)}, bf16[128,128]{1,0:T(8,128)(2,1)S(1)}, u32[]{:S(2)}, u32[]{:S(2)}) collective-permute-start(bf16[128,128]{1,0:T(8,128)(2,1)S(1)} %get-tuple-element.455), channel_id=1, source_target_pairs={{0,3},{1,2},{2,1},{3,0},{4,7},{5,6},{6,5},{7,4},{8,11},{9,10},{10,... | collective-permute-start | bytes 98312 | tf_op jit(solution)/shard_map/ppermute | solution.py:493
  37.0 19.9 %collective-permute-done.142.refs_6_ = bf16[128,128]{1,0:T(8,128)(2,1)S(1)} collective-permute-done((bf16[128,128]{1,0:T(8,128)(2,1)S(1)}, bf16[128,128]{1,0:T(8,128)(2,1)S(1)}, u32[]{:S(2)}, u32[]{:S(2)}) %collective-permute-start.142) | collective-permute-done | bytes 32800 | tf_op jit(solution)/shard_map/ppermute | solution.py:493
  56.9 1.6 %collective-permute-start.139 = (bf16[128,128]{1,0:T(8,128)(2,1)S(1)}, bf16[128,128]{1,0:T(8,128)(2,1)S(1)}, u32[]{:S(2)}, u32[]{:S(2)}) collective-permute-start(bf16[128,128]{1,0:T(8,128)(2,1)S(1)} %get-tuple-element.443), channel_id=1, source_target_pairs={{0,2},{1,3},{2,0},{3,1},{4,6},{5,7},{6,4},{7,5},{8,10},{9,11},{10,... | collective-permute-start | bytes 98312 | tf_op jit(solution)/shard_map/ppermute | solution.py:493
  58.5 3.0 %attention.2 = (bf16[128,128]{1,0:T(8,128)(2,1)S(1)}, bf16[128,128]{1,0:T(8,128)(2,1)S(1)}) custom-call(f32[2,8,128]{2,1,0:T(8,128)S(1)} %get-tuple-element.431.scales_ref, bf16[512,128]{1,0:T(8,128)(2,1)S(1)} %get-tuple-element.432.q_ref, bf16[512,256]{1,0:T(8,128)(2,1)S(1)} %get-tuple-element.433.own_ref, bf16[512,256]{1,0:T(8,128)(2,1)} %get-tuple-element.439.one_any, ...), custom_call_target="tpu_custom_call" | custom-call | flops 402653184 | bytes 2097152 | tf_op jit(solution)/shard_map/attention/pallas_call | solution.py:333
  61.5 0.1 collective-permute-start.140
  61.6 0.5 collective-permute-start.138
  62.1 2.8 %collective-permute-done.140.refs_3_ = bf16[128,128]{1,0:T(8,128)(2,1)S(1)} collective-permute-done((bf16[128,128]{1,0:T(8,128)(2,1)S(1)}, bf16[128,128]{1,0:T(8,128)(2,1)S(1)}, u32[]{:S(2)}, u32[]{:S(2)}) %collective-permute-start.140) | collective-permute-done | bytes 32800 | tf_op jit(solution)/shard_map/ppermute | solution.py:493
  64.9 0.5 collective-permute-start.147
  65.4 0.1 collective-permute-start.150
  65.5 0.4 collective-permute-start.149
  66.0 0.4 collective-permute-done.144.refs_9_
  66.4 0.1 collective-permute-start.146
  66.6 3.2 %collective-permute-done.146.refs_11_ = bf16[256,512]{1,0:T(8,128)(2,1)S(1)} collective-permute-done((bf16[256,512]{1,0:T(8,128)(2,1)S(1)}, bf16[256,512]{1,0:T(8,128)(2,1)S(1)}, u32[]{:S(2)}, u32[]{:S(2)}) %collective-permute-start.146) | collective-permute-done | bytes 262176 | tf_op jit(solution)/shard_map/ppermute | solution.py:414
  69.8 3.3 %final.1 = bf16[128,512]{1,0:T(8,128)(2,1)} custom-call(bf16[128,512]{1,0:T(8,128)(2,1)S(1)} %get-tuple-element.429.share_ref, f32[1,512]{1,0:T(1,128)S(1)} %get-tuple-element.430.gain_ref, bf16[128,128]{1,0:T(8,128)(2,1)S(1)} %get-tuple-element.441.refs_0_, bf16[128,128]{1,0:T(8,128)(2,1)S(1)} %collective-permute-done.138.refs_1_, ...), custom_call_target="tpu_custom_call" | custom-call | flops 536870912 | bytes 6291456 | tf_op jit(solution)/shard_map/final/pallas_call | solution.py:391
  (24 shorter events, 0.1 us)
Async XLA Ops:
  3.4 23.2 %copy-start = (bf16[512,512]{1,0:T(8,128)(2,1)S(1)}, bf16[512,512]{1,0:T(8,128)(2,1)}, u32[]{:S(2)}) copy-start(bf16[512,512]{1,0:T(8,128)(2,1)} %refs_12_.1) | copy-start | bytes 1572868
  3.4 24.8 %copy-start.1 = (bf16[512,512]{1,0:T(8,128)(2,1)S(1)}, bf16[512,512]{1,0:T(8,128)(2,1)}, u32[]{:S(2)}) copy-start(bf16[512,512]{1,0:T(8,128)(2,1)} %refs_16_.1) | copy-start | bytes 1572868
  3.4 7.6 %collective-permute-start.20 = (bf16[4,136,128]{2,1,0:T(8,128)(2,1)S(1)}, bf16[4,136,128]{2,1,0:T(8,128)(2,1)S(1)}, u32[]{:S(2)}, u32[]{:S(2)}) collective-permute-start(bf16[4,136,128]{2,1,0:T(8,128)(2,1)S(1)} %get-tuple-element.254), channel_id=1, source_target_pairs={{0,4},{4,0},{8,12},{12,8},{16,20},{20,16},{24,28},{28,24},{1,5},{5... | collective-permute-start | bytes 417800 | tf_op jit(solution)/shard_map/cond/branch_3_fun/ppermute | solution.py:440
  6.5 19.8 %collective-permute-start.18 = (bf16[512,256]{1,0:T(8,128)(2,1)S(1)}, bf16[512,256]{1,0:T(8,128)(2,1)}, u32[]{:S(2)}, u32[]{:S(2)}) collective-permute-start(bf16[512,256]{1,0:T(8,128)(2,1)S(1)} %get-tuple-element.251), channel_id=1, source_target_pairs={{0,4},{4,0},{8,12},{12,8},{16,20},{20,16},{24,28},{28,24},{1,5},{5... | collective-permute-start | bytes 786440 | tf_op jit(solution)/shard_map/cond/branch_3_fun/ppermute | solution.py:440
  6.6 19.7 %collective-permute-start.19 = (bf16[512,256]{1,0:T(8,128)(2,1)S(1)}, bf16[512,256]{1,0:T(8,128)(2,1)}, u32[]{:S(2)}, u32[]{:S(2)}) collective-permute-start(bf16[512,256]{1,0:T(8,128)(2,1)S(1)} %get-tuple-element.251), channel_id=1, source_target_pairs={{0,16},{4,20},{8,24},{12,28},{16,0},{20,4},{24,8},{28,12},{1,17},{... | collective-permute-start | bytes 786440 | tf_op jit(solution)/shard_map/cond/branch_3_fun/ppermute | solution.py:440
  11.0 0.7 copy-start.5
  11.7 12.3 %collective-permute-start.21 = (bf16[2,136,128]{2,1,0:T(8,128)(2,1)S(1)}, bf16[2,136,128]{2,1,0:T(8,128)(2,1)}, u32[]{:S(2)}, u32[]{:S(2)}) collective-permute-start(bf16[2,136,128]{2,1,0:T(8,128)(2,1)S(1)} %get-tuple-element.256), channel_id=1, source_target_pairs={{0,8},{4,12},{8,0},{12,4},{16,24},{20,28},{24,16},{28,20},{1,9},{5... | collective-permute-start | bytes 208904 | tf_op jit(solution)/shard_map/cond/branch_3_fun/ppermute | solution.py:440
  13.7 12.5 %collective-permute-start.22 = (bf16[2,136,128]{2,1,0:T(8,128)(2,1)S(1)}, bf16[2,136,128]{2,1,0:T(8,128)(2,1)}, u32[]{:S(2)}, u32[]{:S(2)}) collective-permute-start(bf16[2,136,128]{2,1,0:T(8,128)(2,1)S(1)} %get-tuple-element.257), channel_id=1, source_target_pairs={{0,16},{4,20},{8,24},{12,28},{16,0},{20,4},{24,8},{28,12},{1,17},{... | collective-permute-start | bytes 208904 | tf_op jit(solution)/shard_map/cond/branch_3_fun/ppermute | solution.py:440
  16.3 9.9 %collective-permute-start.23 = (bf16[2,136,128]{2,1,0:T(8,128)(2,1)S(1)}, bf16[2,136,128]{2,1,0:T(8,128)(2,1)}, u32[]{:S(2)}, u32[]{:S(2)}) collective-permute-start(bf16[2,136,128]{2,1,0:T(8,128)(2,1)S(1)} %get-tuple-element.258), channel_id=1, source_target_pairs={{0,24},{4,28},{8,16},{12,20},{16,8},{20,12},{24,0},{28,4},{1,25},{... | collective-permute-start | bytes 208904 | tf_op jit(solution)/shard_map/cond/branch_3_fun/ppermute | solution.py:440
  26.6 38.9 %collective-permute-start.148 = (bf16[512,512]{1,0:T(8,128)(2,1)S(1)}, bf16[512,512]{1,0:T(8,128)(2,1)S(1)}, u32[]{:S(2)}, u32[]{:S(2)}) collective-permute-start(bf16[512,512]{1,0:T(8,128)(2,1)S(1)} %copy-done), channel_id=1, source_target_pairs={{0,2},{1,3},{2,0},{3,1},{4,6},{5,7},{6,4},{7,5},{8,10},{9,11},{10,... | collective-permute-start | bytes 1572872 | tf_op jit(solution)/shard_map/ppermute | solution.py:414
  28.2 37.7 %collective-permute-start.151 = (bf16[512,512]{1,0:T(8,128)(2,1)S(1)}, bf16[512,512]{1,0:T(8,128)(2,1)S(1)}, u32[]{:S(2)}, u32[]{:S(2)}) collective-permute-start(bf16[512,512]{1,0:T(8,128)(2,1)S(1)} %copy-done.1), channel_id=1, source_target_pairs={{0,2},{1,3},{2,0},{3,1},{4,6},{5,7},{6,4},{7,5},{8,10},{9,11},{10,... | collective-permute-start | bytes 1572872 | tf_op jit(solution)/shard_map/ppermute | solution.py:414
  28.7 36.7 %collective-permute-start.145 = (bf16[256,512]{1,0:T(8,128)(2,1)S(1)}, bf16[256,512]{1,0:T(8,128)(2,1)S(1)}, u32[]{:S(2)}, u32[]{:S(2)}) collective-permute-start(bf16[256,512]{1,0:T(8,128)(2,1)S(1)} %get-tuple-element.456.refs_8_), channel_id=1, source_target_pairs={{0,2},{1,3},{2,0},{3,1},{4,6},{5,7},{6,4},{7,5},{8,10},{9,11},{10,... | collective-permute-start | bytes 786440 | tf_op jit(solution)/shard_map/ppermute | solution.py:414
  32.0 3.6 %collective-permute-start.141 = (bf16[128,128]{1,0:T(8,128)(2,1)S(1)}, bf16[128,128]{1,0:T(8,128)(2,1)S(1)}, u32[]{:S(2)}, u32[]{:S(2)}) collective-permute-start(bf16[128,128]{1,0:T(8,128)(2,1)S(1)} %get-tuple-element.453), channel_id=1, source_target_pairs={{0,1},{1,0},{2,3},{3,2},{4,5},{5,4},{6,7},{7,6},{8,9},{9,8},{10,11... | collective-permute-start | bytes 98312 | tf_op jit(solution)/shard_map/ppermute | solution.py:493
  32.1 24.8 %collective-permute-start.142 = (bf16[128,128]{1,0:T(8,128)(2,1)S(1)}, bf16[128,128]{1,0:T(8,128)(2,1)S(1)}, u32[]{:S(2)}, u32[]{:S(2)}) collective-permute-start(bf16[128,128]{1,0:T(8,128)(2,1)S(1)} %get-tuple-element.454), channel_id=1, source_target_pairs={{0,2},{1,3},{2,0},{3,1},{4,6},{5,7},{6,4},{7,5},{8,10},{9,11},{10,... | collective-permute-start | bytes 98312 | tf_op jit(solution)/shard_map/ppermute | solution.py:493
  35.6 25.9 %collective-permute-start.143 = (bf16[128,128]{1,0:T(8,128)(2,1)S(1)}, bf16[128,128]{1,0:T(8,128)(2,1)S(1)}, u32[]{:S(2)}, u32[]{:S(2)}) collective-permute-start(bf16[128,128]{1,0:T(8,128)(2,1)S(1)} %get-tuple-element.455), channel_id=1, source_target_pairs={{0,3},{1,2},{2,1},{3,0},{4,7},{5,6},{6,5},{7,4},{8,11},{9,10},{10,... | collective-permute-start | bytes 98312 | tf_op jit(solution)/shard_map/ppermute | solution.py:493
  56.9 4.6 %collective-permute-start.139 = (bf16[128,128]{1,0:T(8,128)(2,1)S(1)}, bf16[128,128]{1,0:T(8,128)(2,1)S(1)}, u32[]{:S(2)}, u32[]{:S(2)}) collective-permute-start(bf16[128,128]{1,0:T(8,128)(2,1)S(1)} %get-tuple-element.443), channel_id=1, source_target_pairs={{0,2},{1,3},{2,0},{3,1},{4,6},{5,7},{6,4},{7,5},{8,10},{9,11},{10,... | collective-permute-start | bytes 98312 | tf_op jit(solution)/shard_map/ppermute | solution.py:493
  61.5 3.4 %collective-permute-start.140 = (bf16[128,128]{1,0:T(8,128)(2,1)S(1)}, bf16[128,128]{1,0:T(8,128)(2,1)S(1)}, u32[]{:S(2)}, u32[]{:S(2)}) collective-permute-start(bf16[128,128]{1,0:T(8,128)(2,1)S(1)} %get-tuple-element.444), channel_id=1, source_target_pairs={{0,3},{1,2},{2,1},{3,0},{4,7},{5,6},{6,5},{7,4},{8,11},{9,10},{10,... | collective-permute-start | bytes 98312 | tf_op jit(solution)/shard_map/ppermute | solution.py:493
  61.6 3.3 %collective-permute-start.138 = (bf16[128,128]{1,0:T(8,128)(2,1)S(1)}, bf16[128,128]{1,0:T(8,128)(2,1)S(1)}, u32[]{:S(2)}, u32[]{:S(2)}) collective-permute-start(bf16[128,128]{1,0:T(8,128)(2,1)S(1)} %get-tuple-element.442), channel_id=1, source_target_pairs={{0,1},{1,0},{2,3},{3,2},{4,5},{5,4},{6,7},{7,6},{8,9},{9,8},{10,11... | collective-permute-start | bytes 98312 | tf_op jit(solution)/shard_map/ppermute | solution.py:493
  64.9 1.5 %collective-permute-start.144 = (bf16[256,512]{1,0:T(8,128)(2,1)S(1)}, bf16[256,512]{1,0:T(8,128)(2,1)S(1)}, u32[]{:S(2)}, u32[]{:S(2)}) collective-permute-start(bf16[256,512]{1,0:T(8,128)(2,1)S(1)} %get-tuple-element.456.refs_8_), channel_id=1, source_target_pairs={{0,1},{1,0},{2,3},{3,2},{4,5},{5,4},{6,7},{7,6},{8,9},{9,8},{10,11... | collective-permute-start | bytes 786440 | tf_op jit(solution)/shard_map/ppermute | solution.py:414
  64.9 4.9 %collective-permute-start.147 = (bf16[512,512]{1,0:T(8,128)(2,1)S(1)}, bf16[512,512]{1,0:T(8,128)(2,1)S(1)}, u32[]{:S(2)}, u32[]{:S(2)}) collective-permute-start(bf16[512,512]{1,0:T(8,128)(2,1)S(1)} %copy-done), channel_id=1, source_target_pairs={{0,1},{1,0},{2,3},{3,2},{4,5},{5,4},{6,7},{7,6},{8,9},{9,8},{10,11... | collective-permute-start | bytes 1572872 | tf_op jit(solution)/shard_map/ppermute | solution.py:414
  65.4 4.4 %collective-permute-start.150 = (bf16[512,512]{1,0:T(8,128)(2,1)S(1)}, bf16[512,512]{1,0:T(8,128)(2,1)S(1)}, u32[]{:S(2)}, u32[]{:S(2)}) collective-permute-start(bf16[512,512]{1,0:T(8,128)(2,1)S(1)} %copy-done.1), channel_id=1, source_target_pairs={{0,1},{1,0},{2,3},{3,2},{4,5},{5,4},{6,7},{7,6},{8,9},{9,8},{10,11... | collective-permute-start | bytes 1572872 | tf_op jit(solution)/shard_map/ppermute | solution.py:414
  65.5 4.3 %collective-permute-start.149 = (bf16[512,512]{1,0:T(8,128)(2,1)S(1)}, bf16[512,512]{1,0:T(8,128)(2,1)S(1)}, u32[]{:S(2)}, u32[]{:S(2)}) collective-permute-start(bf16[512,512]{1,0:T(8,128)(2,1)S(1)} %collective-permute-done.148.refs_14_), channel_id=1, source_target_pairs={{0,1},{1,0},{2,3},{3,2},{4,5},{5,4},{6,7},{7,6},{8,9},{9,8},{10,11... | collective-permute-start | bytes 1572872 | tf_op jit(solution)/shard_map/ppermute | solution.py:414
  65.9 3.9 %collective-permute-start.152 = (bf16[512,512]{1,0:T(8,128)(2,1)S(1)}, bf16[512,512]{1,0:T(8,128)(2,1)S(1)}, u32[]{:S(2)}, u32[]{:S(2)}) collective-permute-start(bf16[512,512]{1,0:T(8,128)(2,1)S(1)} %collective-permute-done.151.refs_18_), channel_id=1, source_target_pairs={{0,1},{1,0},{2,3},{3,2},{4,5},{5,4},{6,7},{7,6},{8,9},{9,8},{10,11... | collective-permute-start | bytes 1572872 | tf_op jit(solution)/shard_map/ppermute | solution.py:414
  66.4 3.4 %collective-permute-start.146 = (bf16[256,512]{1,0:T(8,128)(2,1)S(1)}, bf16[256,512]{1,0:T(8,128)(2,1)S(1)}, u32[]{:S(2)}, u32[]{:S(2)}) collective-permute-start(bf16[256,512]{1,0:T(8,128)(2,1)S(1)} %collective-permute-done.145.refs_10_), channel_id=1, source_target_pairs={{0,1},{1,0},{2,3},{3,2},{4,5},{5,4},{6,7},{7,6},{8,9},{9,8},{10,11... | collective-permute-start | bytes 786440 | tf_op jit(solution)/shard_map/ppermute | solution.py:414

commit v3 on v2

v3 whole, which is shorter than its diff:
```python
import functools
import math

import jax
import jax.numpy as jnp
from jax import lax
from jax.experimental import pallas as pl
from jax.experimental.pallas import tpu as pltpu
from jax.sharding import PartitionSpec as P


HEAD_SIZE = 64
EPSILON = 1e-05
FLAG_ROWS = 8
EDGE_STEP = 512

f32 = jnp.float32
bf16 = jnp.bfloat16
f8 = jnp.float8_e4m3fn

VMEM = pl.BlockSpec(memory_space=pltpu.VMEM)
SMEM = pl.BlockSpec(memory_space=pltpu.SMEM)
HBM = pl.BlockSpec(memory_space=pltpu.HBM)

NT = (((1,), (1,)), ((), ()))
NN = (((1,), (0,)), ((), ()))

PARAMS = pltpu.CompilerParams(vmem_limit_bytes=24 << 20)


def dot(a, b, dims=NN):
    return lax.dot_general(a, b, dims, preferred_element_type=f32)


def norm_rows(rows, gain):
    mean = jnp.mean(rows, -1, keepdims=True)
    centred = rows - mean
    variance = jnp.mean(centred * centred, -1, keepdims=True)
    return (centred * lax.rsqrt(variance + EPSILON) * gain).astype(bf16)


def one_hot_columns(index_row, count, live=None):
    hit = lax.broadcasted_iota(jnp.int32, (count, index_row.shape[1]), 0) == index_row
    if live is not None:
        hit = jnp.logical_and(hit, live)
    return jnp.where(hit, 1.0, 0.0).astype(bf16)


def narrow_one_hot(index_row, count):
    numbers = lax.broadcasted_iota(jnp.int16, (count, index_row.shape[1]), 0)
    hit = numbers == index_row.astype(jnp.int16)
    return jnp.where(hit, jnp.ones((), bf16), jnp.zeros((), bf16)).astype(f8)


def in_hbm(*arrays):
    return [pltpu.with_memory_space_constraint(array, pltpu.HBM) for array in arrays]


def xor_route(count, mask):
    return [(i, i ^ mask) for i in range(count)]


def prologue_kernel(
    x_hbm, gain_hbm, w_hbm, sender_hbm, up_hbm, down_hbm, wo_hbm, wn_hbm, late_gain_hbm, landing_hbm,
    tally_hbm, companion_hbm, scale_hbm,
    low_ref, high_ref, pair_ref, q_ref, kv_ref, k_ref, v_ref, bundle_ref, scales_ref,
    share_ref, late_gain_ref, landing_ref, *rest,
):
    out_refs = rest[:-8]
    x_ref, gain_ref, w_ref, sender_ref, tally_ref, companion_ref, scale_ref, sems = rest[-8:]
    nodes, _ = x_ref.shape
    cols = q_ref.shape[1]
    sources = (
        (x_hbm, x_ref),
        (gain_hbm, gain_ref),
        (w_hbm, w_ref),
        (sender_hbm, sender_ref),
        (late_gain_hbm, late_gain_ref),
        (landing_hbm, landing_ref),
        (tally_hbm, tally_ref),
        (companion_hbm, companion_ref),
        (scale_hbm, scale_ref),
    )
    first = 0
    for piece in (up_hbm, down_hbm, wo_hbm, wn_hbm):
        sources += ((piece, bundle_ref.at[pl.ds(first, piece.shape[0])]),)
        first += piece.shape[0]
    copies = [
        pltpu.make_async_copy(source, target, sems.at[i])
        for i, (source, target) in enumerate(sources)
    ]
    for copy in copies:
        copy.start()

    copies[0].wait()
    copies[1].wait()
    normed = norm_rows(x_ref[...].astype(f32), gain_ref[...])
    copies[2].wait()
    weights = jnp.concatenate([w_ref[0], w_ref[1], w_ref[2]], axis=1)
    projected = dot(normed, weights).astype(bf16)
    q_ref[...] = projected[:, :cols]
    kv_ref[...] = projected[:, cols:]
    k_ref[...] = projected[:, cols : 2 * cols]
    v_ref[...] = projected[:, 2 * cols :]

    for copy in copies[3:-4]:
        copy.wait()
    one, two = companion_ref[0, 0], companion_ref[1, 0]
    low, high = jnp.minimum(one, two), jnp.maximum(one, two)
    low_ref[0] = low - 1
    high_ref[0] = high - 1
    pair_ref[0] = lax.shift_right_logical((high - 1) * (high - 2), 1) + low - 1
    for h in range(scales_ref.shape[0]):
        scales_ref[h] = jnp.full(scales_ref.shape[1:], scale_ref[h], f32)

    part = lax.axis_index("mp")
    rows = share_ref.shape[0]
    share_ref[...] = x_ref[pl.ds(pl.multiple_of(part * rows, rows), rows), :]
    quarter = x_ref[:, pl.ds(pl.multiple_of(part * cols, 128), cols)]
    quarter_t = quarter.astype(f32).T.astype(bf16)
    cap = sender_ref.shape[1]
    slot = lax.broadcasted_iota(jnp.int32, (1, cap), 1)
    (out_ref,) = out_refs
    for dest in range(out_ref.shape[0]):
        live = slot < tally_ref[0, dest]
        pick = one_hot_columns(sender_ref[dest : dest + 1, :], nodes, live)
        out_ref[dest, :cols, :] = dot(quarter_t, pick).astype(bf16)
        out_ref[dest, cols:, :] = jnp.broadcast_to(
            jnp.where(live, 1.0, 0.0), (FLAG_ROWS, cap)
        ).astype(bf16)
    for copy in copies[-4:]:
        copy.wait()


def prologue(
    tally, companion, scale, x, gain, w, sender, pieces, late_gain, landing, shares
):
    nodes, width = x.shape
    cols = w.shape[2]
    peers, cap = sender.shape
    return pl.pallas_call(
        prologue_kernel,
        out_shape=[jax.ShapeDtypeStruct((1,), jnp.int32)] * 3
        + [jax.ShapeDtypeStruct((nodes, n * cols), bf16) for n in (1, 2, 1, 1)]
        + [
            jax.ShapeDtypeStruct((sum(p.shape[0] for p in pieces), width), bf16),
            jax.ShapeDtypeStruct((scale.shape[0], 8, 128), f32),
            jax.ShapeDtypeStruct((nodes // shares, width), bf16),
            jax.ShapeDtypeStruct(late_gain.shape, f32),
            jax.ShapeDtypeStruct(landing.shape, jnp.int32),
        ]
        + [jax.ShapeDtypeStruct((peers, cols + FLAG_ROWS, cap), bf16)],
        in_specs=[HBM] * (9 + len(pieces)),
        out_specs=[SMEM] * 3 + [VMEM] * 10,
        scratch_shapes=[
            pltpu.VMEM(x.shape, bf16),
            pltpu.VMEM(gain.shape, f32),
            pltpu.VMEM(w.shape, bf16),
            pltpu.VMEM(sender.shape, jnp.int32),
            pltpu.SMEM(tally.shape, jnp.int32),
            pltpu.SMEM(companion.shape, jnp.int32),
            pltpu.SMEM(scale.shape, f32),
            pltpu.SemaphoreType.DMA((9 + len(pieces),)),
        ],
        name="prologue",
        compiler_params=PARAMS,
        cost_estimate=pl.CostEstimate(
            flops=2 * nodes * width * 3 * cols, bytes_accessed=4 << 20, transcendentals=0
        ),
    )(
        *in_hbm(
            x, gain, w, sender, *pieces, late_gain, landing, tally, companion, scale
        )
    )


def edge_kernel(
    tail_hbm, sink_hbm, x_hbm, local_ref, degree_ref, tail_ref, sink_ref, x_ref, counts_ref, sems
):
    copies = [
        pltpu.make_async_copy(tail_hbm, tail_ref, sems.at[0]),
        pltpu.make_async_copy(sink_hbm, sink_ref, sems.at[1]),
        pltpu.make_async_copy(x_hbm, x_ref, sems.at[2]),
    ]
    for copy in copies:
        copy.start()
    nodes, rows = counts_ref.shape
    edges = tail_ref.shape[1]
    step = math.gcd(edges, EDGE_STEP)
    first = lax.axis_index("mp") * rows
    counts_ref[...] = jnp.zeros_like(counts_ref)
    copies[0].wait()
    copies[1].wait()

    def add(turn, unused):
        at = pl.ds(pl.multiple_of(turn * step, step), step)
        tail = narrow_one_hot(tail_ref[:, at], nodes)
        sink = narrow_one_hot(sink_ref[:, at] - first, rows)
        counts_ref[...] += dot(tail, sink, NT)
        return unused

    lax.fori_loop(0, edges // step, add, 0)
    counts = counts_ref[...].T
    high = jnp.floor(counts * (1.0 / 256.0))
    low = counts - 256.0 * high
    pair = jnp.concatenate([high, low], axis=0).astype(bf16)
    copies[2].wait()
    sums = dot(pair, x_ref[...])
    own = x_ref[pl.ds(pl.multiple_of(first, rows), rows), :]
    local_ref[...] = 256.0 * sums[:rows] + sums[rows:] + own.astype(f32)
    degree = jnp.sum(counts, -1, keepdims=True)
    degree_ref[...] = jnp.broadcast_to(1.0 + degree, degree_ref.shape)


def edge_sums(tail, sink, x, rows):
    edges = tail.shape[1]
    nodes, width = x.shape
    return pl.pallas_call(
        edge_kernel,
        out_shape=[
            jax.ShapeDtypeStruct((rows, width), f32),
            jax.ShapeDtypeStruct((rows, 128), f32),
        ],
        in_specs=[HBM] * 3,
        out_specs=[VMEM] * 2,
        scratch_shapes=[
            pltpu.VMEM((1, edges), jnp.int32),
            pltpu.VMEM((1, edges), jnp.int32),
            pltpu.VMEM((nodes, width), bf16),
            pltpu.VMEM((nodes, rows), f32),
            pltpu.SemaphoreType.DMA((3,)),
        ],
        name="edge_sums",
        compiler_params=PARAMS,
        cost_estimate=pl.CostEstimate(
            flops=2 * nodes * nodes * edges, bytes_accessed=2 << 20, transcendentals=0
        ),
    )(*in_hbm(tail, sink, x))


def landing_kernel(edge_degree_ref, landing_ref, arrived_ref, degree_ref, *refs):
    outs, whole_ref = refs[:-1], refs[-1]
    part = lax.axis_index("mp")
    nodes = whole_ref.shape[0]
    rows, cols = outs[0].shape
    peers = arrived_ref.shape[0]
    land = jnp.concatenate(
        [one_hot_columns(landing_ref[p : p + 1, :], nodes) for p in range(peers)], axis=1
    )
    arrived = jnp.concatenate([arrived_ref[p] for p in range(peers)], axis=1)
    boundary = dot(land, arrived, NT)
    whole_ref[:, : boundary.shape[1]] = boundary
    for k, out_ref in enumerate(outs):
        at = jnp.bitwise_xor(part, k) * rows
        out_ref[...] = whole_ref[pl.ds(pl.multiple_of(at, rows), rows), :cols]
    own = pl.ds(pl.multiple_of(part * rows, rows), rows)
    degree_ref[...] = edge_degree_ref[...] + whole_ref[own, cols : cols + 1]


def landed_sums(edge_degree, landing, arrived, nodes, cols, shares):
    rows = nodes // shares
    return pl.pallas_call(
        landing_kernel,
        out_shape=[jax.ShapeDtypeStruct((rows, 128), f32)]
        + [jax.ShapeDtypeStruct((rows, cols), f32)] * shares,
        in_specs=[VMEM] * 3,
        out_specs=[VMEM] * (1 + shares),
        scratch_shapes=[pltpu.VMEM((nodes, 2 * cols), f32)],
        name="landing",
        compiler_params=PARAMS,
        cost_estimate=pl.CostEstimate(
            flops=2 * nodes * 1024 * 256, bytes_accessed=2 << 20, transcendentals=0
        ),
    )(edge_degree, landing, arrived)


def attention_kernel(
    offsets, scales_ref, q_ref, own_ref, one_any, two_any, *refs
):
    outs, (one_ref, two_ref, block_ref, sems) = refs[:-4], refs[-4:]
    copies = [
        pltpu.make_async_copy(one_any, one_ref, sems.at[0]),
        pltpu.make_async_copy(two_any, two_ref, sems.at[1]),
    ]
    for copy in copies:
        copy.start()
    part = lax.axis_index("mp")
    rows, cols = outs[0].shape
    heads = cols // HEAD_SIZE
    count = len(offsets)
    base = jnp.bitwise_xor(part, offsets[0]) // count * count
    at = pl.multiple_of(base * rows, count * rows)
    sources = (own_ref, one_ref, two_ref)
    for h in range(heads):
        band = slice(h * HEAD_SIZE, (h + 1) * HEAD_SIZE)
        q = q_ref[pl.ds(at, count * rows), band]
        factor = scales_ref[h, :1, :1] * math.log2(math.e)
        parts = []
        for i, r in enumerate(sources):
            if h == 0 and i > 0:
                copies[i - 1].wait()
            parts.append(dot(q, r[:, band], NT) * factor)
        top = functools.reduce(jnp.maximum, [jnp.max(s, -1, keepdims=True) for s in parts])
        powers = [jnp.exp2(s - top) for s in parts]
        inverse = 1.0 / sum(jnp.sum(p, -1, keepdims=True) for p in powers)
        value_band = slice(cols + h * HEAD_SIZE, cols + (h + 1) * HEAD_SIZE)
        attended = sum(
            dot((p * inverse).astype(bf16), r[:, value_band]) for p, r in zip(powers, sources)
        )
        block_ref[:, band] = attended.astype(bf16)
    for k, out_ref in zip(offsets, outs):
        place = (jnp.bitwise_xor(part, k) - base) * rows
        out_ref[...] = block_ref[pl.ds(pl.multiple_of(place, rows), rows), :]


def attention(scales, q, own, one, two, shares, offsets):
    nodes, cols = q.shape
    rows = nodes // shares
    any_space = pl.BlockSpec(memory_space=pl.ANY)
    return pl.pallas_call(
        functools.partial(attention_kernel, offsets),
        out_shape=[jax.ShapeDtypeStruct((rows, cols), bf16)] * len(offsets),
        in_specs=[VMEM] * 3 + [any_space] * 2,
        out_specs=[VMEM] * len(offsets),
        scratch_shapes=[
            pltpu.VMEM(one.shape, bf16),
            pltpu.VMEM(two.shape, bf16),
            pltpu.VMEM((len(offsets) * rows, cols), bf16),
            pltpu.SemaphoreType.DMA((2,)),
        ],
        name="attention",
        compiler_params=PARAMS,
        cost_estimate=pl.CostEstimate(
            flops=4 * rows * len(offsets) * 3 * nodes * 256,
            bytes_accessed=2 << 20,
            transcendentals=1 << 20,
        ),
    )(scales, q, own, one, two)


def final_kernel(shares, share_ref, gain_ref, local_ref, degree_ref, *refs):
    att, far_sums, bundles = (refs[i * shares : (i + 1) * shares] for i in range(3))
    out_ref, mix_buf, up_buf, down_buf, sems = refs[3 * shares :]
    _, width = out_ref.shape
    wide = up_buf.shape[2]
    mix_at, up_at, down_at = (
        pl.ds(width + wide, mix_buf.shape[1]), pl.ds(0, width), pl.ds(width, wide)
    )
    copies = []
    for i, (at, buf) in enumerate(((mix_at, mix_buf), (up_at, up_buf), (down_at, down_buf))):
        copies.append(
            [
                pltpu.make_async_copy(source.at[at], buf.at[k], sems.at[i, k])
                for k, source in enumerate(bundles)
            ]
        )
    for copy in copies[0]:
        copy.start()
    for k in range(shares):
        copies[1][k].start()
        copies[2][k].start()
    mixed = share_ref[...].astype(f32)
    part = lax.axis_index("mp")
    cols = att[0].shape[1]
    terms = []
    for k in range(shares):
        at = pl.multiple_of(jnp.bitwise_xor(part, k) * cols, 128)
        sums = local_ref[:, pl.ds(at, cols)] + far_sums[k][...]
        terms += [att[k][...], (sums / degree_ref[...]).astype(bf16)]
    terms = jnp.concatenate(terms, axis=1)
    for copy in copies[0]:
        copy.wait()
    mixed = mixed + dot(terms, mix_buf[...].reshape(-1, width))
    normed = norm_rows(mixed, gain_ref[...])
    total = mixed
    for k in range(shares):
        copies[1][k].wait()
        wide = dot(normed, up_buf[k])
        hidden = (0.5 * wide * (1.0 + lax.erf(wide * (0.5**0.5)))).astype(bf16)
        copies[2][k].wait()
        total = total + dot(hidden, down_buf[k])
    out_ref[...] = total.astype(bf16)


def final(share, gain, local, degree, att, far_sums, bundles):
    shares = len(att)
    rows, width = share.shape
    cols = att[0].shape[1]
    wide = bundles[0].shape[0] - width - 2 * cols
    any_space = pl.BlockSpec(memory_space=pl.ANY)
    return pl.pallas_call(
        functools.partial(final_kernel, shares),
        out_shape=jax.ShapeDtypeStruct((rows, width), bf16),
        in_specs=[VMEM] * (4 + 2 * shares) + [any_space] * shares,
        out_specs=VMEM,
        scratch_shapes=[
            pltpu.VMEM((shares, *shape), bf16)
            for shape in ((2 * cols, width), (width, wide), (wide, width))
        ]
        + [pltpu.SemaphoreType.DMA((3, shares))],
        name="final",
        compiler_params=PARAMS,
        cost_estimate=pl.CostEstimate(
            flops=2 * rows * width * 4096, bytes_accessed=6 << 20, transcendentals=1 << 18
        ),
    )(share, gain, local, degree, *att, *far_sums, *bundles)


def gather_pieces(piece, axis):
    count = lax.axis_size(axis)
    pieces = {0: piece}
    bit = count // 2
    while bit:
        for k in list(pieces):
            pieces[k | bit] = lax.ppermute(pieces[k], axis, xor_route(count, bit))
        bit //= 2
    return [pieces[k] for k in range(count)]


def layer(
    x,
    mixer_gain,
    perceptron_gain,
    projectors,
    scale,
    out_projector,
    neighbour_projector,
    expand,
    contract,
    companion,
    sender,
    tally,
    landing,
    tail,
    sink,
):
    peers = lax.axis_size("dom")
    shares = lax.axis_size("mp")
    cols = projectors.shape[2]

    def send(block, mask):
        return lax.ppermute(block, "dom", xor_route(peers, mask))

    (
        low_mask, high_mask, pair, q, kv, k, v, bundle, scales, share, late_gain, landing,
        outgoing,
    ) = prologue(
        tally, companion, scale, x, mixer_gain[None, :], projectors, sender[0],
        (expand, contract, out_projector, neighbour_projector), perceptron_gain[None, :],
        landing[0], shares,
    )
    bundles = gather_pieces(bundle, "mp")
    nodes = x.shape[0]

    def beside(outgoing, tail, sink, x):
        arrived = lax.all_to_all(outgoing, "dom", split_axis=0, concat_axis=0, tiled=True)
        return arrived, *edge_sums(tail, sink, x, nodes // shares)

    operands = (kv, k, v, outgoing, tail, sink, x)
    if peers * (peers - 1) // 2 <= 32:
        branches = []
        for high in range(1, peers):
            for low in range(1, high):

                def branch(kv, k, v, *rest, low=low, high=high):
                    if low & high & (peers // 2):
                        one_k, one_v = send(k, low), send(v, low)
                        two_k, two_v = send(one_k, low ^ high), send(one_v, low ^ high)
                        one = jnp.concatenate([one_k, one_v], axis=1)
                        two = jnp.concatenate([two_k, two_v], axis=1)
                    else:
                        one, two = send(kv, low), send(kv, high)
                    return one, two, *beside(*rest)

                branches.append(branch)
        one, two, arrived, local, edge_degree = lax.switch(pair[0], branches, *operands)
    else:
        hops = [lambda kv, mask=mask: send(kv, mask) for mask in range(1, peers)]
        one = lax.switch(low_mask[0], hops, kv)
        two = lax.switch(high_mask[0], hops, kv)
        arrived, local, edge_degree = beside(outgoing, tail, sink, x)

    degree, *far_sums = landed_sums(edge_degree, landing, arrived, nodes, cols, shares)

    def swap(chunk, k):
        return lax.ppermute(chunk, "mp", xor_route(shares, k)) if k else chunk

    far_sums = [swap(chunk, k) for k, chunk in enumerate(far_sums)]
    groups = [tuple(range(shares // 2, shares)), tuple(range(shares // 2))]
    att = [None] * shares
    for group in groups:
        chunks = attention(scales, q, kv, one, two, shares, group)
        for k, chunk in zip(group, chunks):
            att[k] = swap(chunk, k)
    return final(share, late_gain, local, degree, att, far_sums, bundles)


def solution(mesh):
    return jax.shard_map(
        layer,
        mesh=mesh,
        in_specs=(
            P("dom", None),
            P(),
            P(),
            P(None, None, "mp"),
            P("mp"),
            P("mp", None),
            P("mp", None),
            P(None, "mp"),
            P("mp", None),
            P(),
            P("dom", None, None),
            P("dom", None),
            P("dom", None, None),
            P("dom", None),
            P("dom", None),
        ),
        out_specs=P(("dom", "mp"), None),
        check_vma=False,
    )
```

time: 74.2 us -> 78.1 us (1.053)
  waiting for transfers between devices: 30.1 us -> 38.2 us
  starting transfers between devices: 19.9 us -> 15.7 us
  Pallas kernels: 21.3 us -> 23 us
    ppermute x9 -> x3, waiting for transfers between devices: 3.68 us -> 29.1 us  [gather_pieces(): pieces[k | bit] = lax.ppermute(pieces[k], axis, xor_route(count, bit))]
    ppermute x6, waiting for transfers between devices: 22.7 us -> 3.85 us  [swap(): return lax.ppermute(chunk, 'mp', xor_route(shares, k)) if k else chunk]
    ppermute x6 -> x2, starting transfers between devices: 10.8 us -> 4.42 us  [send(): return lax.ppermute(block, 'dom', xor_route(peers, mask))]
    all_to_all x0 -> x1, starting transfers between devices: none -> 4.06 us  [beside(): lax.all_to_all(outgoing, 'dom', split_axis=0, concat_axis=0, tiled=True)]
    all_to_all x0 -> x1, waiting for transfers between devices: none -> 2.71 us  [beside(): lax.all_to_all(outgoing, 'dom', split_axis=0, concat_axis=0, tiled=True)]
    ppermute x9 -> x3, starting transfers between devices: 4.86 us -> 3.04 us  [gather_pieces(): pieces[k | bit] = lax.ppermute(pieces[k], axis, xor_route(count, bit))]
    ppermute x6 -> x2, waiting for transfers between devices: 3.72 us -> 2.52 us  [send(): return lax.ppermute(block, 'dom', xor_route(peers, mask))]
    pallas_call x1, Pallas kernels: 2.72 us -> 3.69 us  [prologue(): pl.pallas_call(prologue_kernel, out_shape=[jax.ShapeDtypeStruct((1,), jnp...]
  transfers between devices with their start and end apart: 21 -> 12, of which waited for: 6 -> 5; matrix products, arithmetic and copies ran while one was open for 0% -> 0% of each run, Pallas kernels for 21% -> 20%
where the time goes in v3:
time: 78.1 us; the launch traced here: 77.8 us
  waiting for transfers between devices  38.2 us (49%)
  Pallas kernels  23 us (29%)
  starting transfers between devices  15.7 us (20%)
  between operations  0.79 us (1%)
    ppermute x3, waiting for transfers between devices, gather_pieces(): pieces[k | bit] = lax.ppermute(pieces[k], axis, xor_route(count, bit))  29.1 us
    pallas_call x1, Pallas kernels, edge_sums(): pl.pallas_call(edge_kernel, out_shape=[jax.ShapeDtypeStruct((rows, width)...  7.89 us
    pallas_call x2, Pallas kernels, attention(): pl.pallas_call(functools.partial(attention_kernel, offsets), out_shape=[j...  5.86 us
    ppermute x2, starting transfers between devices, send(): return lax.ppermute(block, 'dom', xor_route(peers, mask))  4.42 us
    ppermute x6, starting transfers between devices, swap(): return lax.ppermute(chunk, 'mp', xor_route(shares, k)) if k else chunk  4.19 us
    all_to_all x1, starting transfers between devices, beside(): lax.all_to_all(outgoing, 'dom', split_axis=0, concat_axis=0, tiled=True)  4.06 us
    pallas_call x1, Pallas kernels, final(): pl.pallas_call(functools.partial(final_kernel, shares), out_shape=jax.Sha...  4.05 us
    ppermute x6, waiting for transfers between devices, swap(): return lax.ppermute(chunk, 'mp', xor_route(shares, k)) if k else chunk  3.85 us
  transfers between devices with their start and end apart: 12, of which 5 were waited for; matrix products, arithmetic and copies ran while one was open for 0% of the time, Pallas kernels for 20%

profile of v3, /device:TPU:0, one launch (start us, length us, event | category | flops | bytes accessed | tf_op | source)
XLA Modules:
  0.0 77.8 jit_solution(10169575894618035354)
XLA Ops:
  0.0 3.7 %prologue.1 = (s32[1]{0:T(128)}, s32[1]{0:T(128)}, s32[1]{0:T(128)}, bf16[512,128]{1,0:T(8,128)(2,1)S(1)}, bf16[512,256]{1,0:T(8,128)(2,1)S(1)}, /*index=5*/bf16...) custom-call(bf16[512,512]{1,0:T(8,128)(2,1)} %x_hbm.1, ...), custom_call_target="tpu_custom_call" | custom-call | flops 201326592 | bytes 4194304 | tf_op jit(solution)/shard_map/prologue/pallas_call | solution.py:141
  3.7 3.0 %collective-permute-start.61 = (bf16[1280,512]{1,0:T(8,128)(2,1)}, bf16[1280,512]{1,0:T(8,128)(2,1)}, u32[]{:S(2)}, u32[]{:S(2)}) collective-permute-start(bf16[1280,512]{1,0:T(8,128)(2,1)} %get-tuple-element.429.refs_8_), channel_id=1, source_target_pairs={{0,2},{1,3},{2,0},{3,1},{4,6},{5,7},{6,4},{7,5},{8,10},{9,11},{10,... | collective-permute-start | bytes 3932168 | tf_op jit(solution)/shard_map/ppermute | solution.py:415
  6.7 0.0 collective-permute-start.60
  6.7 29.1 %collective-permute-done.61.refs_10_ = bf16[1280,512]{1,0:T(8,128)(2,1)} collective-permute-done((bf16[1280,512]{1,0:T(8,128)(2,1)}, bf16[1280,512]{1,0:T(8,128)(2,1)}, u32[]{:S(2)}, u32[]{:S(2)}) %collective-permute-start.61) | collective-permute-done | bytes 1310752 | tf_op jit(solution)/shard_map/ppermute | solution.py:415
  35.8 0.0 collective-permute-start.62
  36.4 21.7 %conditional.1 = (bf16[512,256]{1,0:T(8,128)(2,1)}, bf16[512,256]{1,0:T(8,128)(2,1)}, bf16[8,136,128]{2,1,0:T(8,128)(2,1)}, f32[128,512]{1,0:T(8,128)S(1)}, f32[128,128]{1,0:T(8,128)S(1)}) conditional(s32[]{:T(128)} %bitcast.4, (bf16[512,256]{1,0:T(8,128)(2,1)S(1)}, bf16[8,136,128]{2,1,0:T(8,128)(2,1)}, ...), branch_computations={%region_0.0_spmd, %region_1.0_spmd, %region_2.0_spmd, %region_3.0_... | conditional | flops 8590983168 | bytes 6078696 | solution.py:476
  36.4 2.9 %collective-permute-start.7 = (bf16[512,256]{1,0:T(8,128)(2,1)S(1)}, bf16[512,256]{1,0:T(8,128)(2,1)}, u32[]{:S(2)}, u32[]{:S(2)}) collective-permute-start(bf16[512,256]{1,0:T(8,128)(2,1)S(1)} %get-tuple-element.248), channel_id=1, source_target_pairs={{0,16},{4,20},{8,24},{12,28},{16,0},{20,4},{24,8},{28,12},{1,17},{... | collective-permute-start | bytes 786440 | tf_op jit(solution)/shard_map/cond/branch_3_fun/ppermute | solution.py:442
  39.3 1.5 %collective-permute-start.6 = (bf16[512,256]{1,0:T(8,128)(2,1)S(1)}, bf16[512,256]{1,0:T(8,128)(2,1)}, u32[]{:S(2)}, u32[]{:S(2)}) collective-permute-start(bf16[512,256]{1,0:T(8,128)(2,1)S(1)} %get-tuple-element.248), channel_id=1, source_target_pairs={{0,4},{4,0},{8,12},{12,8},{16,20},{20,16},{24,28},{28,24},{1,5},{5... | collective-permute-start | bytes 786440 | tf_op jit(solution)/shard_map/cond/branch_3_fun/ppermute | solution.py:442
  40.9 4.1 %all-to-all-start.3 = ((bf16[8,136,128]{2,1,0:T(8,128)(2,1)}), bf16[8,136,128]{2,1,0:T(8,128)(2,1)}, u32[]{:S(2)}, u32[]{:S(2)}) async-start(bf16[8,136,128]{2,1,0:T(8,128)(2,1)} %get-tuple-element.249), calls=%async_computation.3 | async-start | bytes 557056 | tf_op jit(solution)/shard_map/cond/branch_3_fun/all_to_all | solution.py:456
  44.9 7.9 %edge_sums.24 = (f32[128,512]{1,0:T(8,128)S(1)}, f32[128,128]{1,0:T(8,128)S(1)}) custom-call(s32[1,16384]{1,0:T(1,128)} %get-tuple-element.250.tail_hbm, s32[1,16384]{1,0:T(1,128)} %get-tuple-element.251.sink_hbm, bf16[512,512]{1,0:T(8,128)(2,1)} %get-tuple-element.252.x_hbm), custom_call_target="tpu_custom_call" | custom-call | flops 8589934592 | bytes 2097152 | tf_op jit(solution)/shard_map/cond/branch_3_fun/edge_sums/pallas_call | solution.py:218
  52.8 2.5 %collective-permute-done.7 = bf16[512,256]{1,0:T(8,128)(2,1)} collective-permute-done((bf16[512,256]{1,0:T(8,128)(2,1)S(1)}, bf16[512,256]{1,0:T(8,128)(2,1)}, u32[]{:S(2)}, u32[]{:S(2)}) %collective-permute-start.7) | collective-permute-done | bytes 262176 | tf_op jit(solution)/shard_map/cond/branch_3_fun/ppermute | solution.py:442
  55.3 0.0 collective-permute-done.6
  55.3 2.7 %all-to-all-done.3 = bf16[8,136,128]{2,1,0:T(8,128)(2,1)} async-done(((bf16[8,136,128]{2,1,0:T(8,128)(2,1)}), bf16[8,136,128]{2,1,0:T(8,128)(2,1)}, u32[]{:S(2)}, u32[]{:S(2)}) %all-to-all-start.3) | async-done | bytes 278560 | tf_op jit(solution)/shard_map/cond/branch_3_fun/all_to_all | solution.py:456
  58.1 2.9 %attention.3 = (bf16[128,128]{1,0:T(8,128)(2,1)S(1)}, bf16[128,128]{1,0:T(8,128)(2,1)S(1)}) custom-call(f32[2,8,128]{2,1,0:T(8,128)S(1)} %get-tuple-element.417.scales_ref, bf16[512,128]{1,0:T(8,128)(2,1)S(1)} %get-tuple-element.418.q_ref, bf16[512,256]{1,0:T(8,128)(2,1)S(1)} %get-tuple-element.408.own_ref, bf16[512,256]{1,0:T(8,128)(2,1)} %get-tuple-element.419.one_any, ...), custom_call_target="tpu_custom_call" | custom-call | flops 402653184 | bytes 2097152 | tf_op jit(solution)/shard_map/attention/pallas_call | solution.py:320
  61.0 1.6 %collective-permute-start.55 = (bf16[128,128]{1,0:T(8,128)(2,1)S(1)}, bf16[128,128]{1,0:T(8,128)(2,1)S(1)}, u32[]{:S(2)}, u32[]{:S(2)}) collective-permute-start(bf16[128,128]{1,0:T(8,128)(2,1)S(1)} %get-tuple-element.423), channel_id=1, source_target_pairs={{0,2},{1,3},{2,0},{3,1},{4,6},{5,7},{6,4},{7,5},{8,10},{9,11},{10,... | collective-permute-start | bytes 98312 | tf_op jit(solution)/shard_map/ppermute | solution.py:486
  62.6 0.0 collective-permute-start.56
  62.6 2.9 %attention.2 = (bf16[128,128]{1,0:T(8,128)(2,1)S(1)}, bf16[128,128]{1,0:T(8,128)(2,1)S(1)}) custom-call(f32[2,8,128]{2,1,0:T(8,128)S(1)} %get-tuple-element.417.scales_ref, bf16[512,128]{1,0:T(8,128)(2,1)S(1)} %get-tuple-element.418.q_ref, bf16[512,256]{1,0:T(8,128)(2,1)S(1)} %get-tuple-element.408.own_ref, bf16[512,256]{1,0:T(8,128)(2,1)} %get-tuple-element.419.one_any, ...), custom_call_target="tpu_custom_call" | custom-call | flops 402653184 | bytes 2097152 | tf_op jit(solution)/shard_map/attention/pallas_call | solution.py:320
  65.6 0.7 collective-permute-start.54
  66.2 1.5 %landing.1 = (f32[128,128]{1,0:T(8,128)S(1)}, f32[128,128]{1,0:T(8,128)S(1)}, f32[128,128]{1,0:T(8,128)S(1)}, f32[128,128]{1,0:T(8,128)S(1)}, f32[128,128]{1,0:T(8,128)S(1)}) custom-call(f32[128,128]{1,0:T(8,128)S(1)} %get-tuple-element.413.edge_degree_ref, s32[8,128]{1,0:T(8,128)S(1)} %get-tuple-element.414.landing_ref, ...), custom_call_target="tpu_custom_call" | custom-call | flops 268435456 | bytes 2097152 | tf_op jit(solution)/shard_map/landing/pallas_call | solution.py:262
  67.8 0.0 collective-permute-done.55.refs_2_
  67.8 0.1 collective-permute-start.57
  67.8 0.0 collective-permute-done.56.refs_3_
  67.8 1.6 %collective-permute-start.58 = (f32[128,128]{1,0:T(8,128)S(1)}, f32[128,128]{1,0:T(8,128)S(1)}, u32[]{:S(2)}, u32[]{:S(2)}) collective-permute-start(f32[128,128]{1,0:T(8,128)S(1)} %get-tuple-element.427), channel_id=1, source_target_pairs={{0,2},{1,3},{2,0},{3,1},{4,6},{5,7},{6,4},{7,5},{8,10},{9,11},{10,... | collective-permute-start | bytes 196616 | tf_op jit(solution)/shard_map/ppermute | solution.py:486
  69.5 0.0 collective-permute-done.54.refs_1_
  69.5 0.2 collective-permute-start.59
  69.7 0.0 collective-permute-done.57.refs_5_
  69.7 2.6 %collective-permute-done.58.refs_6_ = f32[128,128]{1,0:T(8,128)S(1)} collective-permute-done((f32[128,128]{1,0:T(8,128)S(1)}, f32[128,128]{1,0:T(8,128)S(1)}, u32[]{:S(2)}, u32[]{:S(2)}) %collective-permute-start.58) | collective-permute-done | bytes 65568 | tf_op jit(solution)/shard_map/ppermute | solution.py:486
  72.3 1.2 %collective-permute-done.59.refs_7_ = f32[128,128]{1,0:T(8,128)S(1)} collective-permute-done((f32[128,128]{1,0:T(8,128)S(1)}, f32[128,128]{1,0:T(8,128)S(1)}, u32[]{:S(2)}, u32[]{:S(2)}) %collective-permute-start.59) | collective-permute-done | bytes 65568 | tf_op jit(solution)/shard_map/ppermute | solution.py:486
  73.5 0.0 collective-permute-done.60.refs_9_
  73.5 0.0 collective-permute-done.62.refs_11_
  73.5 4.0 %final.1 = bf16[128,512]{1,0:T(8,128)(2,1)} custom-call(bf16[128,512]{1,0:T(8,128)(2,1)S(1)} %get-tuple-element.405.share_ref, f32[1,512]{1,0:T(1,128)S(1)} %get-tuple-element.406.gain_ref, f32[128,512]{1,0:T(8,128)S(1)} %get-tuple-element.412.local_ref, f32[128,128]{1,0:T(8,128)S(1)} %get-tuple-element.416.degree_ref, ...), custom_call_target="tpu_custom_call" | custom-call | flops 536870912 | bytes 6291456 | tf_op jit(solution)/shard_map/final/pallas_call | solution.py:391
Async XLA Ops:
  3.7 32.1 %collective-permute-start.61 = (bf16[1280,512]{1,0:T(8,128)(2,1)}, bf16[1280,512]{1,0:T(8,128)(2,1)}, u32[]{:S(2)}, u32[]{:S(2)}) collective-permute-start(bf16[1280,512]{1,0:T(8,128)(2,1)} %get-tuple-element.429.refs_8_), channel_id=1, source_target_pairs={{0,2},{1,3},{2,0},{3,1},{4,6},{5,7},{6,4},{7,5},{8,10},{9,11},{10,... | collective-permute-start | bytes 3932168 | tf_op jit(solution)/shard_map/ppermute | solution.py:415
  6.7 66.8 %collective-permute-start.60 = (bf16[1280,512]{1,0:T(8,128)(2,1)}, bf16[1280,512]{1,0:T(8,128)(2,1)}, u32[]{:S(2)}, u32[]{:S(2)}) collective-permute-start(bf16[1280,512]{1,0:T(8,128)(2,1)} %get-tuple-element.429.refs_8_), channel_id=1, source_target_pairs={{0,1},{1,0},{2,3},{3,2},{4,5},{5,4},{6,7},{7,6},{8,9},{9,8},{10,11... | collective-permute-start | bytes 3932168 | tf_op jit(solution)/shard_map/ppermute | solution.py:415
  35.8 37.7 %collective-permute-start.62 = (bf16[1280,512]{1,0:T(8,128)(2,1)}, bf16[1280,512]{1,0:T(8,128)(2,1)}, u32[]{:S(2)}, u32[]{:S(2)}) collective-permute-start(bf16[1280,512]{1,0:T(8,128)(2,1)} %collective-permute-done.61.refs_10_), channel_id=1, source_target_pairs={{0,1},{1,0},{2,3},{3,2},{4,5},{5,4},{6,7},{7,6},{8,9},{9,8},{10,11... | collective-permute-start | bytes 3932168 | tf_op jit(solution)/shard_map/ppermute | solution.py:415
  36.4 18.9 %collective-permute-start.7 = (bf16[512,256]{1,0:T(8,128)(2,1)S(1)}, bf16[512,256]{1,0:T(8,128)(2,1)}, u32[]{:S(2)}, u32[]{:S(2)}) collective-permute-start(bf16[512,256]{1,0:T(8,128)(2,1)S(1)} %get-tuple-element.248), channel_id=1, source_target_pairs={{0,16},{4,20},{8,24},{12,28},{16,0},{20,4},{24,8},{28,12},{1,17},{... | collective-permute-start | bytes 786440 | tf_op jit(solution)/shard_map/cond/branch_3_fun/ppermute | solution.py:442
  39.3 16.0 %collective-permute-start.6 = (bf16[512,256]{1,0:T(8,128)(2,1)S(1)}, bf16[512,256]{1,0:T(8,128)(2,1)}, u32[]{:S(2)}, u32[]{:S(2)}) collective-permute-start(bf16[512,256]{1,0:T(8,128)(2,1)S(1)} %get-tuple-element.248), channel_id=1, source_target_pairs={{0,4},{4,0},{8,12},{12,8},{16,20},{20,16},{24,28},{28,24},{1,5},{5... | collective-permute-start | bytes 786440 | tf_op jit(solution)/shard_map/cond/branch_3_fun/ppermute | solution.py:442
  40.9 17.2 %all-to-all-start.3 = ((bf16[8,136,128]{2,1,0:T(8,128)(2,1)}), bf16[8,136,128]{2,1,0:T(8,128)(2,1)}, u32[]{:S(2)}, u32[]{:S(2)}) async-start(bf16[8,136,128]{2,1,0:T(8,128)(2,1)} %get-tuple-element.249), calls=%async_computation.3 | async-start | bytes 557056 | tf_op jit(solution)/shard_map/cond/branch_3_fun/all_to_all | solution.py:456
  61.0 6.8 %collective-permute-start.55 = (bf16[128,128]{1,0:T(8,128)(2,1)S(1)}, bf16[128,128]{1,0:T(8,128)(2,1)S(1)}, u32[]{:S(2)}, u32[]{:S(2)}) collective-permute-start(bf16[128,128]{1,0:T(8,128)(2,1)S(1)} %get-tuple-element.423), channel_id=1, source_target_pairs={{0,2},{1,3},{2,0},{3,1},{4,6},{5,7},{6,4},{7,5},{8,10},{9,11},{10,... | collective-permute-start | bytes 98312 | tf_op jit(solution)/shard_map/ppermute | solution.py:486
  62.6 5.2 %collective-permute-start.56 = (bf16[128,128]{1,0:T(8,128)(2,1)S(1)}, bf16[128,128]{1,0:T(8,128)(2,1)S(1)}, u32[]{:S(2)}, u32[]{:S(2)}) collective-permute-start(bf16[128,128]{1,0:T(8,128)(2,1)S(1)} %get-tuple-element.424), channel_id=1, source_target_pairs={{0,3},{1,2},{2,1},{3,0},{4,7},{5,6},{6,5},{7,4},{8,11},{9,10},{10,... | collective-permute-start | bytes 98312 | tf_op jit(solution)/shard_map/ppermute | solution.py:486
  65.6 3.9 %collective-permute-start.54 = (bf16[128,128]{1,0:T(8,128)(2,1)S(1)}, bf16[128,128]{1,0:T(8,128)(2,1)S(1)}, u32[]{:S(2)}, u32[]{:S(2)}) collective-permute-start(bf16[128,128]{1,0:T(8,128)(2,1)S(1)} %get-tuple-element.422), channel_id=1, source_target_pairs={{0,1},{1,0},{2,3},{3,2},{4,5},{5,4},{6,7},{7,6},{8,9},{9,8},{10,11... | collective-permute-start | bytes 98312 | tf_op jit(solution)/shard_map/ppermute | solution.py:486
  67.8 1.9 %collective-permute-start.57 = (f32[128,128]{1,0:T(8,128)S(1)}, f32[128,128]{1,0:T(8,128)S(1)}, u32[]{:S(2)}, u32[]{:S(2)}) collective-permute-start(f32[128,128]{1,0:T(8,128)S(1)} %get-tuple-element.426), channel_id=1, source_target_pairs={{0,1},{1,0},{2,3},{3,2},{4,5},{5,4},{6,7},{7,6},{8,9},{9,8},{10,11... | collective-permute-start | bytes 196616 | tf_op jit(solution)/shard_map/ppermute | solution.py:486
  67.8 4.5 %collective-permute-start.58 = (f32[128,128]{1,0:T(8,128)S(1)}, f32[128,128]{1,0:T(8,128)S(1)}, u32[]{:S(2)}, u32[]{:S(2)}) collective-permute-start(f32[128,128]{1,0:T(8,128)S(1)} %get-tuple-element.427), channel_id=1, source_target_pairs={{0,2},{1,3},{2,0},{3,1},{4,6},{5,7},{6,4},{7,5},{8,10},{9,11},{10,... | collective-permute-start | bytes 196616 | tf_op jit(solution)/shard_map/ppermute | solution.py:486
  69.5 4.1 %collective-permute-start.59 = (f32[128,128]{1,0:T(8,128)S(1)}, f32[128,128]{1,0:T(8,128)S(1)}, u32[]{:S(2)}, u32[]{:S(2)}) collective-permute-start(f32[128,128]{1,0:T(8,128)S(1)} %get-tuple-element.428), channel_id=1, source_target_pairs={{0,3},{1,2},{2,1},{3,0},{4,7},{5,6},{6,5},{7,4},{8,11},{9,10},{10,... | collective-permute-start | bytes 196616 | tf_op jit(solution)/shard_map/ppermute | solution.py:486

commit v4 on v3

--- a/solution.py
+++ b/solution.py
@@ -13,6 +13,7 @@
 EPSILON = 1e-05
 FLAG_ROWS = 8
 EDGE_STEP = 512
+EDGE_STEP_ON_PATH = 1024
 
 f32 = jnp.float32
 bf16 = jnp.bfloat16
@@ -175,7 +176,7 @@
 
 
 def edge_kernel(
-    tail_hbm, sink_hbm, x_hbm, local_ref, degree_ref, tail_ref, sink_ref, x_ref, counts_ref, sems
+    most, tail_hbm, sink_hbm, x_hbm, local_ref, degree_ref, tail_ref, sink_ref, x_ref, counts_ref, sems
 ):
     copies = [
         pltpu.make_async_copy(tail_hbm, tail_ref, sems.at[0]),
@@ -186,7 +187,7 @@
         copy.start()
     nodes, rows = counts_ref.shape
     edges = tail_ref.shape[1]
-    step = math.gcd(edges, EDGE_STEP)
+    step = math.gcd(edges, most)
     first = lax.axis_index("mp") * rows
     counts_ref[...] = jnp.zeros_like(counts_ref)
     copies[0].wait()
@@ -212,11 +213,11 @@
     degree_ref[...] = jnp.broadcast_to(1.0 + degree, degree_ref.shape)
 
 
-def edge_sums(tail, sink, x, rows):
+def edge_sums(tail, sink, x, rows, most):
     edges = tail.shape[1]
     nodes, width = x.shape
     return pl.pallas_call(
-        edge_kernel,
+        functools.partial(edge_kernel, most),
         out_shape=[
             jax.ShapeDtypeStruct((rows, width), f32),
             jax.ShapeDtypeStruct((rows, 128), f32),
@@ -452,9 +453,9 @@
     bundles = gather_pieces(bundle, "mp")
     nodes = x.shape[0]
 
-    def beside(outgoing, tail, sink, x):
+    def beside(outgoing, tail, sink, x, most=EDGE_STEP):
         arrived = lax.all_to_all(outgoing, "dom", split_axis=0, concat_axis=0, tiled=True)
-        return arrived, *edge_sums(tail, sink, x, nodes // shares)
+        return arrived, *edge_sums(tail, sink, x, nodes // shares, most)
 
     operands = (kv, k, v, outgoing, tail, sink, x)
     if peers * (peers - 1) // 2 <= 32:
@@ -463,14 +464,16 @@
             for low in range(1, high):
 
                 def branch(kv, k, v, *rest, low=low, high=high):
+                    most = EDGE_STEP
                     if low & high & (peers // 2):
+                        most = EDGE_STEP_ON_PATH
                         one_k, one_v = send(k, low), send(v, low)
                         two_k, two_v = send(one_k, low ^ high), send(one_v, low ^ high)
                         one = jnp.concatenate([one_k, one_v], axis=1)
                         two = jnp.concatenate([two_k, two_v], axis=1)
                     else:
                         one, two = send(kv, low), send(kv, high)
-                    return one, two, *beside(*rest)
+                    return one, two, *beside(*rest, most)
 
                 branches.append(branch)
         one, two, arrived, local, edge_degree = lax.switch(pair[0], branches, *operands)

time: 78.1 us -> 78.1 us (level)
  no operation moved by 1% of the time
where the time goes in v4:
time: 78.1 us; the launch traced here: 77.8 us
  waiting for transfers between devices  38.2 us (49%)
  Pallas kernels  23 us (29%)
  starting transfers between devices  15.7 us (20%)
  between operations  0.79 us (1%)
    ppermute x3, waiting for transfers between devices, gather_pieces(): pieces[k | bit] = lax.ppermute(pieces[k], axis, xor_route(count, bit))  29.1 us
    pallas_call x1, Pallas kernels, edge_sums(): pl.pallas_call(functools.partial(edge_kernel, most), out_shape=[jax.Shape...  7.89 us
    pallas_call x2, Pallas kernels, attention(): pl.pallas_call(functools.partial(attention_kernel, offsets), out_shape=[j...  5.86 us
    ppermute x2, starting transfers between devices, send(): return lax.ppermute(block, 'dom', xor_route(peers, mask))  4.42 us
    ppermute x6, starting transfers between devices, swap(): return lax.ppermute(chunk, 'mp', xor_route(shares, k)) if k else chunk  4.19 us
    all_to_all x1, starting transfers between devices, beside(): lax.all_to_all(outgoing, 'dom', split_axis=0, concat_axis=0, tiled=True)  4.06 us
    pallas_call x1, Pallas kernels, final(): pl.pallas_call(functools.partial(final_kernel, shares), out_shape=jax.Sha...  4.05 us
    ppermute x6, waiting for transfers between devices, swap(): return lax.ppermute(chunk, 'mp', xor_route(shares, k)) if k else chunk  3.85 us
  transfers between devices with their start and end apart: 12, of which 5 were waited for; matrix products, arithmetic and copies ran while one was open for 0% of the time, Pallas kernels for 20%

profile of v4, /device:TPU:0, one launch (start us, length us, event | category | flops | bytes accessed | tf_op | source)
XLA Modules:
  0.0 77.8 jit_solution(7713844440849235097)
XLA Ops:
  0.0 3.7 %prologue.1 = (s32[1]{0:T(128)}, s32[1]{0:T(128)}, s32[1]{0:T(128)}, bf16[512,128]{1,0:T(8,128)(2,1)S(1)}, bf16[512,256]{1,0:T(8,128)(2,1)S(1)}, /*index=5*/bf16...) custom-call(bf16[512,512]{1,0:T(8,128)(2,1)} %x_hbm.1, ...), custom_call_target="tpu_custom_call" | custom-call | flops 201326592 | bytes 4194304 | tf_op jit(solution)/shard_map/prologue/pallas_call | solution.py:142
  3.7 3.0 %collective-permute-start.61 = (bf16[1280,512]{1,0:T(8,128)(2,1)}, bf16[1280,512]{1,0:T(8,128)(2,1)}, u32[]{:S(2)}, u32[]{:S(2)}) collective-permute-start(bf16[1280,512]{1,0:T(8,128)(2,1)} %get-tuple-element.429.refs_8_), channel_id=1, source_target_pairs={{0,2},{1,3},{2,0},{3,1},{4,6},{5,7},{6,4},{7,5},{8,10},{9,11},{10,... | collective-permute-start | bytes 3932168 | tf_op jit(solution)/shard_map/ppermute | solution.py:416
  6.7 0.0 collective-permute-start.60
  6.7 29.1 %collective-permute-done.61.refs_10_ = bf16[1280,512]{1,0:T(8,128)(2,1)} collective-permute-done((bf16[1280,512]{1,0:T(8,128)(2,1)}, bf16[1280,512]{1,0:T(8,128)(2,1)}, u32[]{:S(2)}, u32[]{:S(2)}) %collective-permute-start.61) | collective-permute-done | bytes 1310752 | tf_op jit(solution)/shard_map/ppermute | solution.py:416
  35.8 0.0 collective-permute-start.62
  36.4 21.7 %conditional.1 = (bf16[512,256]{1,0:T(8,128)(2,1)}, bf16[512,256]{1,0:T(8,128)(2,1)}, bf16[8,136,128]{2,1,0:T(8,128)(2,1)}, f32[128,512]{1,0:T(8,128)S(1)}, f32[128,128]{1,0:T(8,128)S(1)}) conditional(s32[]{:T(128)} %bitcast.4, (bf16[512,256]{1,0:T(8,128)(2,1)S(1)}, bf16[8,136,128]{2,1,0:T(8,128)(2,1)}, ...), branch_computations={%region_0.0_spmd, %region_1.0_spmd, %region_2.0_spmd, %region_3.0_... | conditional | flops 8590983168 | bytes 6078696 | solution.py:479
  36.4 2.9 %collective-permute-start.7 = (bf16[512,256]{1,0:T(8,128)(2,1)S(1)}, bf16[512,256]{1,0:T(8,128)(2,1)}, u32[]{:S(2)}, u32[]{:S(2)}) collective-permute-start(bf16[512,256]{1,0:T(8,128)(2,1)S(1)} %get-tuple-element.248), channel_id=1, source_target_pairs={{0,16},{4,20},{8,24},{12,28},{16,0},{20,4},{24,8},{28,12},{1,17},{... | collective-permute-start | bytes 786440 | tf_op jit(solution)/shard_map/cond/branch_3_fun/ppermute | solution.py:443
  39.3 1.5 %collective-permute-start.6 = (bf16[512,256]{1,0:T(8,128)(2,1)S(1)}, bf16[512,256]{1,0:T(8,128)(2,1)}, u32[]{:S(2)}, u32[]{:S(2)}) collective-permute-start(bf16[512,256]{1,0:T(8,128)(2,1)S(1)} %get-tuple-element.248), channel_id=1, source_target_pairs={{0,4},{4,0},{8,12},{12,8},{16,20},{20,16},{24,28},{28,24},{1,5},{5... | collective-permute-start | bytes 786440 | tf_op jit(solution)/shard_map/cond/branch_3_fun/ppermute | solution.py:443
  40.9 4.1 %all-to-all-start.3 = ((bf16[8,136,128]{2,1,0:T(8,128)(2,1)}), bf16[8,136,128]{2,1,0:T(8,128)(2,1)}, u32[]{:S(2)}, u32[]{:S(2)}) async-start(bf16[8,136,128]{2,1,0:T(8,128)(2,1)} %get-tuple-element.249), calls=%async_computation.3 | async-start | bytes 557056 | tf_op jit(solution)/shard_map/cond/branch_3_fun/all_to_all | solution.py:457
  44.9 7.9 %edge_sums.24 = (f32[128,512]{1,0:T(8,128)S(1)}, f32[128,128]{1,0:T(8,128)S(1)}) custom-call(s32[1,16384]{1,0:T(1,128)} %get-tuple-element.250.tail_hbm, s32[1,16384]{1,0:T(1,128)} %get-tuple-element.251.sink_hbm, bf16[512,512]{1,0:T(8,128)(2,1)} %get-tuple-element.252.x_hbm), custom_call_target="tpu_custom_call" | custom-call | flops 8589934592 | bytes 2097152 | tf_op jit(solution)/shard_map/cond/branch_3_fun/edge_sums/pallas_call | solution.py:219
  52.8 2.5 %collective-permute-done.7 = bf16[512,256]{1,0:T(8,128)(2,1)} collective-permute-done((bf16[512,256]{1,0:T(8,128)(2,1)S(1)}, bf16[512,256]{1,0:T(8,128)(2,1)}, u32[]{:S(2)}, u32[]{:S(2)}) %collective-permute-start.7) | collective-permute-done | bytes 262176 | tf_op jit(solution)/shard_map/cond/branch_3_fun/ppermute | solution.py:443
  55.3 0.0 collective-permute-done.6
  55.3 2.7 %all-to-all-done.3 = bf16[8,136,128]{2,1,0:T(8,128)(2,1)} async-done(((bf16[8,136,128]{2,1,0:T(8,128)(2,1)}), bf16[8,136,128]{2,1,0:T(8,128)(2,1)}, u32[]{:S(2)}, u32[]{:S(2)}) %all-to-all-start.3) | async-done | bytes 278560 | tf_op jit(solution)/shard_map/cond/branch_3_fun/all_to_all | solution.py:457
  58.1 2.9 %attention.3 = (bf16[128,128]{1,0:T(8,128)(2,1)S(1)}, bf16[128,128]{1,0:T(8,128)(2,1)S(1)}) custom-call(f32[2,8,128]{2,1,0:T(8,128)S(1)} %get-tuple-element.417.scales_ref, bf16[512,128]{1,0:T(8,128)(2,1)S(1)} %get-tuple-element.418.q_ref, bf16[512,256]{1,0:T(8,128)(2,1)S(1)} %get-tuple-element.408.own_ref, bf16[512,256]{1,0:T(8,128)(2,1)} %get-tuple-element.419.one_any, ...), custom_call_target="tpu_custom_call" | custom-call | flops 402653184 | bytes 2097152 | tf_op jit(solution)/shard_map/attention/pallas_call | solution.py:321
  61.0 1.6 %collective-permute-start.55 = (bf16[128,128]{1,0:T(8,128)(2,1)S(1)}, bf16[128,128]{1,0:T(8,128)(2,1)S(1)}, u32[]{:S(2)}, u32[]{:S(2)}) collective-permute-start(bf16[128,128]{1,0:T(8,128)(2,1)S(1)} %get-tuple-element.423), channel_id=1, source_target_pairs={{0,2},{1,3},{2,0},{3,1},{4,6},{5,7},{6,4},{7,5},{8,10},{9,11},{10,... | collective-permute-start | bytes 98312 | tf_op jit(solution)/shard_map/ppermute | solution.py:489
  62.6 0.0 collective-permute-start.56
  62.6 2.9 %attention.2 = (bf16[128,128]{1,0:T(8,128)(2,1)S(1)}, bf16[128,128]{1,0:T(8,128)(2,1)S(1)}) custom-call(f32[2,8,128]{2,1,0:T(8,128)S(1)} %get-tuple-element.417.scales_ref, bf16[512,128]{1,0:T(8,128)(2,1)S(1)} %get-tuple-element.418.q_ref, bf16[512,256]{1,0:T(8,128)(2,1)S(1)} %get-tuple-element.408.own_ref, bf16[512,256]{1,0:T(8,128)(2,1)} %get-tuple-element.419.one_any, ...), custom_call_target="tpu_custom_call" | custom-call | flops 402653184 | bytes 2097152 | tf_op jit(solution)/shard_map/attention/pallas_call | solution.py:321
  65.6 0.7 collective-permute-start.54
  66.2 1.5 %landing.1 = (f32[128,128]{1,0:T(8,128)S(1)}, f32[128,128]{1,0:T(8,128)S(1)}, f32[128,128]{1,0:T(8,128)S(1)}, f32[128,128]{1,0:T(8,128)S(1)}, f32[128,128]{1,0:T(8,128)S(1)}) custom-call(f32[128,128]{1,0:T(8,128)S(1)} %get-tuple-element.413.edge_degree_ref, s32[8,128]{1,0:T(8,128)S(1)} %get-tuple-element.414.landing_ref, ...), custom_call_target="tpu_custom_call" | custom-call | flops 268435456 | bytes 2097152 | tf_op jit(solution)/shard_map/landing/pallas_call | solution.py:263
  67.8 0.0 collective-permute-done.55.refs_2_
  67.8 0.1 collective-permute-start.57
  67.8 0.0 collective-permute-done.56.refs_3_
  67.8 1.6 %collective-permute-start.58 = (f32[128,128]{1,0:T(8,128)S(1)}, f32[128,128]{1,0:T(8,128)S(1)}, u32[]{:S(2)}, u32[]{:S(2)}) collective-permute-start(f32[128,128]{1,0:T(8,128)S(1)} %get-tuple-element.427), channel_id=1, source_target_pairs={{0,2},{1,3},{2,0},{3,1},{4,6},{5,7},{6,4},{7,5},{8,10},{9,11},{10,... | collective-permute-start | bytes 196616 | tf_op jit(solution)/shard_map/ppermute | solution.py:489
  69.5 0.0 collective-permute-done.54.refs_1_
  69.5 0.2 collective-permute-start.59
  69.7 0.0 collective-permute-done.57.refs_5_
  69.7 2.6 %collective-permute-done.58.refs_6_ = f32[128,128]{1,0:T(8,128)S(1)} collective-permute-done((f32[128,128]{1,0:T(8,128)S(1)}, f32[128,128]{1,0:T(8,128)S(1)}, u32[]{:S(2)}, u32[]{:S(2)}) %collective-permute-start.58) | collective-permute-done | bytes 65568 | tf_op jit(solution)/shard_map/ppermute | solution.py:489
  72.3 1.2 %collective-permute-done.59.refs_7_ = f32[128,128]{1,0:T(8,128)S(1)} collective-permute-done((f32[128,128]{1,0:T(8,128)S(1)}, f32[128,128]{1,0:T(8,128)S(1)}, u32[]{:S(2)}, u32[]{:S(2)}) %collective-permute-start.59) | collective-permute-done | bytes 65568 | tf_op jit(solution)/shard_map/ppermute | solution.py:489
  73.5 0.0 collective-permute-done.60.refs_9_
  73.5 0.0 collective-permute-done.62.refs_11_
  73.5 4.0 %final.1 = bf16[128,512]{1,0:T(8,128)(2,1)} custom-call(bf16[128,512]{1,0:T(8,128)(2,1)S(1)} %get-tuple-element.405.share_ref, f32[1,512]{1,0:T(1,128)S(1)} %get-tuple-element.406.gain_ref, f32[128,512]{1,0:T(8,128)S(1)} %get-tuple-element.412.local_ref, f32[128,128]{1,0:T(8,128)S(1)} %get-tuple-element.416.degree_ref, ...), custom_call_target="tpu_custom_call" | custom-call | flops 536870912 | bytes 6291456 | tf_op jit(solution)/shard_map/final/pallas_call | solution.py:392
Async XLA Ops:
  3.7 32.1 %collective-permute-start.61 = (bf16[1280,512]{1,0:T(8,128)(2,1)}, bf16[1280,512]{1,0:T(8,128)(2,1)}, u32[]{:S(2)}, u32[]{:S(2)}) collective-permute-start(bf16[1280,512]{1,0:T(8,128)(2,1)} %get-tuple-element.429.refs_8_), channel_id=1, source_target_pairs={{0,2},{1,3},{2,0},{3,1},{4,6},{5,7},{6,4},{7,5},{8,10},{9,11},{10,... | collective-permute-start | bytes 3932168 | tf_op jit(solution)/shard_map/ppermute | solution.py:416
  6.7 66.8 %collective-permute-start.60 = (bf16[1280,512]{1,0:T(8,128)(2,1)}, bf16[1280,512]{1,0:T(8,128)(2,1)}, u32[]{:S(2)}, u32[]{:S(2)}) collective-permute-start(bf16[1280,512]{1,0:T(8,128)(2,1)} %get-tuple-element.429.refs_8_), channel_id=1, source_target_pairs={{0,1},{1,0},{2,3},{3,2},{4,5},{5,4},{6,7},{7,6},{8,9},{9,8},{10,11... | collective-permute-start | bytes 3932168 | tf_op jit(solution)/shard_map/ppermute | solution.py:416
  35.8 37.7 %collective-permute-start.62 = (bf16[1280,512]{1,0:T(8,128)(2,1)}, bf16[1280,512]{1,0:T(8,128)(2,1)}, u32[]{:S(2)}, u32[]{:S(2)}) collective-permute-start(bf16[1280,512]{1,0:T(8,128)(2,1)} %collective-permute-done.61.refs_10_), channel_id=1, source_target_pairs={{0,1},{1,0},{2,3},{3,2},{4,5},{5,4},{6,7},{7,6},{8,9},{9,8},{10,11... | collective-permute-start | bytes 3932168 | tf_op jit(solution)/shard_map/ppermute | solution.py:416
  36.4 18.9 %collective-permute-start.7 = (bf16[512,256]{1,0:T(8,128)(2,1)S(1)}, bf16[512,256]{1,0:T(8,128)(2,1)}, u32[]{:S(2)}, u32[]{:S(2)}) collective-permute-start(bf16[512,256]{1,0:T(8,128)(2,1)S(1)} %get-tuple-element.248), channel_id=1, source_target_pairs={{0,16},{4,20},{8,24},{12,28},{16,0},{20,4},{24,8},{28,12},{1,17},{... | collective-permute-start | bytes 786440 | tf_op jit(solution)/shard_map/cond/branch_3_fun/ppermute | solution.py:443
  39.3 16.0 %collective-permute-start.6 = (bf16[512,256]{1,0:T(8,128)(2,1)S(1)}, bf16[512,256]{1,0:T(8,128)(2,1)}, u32[]{:S(2)}, u32[]{:S(2)}) collective-permute-start(bf16[512,256]{1,0:T(8,128)(2,1)S(1)} %get-tuple-element.248), channel_id=1, source_target_pairs={{0,4},{4,0},{8,12},{12,8},{16,20},{20,16},{24,28},{28,24},{1,5},{5... | collective-permute-start | bytes 786440 | tf_op jit(solution)/shard_map/cond/branch_3_fun/ppermute | solution.py:443
  40.9 17.2 %all-to-all-start.3 = ((bf16[8,136,128]{2,1,0:T(8,128)(2,1)}), bf16[8,136,128]{2,1,0:T(8,128)(2,1)}, u32[]{:S(2)}, u32[]{:S(2)}) async-start(bf16[8,136,128]{2,1,0:T(8,128)(2,1)} %get-tuple-element.249), calls=%async_computation.3 | async-start | bytes 557056 | tf_op jit(solution)/shard_map/cond/branch_3_fun/all_to_all | solution.py:457
  61.0 6.8 %collective-permute-start.55 = (bf16[128,128]{1,0:T(8,128)(2,1)S(1)}, bf16[128,128]{1,0:T(8,128)(2,1)S(1)}, u32[]{:S(2)}, u32[]{:S(2)}) collective-permute-start(bf16[128,128]{1,0:T(8,128)(2,1)S(1)} %get-tuple-element.423), channel_id=1, source_target_pairs={{0,2},{1,3},{2,0},{3,1},{4,6},{5,7},{6,4},{7,5},{8,10},{9,11},{10,... | collective-permute-start | bytes 98312 | tf_op jit(solution)/shard_map/ppermute | solution.py:489
  62.6 5.2 %collective-permute-start.56 = (bf16[128,128]{1,0:T(8,128)(2,1)S(1)}, bf16[128,128]{1,0:T(8,128)(2,1)S(1)}, u32[]{:S(2)}, u32[]{:S(2)}) collective-permute-start(bf16[128,128]{1,0:T(8,128)(2,1)S(1)} %get-tuple-element.424), channel_id=1, source_target_pairs={{0,3},{1,2},{2,1},{3,0},{4,7},{5,6},{6,5},{7,4},{8,11},{9,10},{10,... | collective-permute-start | bytes 98312 | tf_op jit(solution)/shard_map/ppermute | solution.py:489
  65.6 3.9 %collective-permute-start.54 = (bf16[128,128]{1,0:T(8,128)(2,1)S(1)}, bf16[128,128]{1,0:T(8,128)(2,1)S(1)}, u32[]{:S(2)}, u32[]{:S(2)}) collective-permute-start(bf16[128,128]{1,0:T(8,128)(2,1)S(1)} %get-tuple-element.422), channel_id=1, source_target_pairs={{0,1},{1,0},{2,3},{3,2},{4,5},{5,4},{6,7},{7,6},{8,9},{9,8},{10,11... | collective-permute-start | bytes 98312 | tf_op jit(solution)/shard_map/ppermute | solution.py:489
  67.8 1.9 %collective-permute-start.57 = (f32[128,128]{1,0:T(8,128)S(1)}, f32[128,128]{1,0:T(8,128)S(1)}, u32[]{:S(2)}, u32[]{:S(2)}) collective-permute-start(f32[128,128]{1,0:T(8,128)S(1)} %get-tuple-element.426), channel_id=1, source_target_pairs={{0,1},{1,0},{2,3},{3,2},{4,5},{5,4},{6,7},{7,6},{8,9},{9,8},{10,11... | collective-permute-start | bytes 196616 | tf_op jit(solution)/shard_map/ppermute | solution.py:489
  67.8 4.5 %collective-permute-start.58 = (f32[128,128]{1,0:T(8,128)S(1)}, f32[128,128]{1,0:T(8,128)S(1)}, u32[]{:S(2)}, u32[]{:S(2)}) collective-permute-start(f32[128,128]{1,0:T(8,128)S(1)} %get-tuple-element.427), channel_id=1, source_target_pairs={{0,2},{1,3},{2,0},{3,1},{4,6},{5,7},{6,4},{7,5},{8,10},{9,11},{10,... | collective-permute-start | bytes 196616 | tf_op jit(solution)/shard_map/ppermute | solution.py:489
  69.5 4.1 %collective-permute-start.59 = (f32[128,128]{1,0:T(8,128)S(1)}, f32[128,128]{1,0:T(8,128)S(1)}, u32[]{:S(2)}, u32[]{:S(2)}) collective-permute-start(f32[128,128]{1,0:T(8,128)S(1)} %get-tuple-element.428), channel_id=1, source_target_pairs={{0,3},{1,2},{2,1},{3,0},{4,7},{5,6},{6,5},{7,4},{8,11},{9,10},{10,... | collective-permute-start | bytes 196616 | tf_op jit(solution)/shard_map/ppermute | solution.py:489
